TPU v7x, 128 devices: a whole 4x4x4 slice. The times are simulated.
128 devices in a mesh: rep: 4 (over z_hi, core), ctx: 4 (over y), fsdp: 8 (over z_lo, x).
Axes of the slice: x: 4, y: 4, z: 4 (z_hi: 2, z_lo: 2; z = z_hi * 2 + z_lo), core: 2. Of those that a mesh axis runs over, the one named last changes fastest.
Arguments:
- tokens: bfloat16 [32, 1024, 1024], P(('rep', 'fsdp'), 'ctx'), may hold values from -6 to 6
- norm_gain: bfloat16 [1024], P(('ctx', 'fsdp')), may hold values from 0.5 to 1.5
- norm_shift: bfloat16 [1024], P(('ctx', 'fsdp')), may hold values from -2 to 2
- triple_weight: bfloat16 [1024, 3072], P(('ctx', 'fsdp')), may hold values from -0.25 to 0.25
- mixer_weight: bfloat16 [1024, 1024], P(('ctx', 'fsdp')), may hold values from -0.75 to 0.75
- inner_weight: bfloat16 [1024, 4096], P(('ctx', 'fsdp')), may hold values from -0.1875 to 0.1875
- inner_bias: bfloat16 [4096], P(('ctx', 'fsdp')), may hold values from -2 to 2
- outer_weight: bfloat16 [4096, 1024], P(('ctx', 'fsdp')), may hold values from -0.125 to 0.125
- outer_bias: bfloat16 [1024], P(('ctx', 'fsdp')), may hold values from -2 to 2
- prefix_length: int32 [32], P(('rep', 'fsdp')), may hold values from 102 to 512
- pad_mask: int32 [32], P(('rep', 'fsdp')), may hold values from 0 to 31, each once
- cotangent: bfloat16 [32, 1024, 1024], P(('rep', 'fsdp'), 'ctx'), may hold values from -6 to 6
Outputs:
- layer_output: bfloat16 [32, 1024, 1024], P(('rep', 'fsdp'), 'ctx')
- input_grad: bfloat16 [32, 1024, 1024], P(('rep', 'fsdp'), 'ctx')
- grad_norm_gain: float32 [1024], P(('ctx', 'fsdp'))
- grad_norm_shift: float32 [1024], P(('ctx', 'fsdp'))
- grad_triple_weight: float32 [1024, 3072], P(('ctx', 'fsdp'))
- grad_mixer_weight: float32 [1024, 1024], P(('ctx', 'fsdp'))
- grad_inner_weight: float32 [1024, 4096], P(('ctx', 'fsdp'))
- grad_inner_bias: float32 [4096], P(('ctx', 'fsdp'))
- grad_outer_weight: float32 [4096, 1024], P(('ctx', 'fsdp'))
- grad_outer_bias: float32 [1024], P(('ctx', 'fsdp'))
Inputs may be any that keep to these rules, and one draw needn't show every extreme that they name: `pad_mask`: each number of 0 to 31 stands in exactly one slot; the slot holding 0 is the pad slot.
All inputs are finite; a program needn't handle non-finite values.
Results may differ from a plain program's by a relative error of at most 0.025.
Values may be sent and summed in bfloat16 or wider, within the bound.
No kernel may reach another device: no remote copies, remote signals or barrier semaphores. Data moves between devices by JAX's collectives and lax.ppermute only.
A program may use at most 192 MiB of HBM per device.

v0:
```python
from functools import partial

import jax
import jax.numpy as jnp
from jax import lax
from jax.experimental import pallas as pl
from jax.experimental.pallas import tpu as pltpu
from jax.sharding import PartitionSpec as P

HEADS = 16
HEAD_DIM = 64
ROT = 32


eps = 1e-05


def angles(positions):
    frequency = 10000.0 ** (-(jnp.arange(ROT // 2, dtype=jnp.float32) * 2.0) / ROT)
    phases = positions.astype(jnp.float32)[:, None] * frequency[None, :]
    return (jnp.cos(phases), jnp.sin(phases))


def rotate(field, cos_table, sin_table):
    leading = field.shape[:-1]
    paired = field[..., :ROT].reshape(leading + (ROT // 2, 2))
    even_part = paired[..., 0]
    odd_part = paired[..., 1]
    cos_wide = cos_table[:, None, :]
    sin_wide = sin_table[:, None, :]
    turned = jnp.stack(
        [even_part * cos_wide - odd_part * sin_wide, odd_part * cos_wide + even_part * sin_wide], -1
    )
    return jnp.concatenate([turned.reshape(leading + (ROT,)), field[..., ROT:]], -1)


def ring_pairs(n, step):
    return [(i, (i + step) % n) for i in range(n)]


def ring_gather(block, axis):
    n = lax.axis_size(axis)
    half = block.shape[0] // 2
    from_left = lax.ppermute(block, axis, ring_pairs(n, 1))
    from_right = lax.ppermute(block, axis, ring_pairs(n, -1))
    far_first = lax.ppermute(from_left[:half], axis, ring_pairs(n, 1))
    far_second = lax.ppermute(from_right[half:], axis, ring_pairs(n, -1))
    far = jnp.concatenate([far_first, far_second], 0)
    return jnp.stack([block, from_right, far, from_left])


def ring_scatter(parts, axis):
    n = lax.axis_size(axis)
    half = parts.shape[1] // 2
    wire = jnp.bfloat16
    got_left = lax.ppermute(parts[2, :half].astype(wire), axis, ring_pairs(n, 1))
    got_right = lax.ppermute(parts[2, half:].astype(wire), axis, ring_pairs(n, -1))
    to_right = jnp.concatenate([parts[1, :half] + got_left.astype(jnp.float32), parts[1, half:]], 0)
    to_left = jnp.concatenate([parts[3, :half], parts[3, half:] + got_right.astype(jnp.float32)], 0)
    from_left = lax.ppermute(to_right.astype(wire), axis, ring_pairs(n, 1))
    from_right = lax.ppermute(to_left.astype(wire), axis, ring_pairs(n, -1))
    return parts[0] + from_left.astype(jnp.float32) + from_right.astype(jnp.float32)


def ring_all_to_all(payload, axis):
    n = lax.axis_size(axis)
    me = lax.axis_index(axis)
    pick = lambda d: lax.dynamic_index_in_dim(payload, d % n, 0, keepdims=False)
    got = [pick(me)] + [
        lax.ppermute(pick(me + s), axis, ring_pairs(n, s)) for s in range(1, n)
    ]
    mirrored = jnp.stack([got[(-k) % n] for k in range(n)])
    doubled = jnp.concatenate([mirrored, mirrored], 0)
    return lax.dynamic_slice_in_dim(doubled, n - me, n, 0)


def replica_sum(values, axis):
    n = lax.axis_size(axis)
    f32, wire = jnp.float32, jnp.bfloat16
    values = values.astype(wire)
    if n != 4:
        return lax.psum(values, axis).astype(f32)
    pair = values.astype(f32) + lax.ppermute(values, axis, [(i, i ^ 1) for i in range(n)]).astype(f32)
    pair = pair.astype(wire)
    return pair.astype(f32) + lax.ppermute(pair, axis, [(i, i ^ 2) for i in range(n)]).astype(f32)


def attention_kernel(span_ref, q_ref, k_ref, v_ref, gm_ref, qpos_ref, kpos_ref,
                     mix_ref, gq_ref, gk_ref, gv_ref):
    f32, bf16 = jnp.float32, jnp.bfloat16
    block = pl.program_id(1)
    q = q_ref[...]
    k = k_ref[...]
    v = v_ref[...]
    gm = gm_ref[...]
    scores = lax.dot_general(q, k, (((1,), (1,)), ((), ())), preferred_element_type=f32)
    qpos = qpos_ref[...]
    kpos = kpos_ref[...]
    allowed = (kpos <= qpos) | (kpos < span_ref[0])
    scores = jnp.where(allowed, scores, -1e30)
    peak = jnp.max(scores, axis=1, keepdims=True)
    exps = jnp.exp(scores - peak)
    total = jnp.sum(exps, axis=1, keepdims=True)
    probs = exps * (1.0 / total)
    low_probs = probs.astype(bf16)
    mix_ref[...] = jnp.dot(low_probs, v, preferred_element_type=f32).astype(mix_ref.dtype)
    grad_probs = lax.dot_general(gm, v, (((1,), (1,)), ((), ())), preferred_element_type=f32)
    inner = jnp.sum(probs * grad_probs, axis=1, keepdims=True)
    grad_scores = (probs * (grad_probs - inner)).astype(bf16)
    gq_ref[...] = jnp.dot(grad_scores, k, preferred_element_type=f32)
    gk_part = lax.dot_general(grad_scores, q, (((0,), (0,)), ((), ())), preferred_element_type=f32)
    gv_part = lax.dot_general(low_probs, gm, (((0,), (0,)), ((), ())), preferred_element_type=f32)

    @pl.when(block == 0)
    def _():
        gk_ref[...] = gk_part
        gv_ref[...] = gv_part

    @pl.when(block != 0)
    def _():
        gk_ref[...] += gk_part
        gv_ref[...] += gv_part


def fused_attention(span, queries, keys, values, grad_mixture, positions, rows=256):
    heads, length, dim = queries.shape
    blocks = length // rows
    qpos = positions.reshape(length, 1).astype(jnp.int32)
    kpos = positions.reshape(1, length).astype(jnp.int32)
    row_block = pl.BlockSpec((None, rows, dim), lambda h, b, s: (h, b, 0))
    whole = pl.BlockSpec((None, length, dim), lambda h, b, s: (h, 0, 0))
    f32 = jnp.float32
    return pl.pallas_call(
        attention_kernel,
        out_shape=(
            jax.ShapeDtypeStruct((heads, length, dim), jnp.bfloat16),
            jax.ShapeDtypeStruct((heads, length, dim), f32),
            jax.ShapeDtypeStruct((heads, length, dim), f32),
            jax.ShapeDtypeStruct((heads, length, dim), f32),
        ),
        grid_spec=pltpu.PrefetchScalarGridSpec(
            num_scalar_prefetch=1,
            grid=(heads, blocks),
            in_specs=[
                row_block, whole, whole, row_block,
                pl.BlockSpec((rows, 1), lambda h, b, s: (b, 0)),
                pl.BlockSpec((1, length), lambda h, b, s: (0, 0)),
            ],
            out_specs=[row_block, row_block, whole, whole],
        ),
        compiler_params=pltpu.CompilerParams(dimension_semantics=("arbitrary", "arbitrary")),
        cost_estimate=pl.CostEstimate(
            flops=12 * heads * length * length * dim,
            transcendentals=heads * length * length,
            bytes_accessed=heads * length * dim * (4 * 2 + 3 * 4 + 2),
        ),
    )(span.reshape(1).astype(jnp.int32), queries, keys, values, grad_mixture, qpos, kpos)


def local(
    tokens,
    norm_gain,
    norm_shift,
    triple_weight,
    mixer_weight,
    inner_weight,
    inner_bias,
    outer_weight,
    outer_bias,
    prefix_length,
    pad_mask,
    cotangent,
):
    nc = lax.axis_size("ctx")
    nf = lax.axis_size("fsdp")
    me = lax.axis_index("ctx")
    _, own_rows, width = tokens.shape
    length = own_rows * nc
    shard_rows = triple_weight.shape[0]
    heads_here = HEADS // nc
    head_cols = heads_here * HEAD_DIM
    ff_here = inner_weight.shape[1] // nc
    ff_rows = outer_weight.shape[0]
    f32, bf16 = jnp.float32, jnp.bfloat16

    triple_cols = (
        triple_weight.reshape(shard_rows, 3, nc, head_cols)
        .transpose(2, 0, 1, 3)
        .reshape(nc, shard_rows, 3 * head_cols)
    )
    inner_cols = inner_weight.reshape(shard_rows, nc, ff_here).transpose(1, 0, 2)
    small = jnp.stack([norm_gain, norm_shift, outer_bias], -1)
    small = jnp.pad(small, ((0, 0), (0, 128 - small.shape[-1])))
    small = jnp.broadcast_to(small[None], (nc,) + small.shape)
    column_payload = jnp.concatenate([triple_cols, inner_cols, small], -1)
    column_payload = ring_all_to_all(column_payload, "ctx")
    column_block = lax.all_gather(column_payload, "fsdp", axis=0, tiled=False)
    column_block = column_block.swapaxes(0, 1).reshape(nc * nf * shard_rows, -1)
    triple_here = column_block[:, : 3 * head_cols]
    inner_here = column_block[:, 3 * head_cols : 3 * head_cols + ff_here]
    gain = column_block[:, 3 * head_cols + ff_here].astype(f32)
    shift = column_block[:, 3 * head_cols + ff_here + 1].astype(f32)
    obias = column_block[:, 3 * head_cols + ff_here + 2].astype(f32)

    bias_rows = jnp.pad(inner_bias[None], ((0, 15), (0, width - inner_bias.shape[0])))
    row_payload = jnp.concatenate([mixer_weight, outer_weight, bias_rows], 0)
    row_block = lax.all_gather(row_payload, "fsdp", axis=0, tiled=False)
    mixer_here = row_block[:, :shard_rows].reshape(nf * shard_rows, width)
    outer_here = row_block[:, shard_rows : shard_rows + ff_rows].reshape(nf * ff_rows, width)
    ibias_here = row_block[:, shard_rows + ff_rows, : inner_bias.shape[0]].reshape(-1).astype(f32)

    visible = (pad_mask[0] != 0).astype(f32)
    own_upstream = cotangent[0].astype(f32) * visible
    both = jnp.concatenate([tokens[0], own_upstream.astype(bf16)], -1)
    both = ring_gather(both, "ctx").reshape(length, 2 * width)
    all_tokens = both[:, :width]
    all_upstream = both[:, width:]

    input_rows = all_tokens.astype(f32)
    center = input_rows - jnp.mean(input_rows, -1, keepdims=True)
    scaling = lax.rsqrt(jnp.mean(center * center, -1, keepdims=True) + eps)
    whitened = center * scaling
    normed = (whitened * gain + shift).astype(bf16)

    owners = (me + jnp.arange(nc)) % nc
    positions = (owners[:, None] * own_rows + jnp.arange(own_rows)[None, :]).reshape(length)
    cos_table, sin_table = angles(positions)
    query_key_value = jnp.dot(normed, triple_here, preferred_element_type=f32)
    heads_shape = (length, heads_here, HEAD_DIM)
    queries = (
        rotate(query_key_value[:, :head_cols].reshape(heads_shape), cos_table, sin_table)
        * HEAD_DIM ** (-0.5)
    ).astype(bf16)
    key_rows = rotate(
        query_key_value[:, head_cols : 2 * head_cols].reshape(heads_shape), cos_table, sin_table
    ).astype(bf16)
    value_rows = query_key_value[:, 2 * head_cols :].reshape(heads_shape).astype(bf16)
    span = prefix_length[0]
    grad_mixture = jnp.dot(all_upstream, mixer_here.T, preferred_element_type=f32).astype(bf16)
    by_head = lambda values: values.reshape(heads_shape).swapaxes(0, 1)
    mixture, grad_queries, grad_keys, grad_values = fused_attention(
        span, by_head(queries), by_head(key_rows), by_head(value_rows), by_head(grad_mixture), positions
    )
    grad_queries, grad_keys, grad_values = (
        values.swapaxes(0, 1) for values in (grad_queries, grad_keys, grad_values)
    )
    mixture = mixture.swapaxes(0, 1).reshape(length, head_cols)
    attention = jnp.dot(mixture, mixer_here, preferred_element_type=f32)
    preact = jnp.dot(normed, inner_here, preferred_element_type=f32) + ibias_here
    gelu_result = jax.nn.gelu(preact, approximate=True).astype(bf16)
    feedforward = jnp.dot(gelu_result, outer_here, preferred_element_type=f32)
    block_sum = (attention + feedforward).astype(bf16).reshape(nc, own_rows, width)
    block_sum = lax.dynamic_slice_in_dim(jnp.concatenate([block_sum, block_sum], 0), nc - me, nc, 0)
    block_sum = lax.psum_scatter(block_sum, "ctx", scatter_dimension=0, tiled=True)[0].astype(f32)
    layer_output = (tokens[0].astype(f32) + block_sum + obias).astype(bf16)

    ones_block = jnp.ones((length, 16), bf16)
    row_lhs = jnp.concatenate([mixture, gelu_result, ones_block], -1)
    row_product = jnp.dot(row_lhs.T, all_upstream, preferred_element_type=f32).astype(bf16)
    grad_activated = jnp.dot(all_upstream, outer_here.T, preferred_element_type=f32)
    unused_value, gelu_pull = jax.vjp(partial(jax.nn.gelu, approximate=True), preact)
    grad_before_gelu = gelu_pull(grad_activated)[0].astype(bf16)
    grad_inner_weight = jnp.dot(normed.T, grad_before_gelu, preferred_element_type=f32)
    grad_inner_bias = jnp.sum(grad_before_gelu.astype(f32), 0)
    flat_shape = (length, head_cols)
    grad_query_key_value = jnp.concatenate(
        [
            rotate(grad_queries * HEAD_DIM ** (-0.5), cos_table, -sin_table).reshape(flat_shape),
            rotate(grad_keys, cos_table, -sin_table).reshape(flat_shape),
            grad_values.reshape(flat_shape),
        ],
        -1,
    ).astype(bf16)
    grad_triple_weight = jnp.dot(normed.T, grad_query_key_value, preferred_element_type=f32)
    grad_normed = jnp.dot(grad_query_key_value, triple_here.T, preferred_element_type=f32)
    grad_normed = grad_normed + jnp.dot(grad_before_gelu, inner_here.T, preferred_element_type=f32)
    grad_normed = ring_scatter(grad_normed.reshape(nc, own_rows, width), "ctx")

    own_whitened = whitened[:own_rows]
    own_scaling = scaling[:own_rows]
    grad_norm_gain = jnp.sum(grad_normed * own_whitened, 0)
    grad_norm_shift = jnp.sum(grad_normed, 0)
    grad_white = grad_normed * gain
    grad_inputs = own_scaling * (
        grad_white
        - jnp.mean(grad_white, -1, keepdims=True)
        - own_whitened * jnp.mean(grad_white * own_whitened, -1, keepdims=True)
    )
    input_grad = (own_upstream + grad_inputs).astype(bf16)

    small_grads = jnp.stack([grad_norm_gain, grad_norm_shift], -1)
    small_grads = jnp.pad(small_grads, ((0, 0), (0, 128 - small_grads.shape[-1])))
    column_grads = jnp.concatenate(
        [grad_triple_weight, grad_inner_weight, small_grads], -1
    ).astype(bf16)
    column_grads = column_grads.reshape(nc, nf, shard_rows, -1).swapaxes(0, 1).reshape(width, -1)
    column_grads = lax.psum_scatter(column_grads, "fsdp", scatter_dimension=0, tiled=True)
    column_grads = replica_sum(column_grads, "rep").astype(bf16)
    column_grads = column_grads.reshape(nc, shard_rows, -1)
    column_grads = ring_all_to_all(column_grads, "ctx").astype(f32)
    grad_triple_out = (
        column_grads[:, :, : 3 * head_cols]
        .reshape(nc, shard_rows, 3, head_cols)
        .transpose(1, 2, 0, 3)
        .reshape(shard_rows, 3 * nc * head_cols)
    )
    grad_inner_out = (
        column_grads[:, :, 3 * head_cols : 3 * head_cols + ff_here]
        .transpose(1, 0, 2)
        .reshape(shard_rows, nc * ff_here)
    )
    grad_gain_out = jnp.sum(column_grads[:, :, 3 * head_cols + ff_here], 0)
    grad_shift_out = jnp.sum(column_grads[:, :, 3 * head_cols + ff_here + 1], 0)

    mixer_part = row_product[:head_cols].reshape(nf, shard_rows, width)
    outer_part = row_product[head_cols : head_cols + ff_here].reshape(nf, ff_rows, width)
    sums_part = jnp.broadcast_to(row_product[head_cols + ff_here :][None], (nf, 16, width))
    row_grads = jnp.concatenate([mixer_part, outer_part, sums_part], 1)
    row_grads = row_grads.at[:, ff_rows + shard_rows + 1, :ff_rows].set(
        grad_inner_bias.reshape(nf, ff_rows).astype(bf16)
    )
    row_grads = lax.psum_scatter(row_grads, "fsdp", scatter_dimension=0, tiled=True)
    row_grads = replica_sum(row_grads, "rep")[0]
    grad_mixer_out = row_grads[:shard_rows]
    grad_outer_out = row_grads[shard_rows : shard_rows + ff_rows]
    grad_ibias_out = row_grads[shard_rows + ff_rows + 1, :ff_rows]
    fsdp_me = lax.axis_index("fsdp")
    grad_obias_out = lax.dynamic_slice_in_dim(
        row_grads[shard_rows + ff_rows], (me * nf + fsdp_me) * shard_rows, shard_rows
    )

    return (
        layer_output[None],
        input_grad[None],
        grad_gain_out,
        grad_shift_out,
        grad_triple_out,
        grad_mixer_out,
        grad_inner_out,
        grad_ibias_out,
        grad_outer_out,
        grad_obias_out,
    )


def solution(mesh):
    placed = (
        P(("rep", "fsdp"), "ctx", None),
        P(("ctx", "fsdp")),
        P(("ctx", "fsdp")),
        P(("ctx", "fsdp"), None),
        P(("ctx", "fsdp"), None),
        P(("ctx", "fsdp"), None),
        P(("ctx", "fsdp")),
        P(("ctx", "fsdp"), None),
        P(("ctx", "fsdp")),
        P(("rep", "fsdp")),
        P(("rep", "fsdp")),
        P(("rep", "fsdp"), "ctx", None),
    )
    return jax.shard_map(
        local,
        mesh=mesh,
        in_specs=placed,
        out_specs=(
            P(("rep", "fsdp"), "ctx", None),
            P(("rep", "fsdp"), "ctx", None),
            P(("ctx", "fsdp")),
            P(("ctx", "fsdp")),
            P(("ctx", "fsdp"), None),
            P(("ctx", "fsdp"), None),
            P(("ctx", "fsdp"), None),
            P(("ctx", "fsdp")),
            P(("ctx", "fsdp"), None),
            P(("ctx", "fsdp")),
        ),
        check_vma=False,
    )
```

profile of v0, /device:TPU:0, one launch (start us, length us, event | category | flops | bytes accessed | tf_op | source)
XLA Modules:
  0.0 366.7 jit_solution(15363036287472070494)
XLA Ops:
  7.2 1.7 fusion.43
  13.9 3.2 collective-permute-start.4
  18.9 3.4 collective-permute-done.4
  22.5 2.3 collective-permute-done.5
  26.3 3.0 concatenate.73
  34.2 22.1 %collective-permute-done = bf16[256,2048]{1,0:T(8,128)(2,1)S(1)} collective-permute-done((bf16[256,2048]{1,0:T(8,128)(2,1)S(1)}, bf16[256,2048]{1,0:T(8,128)(2,1)S(1)}, u32[]{:S(2)}, u32[]{:S(2)}) %collective-permute-start) | collective-permute-done | bytes 1048608 | tf_op jit(solution)/shard_map/ppermute | solution.py:45
  61.5 8.8 %collective-permute-done.3 = bf16[128,2048]{1,0:T(8,128)(2,1)} collective-permute-done((bf16[128,2048]{1,0:T(8,128)(2,1)}, bf16[128,2048]{1,0:T(8,128)(2,1)}, u32[]{:S(2)}, u32[]{:S(2)}) %collective-permute-start.3) | collective-permute-done | bytes 524320 | tf_op jit(solution)/shard_map/ppermute | solution.py:47
  70.4 2.8 collective-permute-done.2
  76.0 1.6 copy-done
  79.6 3.4 slice.270
  85.9 21.2 %all-gather.5.cloned.1.call-done = bf16[32,32,1920]{2,1,0:T(8,128)(2,1)} async-done(((bf16[4,32,1920]{2,1,0:T(8,128)(2,1)}), bf16[32,32,1920]{2,1,0:T(8,128)(2,1)}) %all-gather.5.cloned.1.call-update) | async-done | bytes 3932176 | tf_op jit(solution)/shard_map/all_gather | solution.py:197
  107.0 2.6 copy.171
  110.4 2.3 fusion.28
  119.2 1.7 copy.174
  120.9 3.0 copy.203
  123.9 2.9 maximum_bitcast_fusion.1.k_ref
  126.8 1.6 fusion.34.q_ref
  128.4 31.0 %shard_map.195 = (bf16[4,1024,64]{2,1,0:T(8,128)(2,1)}, f32[4,1024,64]{2,1,0:T(8,128)}, f32[4,1024,64]{2,1,0:T(8,128)}, f32[4,1024,64]{2,1,0:T(8,128)}) custom-call(s32[1]{0:T(128)S(6)} %copy.228.span_ref, bf16[4,1024,64]{2,1,0:T(8,128)(2,1)} %fusion.34.q_ref, bf16[4,1024,64]{2,1,0:T(8,128)(2,1)} %maximum_bitcast_fusion.1.k_ref, ...), custom_call_target="tpu_custom_call" | custom-call | flops 3221225472 | bytes 5767168 | tf_op jit(solution)/shard_map/pallas_call | solution.py:133
  161.0 6.3 %multiply_convert_fusion = (bf16[1024,1024]{0,1:T(8,128)(2,1)S(1)}, f32[1024,1024]{0,1:T(8,128)S(1)}) fusion(f32[1024]{0:T(1024)S(1)} %bitcast.235, bf16[1024,1920]{1,0:T(8,128)(2,1)} %bitcast.175, f32[1024]{0:T(1024)S(1)} %get-tuple-element.33, f32[1024]{0:T(1024)S(1)} %get-tuple-element.34, f32[1024]{0:T(1024)S(1)} %add_rsqrt_fusion, ...), kind=kOutput, calls=%fused_computation.18 | convolution fusion | flops 2164260864 | bytes 10506240 | tf_op jit(solution)/shard_map/dot_general | solution.py:249
  167.3 4.0 %convolution_convert_fusion = bf16[1296,1024]{1,0:T(8,128)(2,1)S(1)} fusion(bf16[1024,1024]{0,1:T(8,128)(2,1)S(1)} %get-tuple-element.79, bf16[1024,256]{0,1:T(8,128)(2,1)S(1)} %bitcast.191, bf16[1024,2048]{1,0:T(8,128)(2,1)S(1)} %bitcast.163, bf16[1296]{0:T(1024)(128)(2,1)S(1)} %pad.25.clone), kind=kOutput, calls=%fused_computation.21 | convolution fusion | flops 2727198720 | bytes 7376896 | tf_op jit(solution)/shard_map/dot_general | solution.py:259
  173.0 6.3 %fusion.57 = (bf16[1024]{0:T(1024)(128)(2,1)S(1)}, bf16[1024,1024]{0,1:T(8,128)(2,1)}) fusion(f32[1024,1024]{0,1:T(8,128)S(1)} %get-tuple-element.80, f32[1024]{0:T(1024)S(1)} %bitcast.236, bf16[1024,1024]{1,0:T(8,128)(2,1)S(1)} %bitcast.201, bf16[1024,2048]{1,0:T(8,128)(2,1)S(1)} %bitcast.164), kind=kOutput, calls=%fused_computation.161 | convolution fusion | flops 2170551296 | bytes 10491904 | tf_op jit(solution)/shard_map/dot_general | solution.py:260
  181.7 4.2 %fusion = f32[1024,1024]{1,0:T(8,128)} fusion(f32[1024]{0:T(1024)S(1)} %add_rsqrt_fusion, f32[1024]{0:T(1024)S(1)} %broadcast_multiply_fusion, bf16[1024,2048]{1,0:T(8,128)(2,1)} %bitcast.160), kind=kLoop, calls=%fused_computation.4 | loop fusion | flops 3145728 | bytes 6299648 | tf_op jit(solution)/shard_map/mul | solution.py:222
  187.7 3.7 %multiply_bitcast_fusion = (f32[1024,4,64]{2,0,1:T(8,128)S(1)}, bf16[1024,4,64]{2,0,1:T(8,128)(2,1)}) fusion(f32[4,1024,64]{2,1,0:T(8,128)} %get-tuple-element.27, f32[4,1024,64]{2,1,0:T(8,128)} %get-tuple-element.29), kind=kLoop, calls=%fused_computation.32 | loop fusion | flops 524288 | bytes 3670016 | tf_op jit(solution)/shard_map/mul | solution.py:268
  191.5 2.3 copy.188
  196.6 2.1 subtract_convert_fusion.1
  199.5 1.6 pad_maximum_fusion.6
  201.0 2.4 copy.187
  205.0 3.7 %fusion.26 = f32[1024,1024]{1,0:T(8,128)S(1)} fusion(bf16[1024,1920]{1,0:T(8,128)(2,1)} %bitcast.176, bf16[1024,256]{0,1:T(8,128)(2,1)} %bitcast.217, bf16[1024,256]{0,1:T(8,128)(2,1)} %bitcast.219, bf16[1024,256]{0,1:T(8,128)(2,1)S(1)} %bitcast.221), kind=kOutput, calls=%fused_computation.45 | convolution fusion | flops 1615331328 | bytes 7340032 | tf_op jit(solution)/shard_map/dot_general | solution.py:275
  208.8 2.4 convolution_add_fusion
  213.2 2.0 collective-permute-start.9
  215.2 2.7 convolution_convert_fusion.1
  217.9 3.0 collective-permute-done.7
  221.3 3.1 collective-permute-start.10
  224.6 3.4 convolution_convert_fusion.2
  228.0 6.5 %collective-permute-done.10 = bf16[256,1024]{1,0:T(8,128)(2,1)S(1)} collective-permute-done((bf16[256,1024]{1,0:T(8,128)(2,1)S(1)}, bf16[256,1024]{1,0:T(8,128)(2,1)S(1)}, u32[]{:S(2)}, u32[]{:S(2)}) %collective-permute-start.10) | collective-permute-done | bytes 524320 | tf_op jit(solution)/shard_map/ppermute | solution.py:61
  234.5 3.5 collective-permute-done.8
  238.0 1.8 multiply_reduce_fusion
  241.7 2.3 copy.199
  244.1 4.7 %fusion.58 = f32[1024,1024]{1,0:T(8,128)S(1)} fusion(bf16[1024,1024]{0,1:T(8,128)(2,1)} %copy-done.28, bf16[1024,1024]{1,0:T(8,128)(2,1)} %bitcast.200), kind=kOutput, calls=%fused_computation.162 | convolution fusion | flops 2147483648 | bytes 8388608 | tf_op jit(solution)/shard_map/dot_general | solution.py:251
  249.6 2.1 fusion.14
  252.0 2.4 fusion.38
  254.3 36.5 %reduce-scatter.6.cloned.1.call-done = bf16[128,1920]{1,0:T(8,128)(2,1)} async-done(((bf16[1024,1920]{1,0:T(8,128)(2,1)}), bf16[128,1920]{1,0:T(8,128)(2,1)}) %reduce-scatter.6.cloned.1.call-update) | async-done | bytes 491536 | tf_op jit(solution)/shard_map/reduce_scatter | solution.py:297
  291.1 30.6 %reduce-scatter.4.cloned.1.call-done = bf16[1,256,1024]{2,1,0:T(8,128)(2,1)} async-done(((bf16[4,256,1024]{2,1,0:T(8,128)(2,1)}), bf16[1,256,1024]{2,1,0:T(8,128)(2,1)}) %reduce-scatter.4.cloned.1.call-update) | async-done | bytes 524304 | tf_op jit(solution)/shard_map/reduce_scatter | solution.py:254
  321.7 2.0 add_convert_fusion.2
  323.9 3.2 collective-permute-start.17
  328.7 8.0 %collective-permute-done.17 = bf16[1,176,1024]{2,1,0:T(8,128)(2,1)S(1)} collective-permute-done((bf16[1,176,1024]{2,1,0:T(8,128)(2,1)S(1)}, bf16[1,176,1024]{2,1,0:T(8,128)(2,1)S(1)}, u32[]{:S(2)}, u32[]{:S(2)}) %collective-permute-start.17) | collective-permute-done | bytes 360480 | tf_op jit(solution)/shard_map/ppermute | solution.py:85
  338.4 7.8 %collective-permute-done.12 = bf16[128,1920]{1,0:T(8,128)(2,1)S(1)} collective-permute-done((bf16[128,1920]{1,0:T(8,128)(2,1)S(1)}, bf16[128,1920]{1,0:T(8,128)(2,1)S(1)}, u32[]{:S(2)}, u32[]{:S(2)}) %collective-permute-start.12) | collective-permute-done | bytes 491552 | tf_op jit(solution)/shard_map/ppermute | solution.py:85
  351.3 4.8 %collective-permute-done.14 = bf16[32,1920]{1,0:T(8,128)(2,1)S(1)} collective-permute-done((bf16[32,1920]{1,0:T(8,128)(2,1)S(1)}, bf16[32,1920]{1,0:T(8,128)(2,1)S(1)}, u32[]{:S(2)}, u32[]{:S(2)}) %collective-permute-start.14) | collective-permute-done | bytes 122912 | tf_op jit(solution)/shard_map/ppermute | solution.py:70
  (204 shorter events, 61.6 us)
Async XLA Ops:
  7.2 71.1 %all-gather.7.cloned.1.call-start = ((), (), s32[]{:S(2)}) async-start(), calls=%async_computation.7 | async-start | bytes 3244032 | tf_op jit(solution)/shard_map/all_gather | solution.py:207
  9.0 98.0 %all-gather.5.cloned.1.call-start = ((), (), s32[]{:S(2)}) async-start(), calls=%async_computation.6 | async-start | bytes 4423680 | tf_op jit(solution)/shard_map/all_gather | solution.py:197
  13.9 17.3 %copy-start.18 = (bf16[1,256,1024]{2,1,0:T(8,128)(2,1)S(1)}, bf16[1,256,1024]{2,1,0:T(8,128)(2,1)}, u32[]{:S(2)}) copy-start(bf16[1,256,1024]{2,1,0:T(8,128)(2,1)} %param.25) | copy-start | bytes 1572868
  13.9 8.4 %collective-permute-start.4 = (bf16[32,1920]{1,0:T(8,128)(2,1)S(1)}, bf16[32,1920]{1,0:T(8,128)(2,1)S(1)}, u32[]{:S(2)}, u32[]{:S(2)}) collective-permute-start(bf16[32,1920]{1,0:T(8,128)(2,1)S(1)} %bitcast.226), channel_id=1, source_target_pairs={{0,24},{8,0},{16,8},{24,16},{1,25},{9,1},{17,9},{25,17},{2,26},{10... | collective-permute-start | bytes 368648 | tf_op jit(solution)/shard_map/ppermute | solution.py:70
  17.1 7.7 %collective-permute-start.5 = (bf16[32,1920]{1,0:T(8,128)(2,1)S(1)}, bf16[32,1920]{1,0:T(8,128)(2,1)S(1)}, u32[]{:S(2)}, u32[]{:S(2)}) collective-permute-start(bf16[32,1920]{1,0:T(8,128)(2,1)S(1)} %bitcast.228), channel_id=1, source_target_pairs={{0,16},{8,24},{16,0},{24,8},{1,17},{9,25},{17,1},{25,9},{2,18},{10... | collective-permute-start | bytes 368648 | tf_op jit(solution)/shard_map/ppermute | solution.py:70
  17.8 13.5 %copy-start.16 = (bf16[1,256,1024]{2,1,0:T(8,128)(2,1)S(1)}, bf16[1,256,1024]{2,1,0:T(8,128)(2,1)}, u32[]{:S(2)}) copy-start(bf16[1,256,1024]{2,1,0:T(8,128)(2,1)} %param.14) | copy-start | bytes 1572868
  17.9 8.3 %collective-permute-start.6 = (bf16[32,1920]{1,0:T(8,128)(2,1)S(1)}, bf16[32,1920]{1,0:T(8,128)(2,1)S(1)}, u32[]{:S(2)}, u32[]{:S(2)}) collective-permute-start(bf16[32,1920]{1,0:T(8,128)(2,1)S(1)} %bitcast.230), channel_id=1, source_target_pairs={{0,8},{8,16},{16,24},{24,0},{1,9},{9,17},{17,25},{25,1},{2,10},{10... | collective-permute-start | bytes 368648 | tf_op jit(solution)/shard_map/ppermute | solution.py:70
  30.5 221.4 %reduce-scatter.8.cloned.1.call-start = ((), (), s32[]{:S(2)}) async-start(), calls=%async_computation.5 | async-start | bytes 3244032 | tf_op jit(solution)/shard_map/reduce_scatter | solution.py:322
  31.5 24.9 %collective-permute-start = (bf16[256,2048]{1,0:T(8,128)(2,1)S(1)}, bf16[256,2048]{1,0:T(8,128)(2,1)S(1)}, u32[]{:S(2)}, u32[]{:S(2)}) collective-permute-start(bf16[256,2048]{1,0:T(8,128)(2,1)S(1)} %get-tuple-element.51), channel_id=1, source_target_pairs={{0,24},{8,0},{16,8},{24,16},{1,25},{9,1},{17,9},{25,17},{2,26},{10... | collective-permute-start | bytes 3145736 | tf_op jit(solution)/shard_map/ppermute | solution.py:45
  32.1 26.6 %collective-permute-start.1 = (bf16[256,2048]{1,0:T(8,128)(2,1)S(1)}, bf16[256,2048]{1,0:T(8,128)(2,1)S(1)}, u32[]{:S(2)}, u32[]{:S(2)}) collective-permute-start(bf16[256,2048]{1,0:T(8,128)(2,1)S(1)} %get-tuple-element.51), channel_id=1, source_target_pairs={{0,8},{8,16},{16,24},{24,0},{1,9},{9,17},{17,25},{25,1},{2,10},{10... | collective-permute-start | bytes 3145736 | tf_op jit(solution)/shard_map/ppermute | solution.py:44
  57.2 13.1 %collective-permute-start.3 = (bf16[128,2048]{1,0:T(8,128)(2,1)}, bf16[128,2048]{1,0:T(8,128)(2,1)}, u32[]{:S(2)}, u32[]{:S(2)}) collective-permute-start(bf16[128,2048]{1,0:T(8,128)(2,1)} %slice.250), channel_id=1, source_target_pairs={{0,24},{8,0},{16,8},{24,16},{1,25},{9,1},{17,9},{25,17},{2,26},{10... | collective-permute-start | bytes 1572872 | tf_op jit(solution)/shard_map/ppermute | solution.py:47
  59.5 13.6 %collective-permute-start.2 = (bf16[128,2048]{1,0:T(8,128)(2,1)}, bf16[128,2048]{1,0:T(8,128)(2,1)}, u32[]{:S(2)}, u32[]{:S(2)}) collective-permute-start(bf16[128,2048]{1,0:T(8,128)(2,1)} %slice.249), channel_id=1, source_target_pairs={{0,8},{8,16},{16,24},{24,0},{1,9},{9,17},{17,25},{25,1},{2,10},{10... | collective-permute-start | bytes 1572872 | tf_op jit(solution)/shard_map/ppermute | solution.py:46
  60.2 15.4 %copy-start.24 = (s32[1,1,4,256]{3,1,2,0:T(1,128)}, s32[1,1,4,256]{3,1,2,0:T(1,128)S(1)}, u32[]{:S(2)}) copy-start(s32[1,1,4,256]{3,1,2,0:T(1,128)S(1)} %copy.209) | copy-start | bytes 12292
  78.3 4.7 %copy-start.1 = (bf16[4,256,2048]{2,1,0:T(8,128)(2,1)S(1)}, bf16[4,256,2048]{2,1,0:T(8,128)(2,1)}, u32[]{:S(2)}) copy-start(bf16[4,256,2048]{2,1,0:T(8,128)(2,1)} %copy-done) | copy-start | bytes 12582916
  79.6 4.2 %copy-start.13 = (bf16[8,32,1024]{2,1,0:T(8,128)(2,1)}, bf16[8,32,1024]{2,1,0:T(8,128)(2,1)S(1)}, u32[]{:S(2)}) copy-start(bf16[8,32,1024]{2,1,0:T(8,128)(2,1)S(1)} %slice.267) | copy-start | bytes 1572868
  107.0 3.4 copy-start.2
  109.7 3.0 copy-start.7
  110.2 50.8 %copy-start.25 = (f32[1024]{0:T(1024)}, f32[1024]{0:T(1024)S(1)}, u32[]{:S(2)}) copy-start(f32[1024]{0:T(1024)S(1)} %get-tuple-element.33) | copy-start | bytes 12292
  123.9 2.9 copy-start.6
  160.9 6.3 %copy-start.11 = (bf16[1024,4,64]{0,2,1:T(8,128)(2,1)}, bf16[1024,4,64]{0,2,1:T(8,128)(2,1)S(1)}, u32[]{:S(2)}) copy-start(bf16[1024,4,64]{0,2,1:T(8,128)(2,1)S(1)} %copy.181) | copy-start | bytes 1572868
  161.0 6.3 %copy-start.3 = (bf16[4,256,2048]{2,1,0:T(8,128)(2,1)S(1)}, bf16[4,256,2048]{2,1,0:T(8,128)(2,1)}, u32[]{:S(2)}) copy-start(bf16[4,256,2048]{2,1,0:T(8,128)(2,1)} %copy-done) | copy-start | bytes 12582916
  167.3 4.1 %copy-start.28 = (bf16[1024,1024]{0,1:T(8,128)(2,1)}, bf16[1024,1024]{0,1:T(8,128)(2,1)S(1)}, u32[]{:S(2)}) copy-start(bf16[1024,1024]{0,1:T(8,128)(2,1)S(1)} %get-tuple-element.79) | copy-start | bytes 6291460
  181.4 4.5 %copy-start.9 = (f32[4,1024,64]{2,1,0:T(8,128)S(1)}, f32[4,1024,64]{2,1,0:T(8,128)}, u32[]{:S(2)}) copy-start(f32[4,1024,64]{2,1,0:T(8,128)} %get-tuple-element.28) | copy-start | bytes 3145732
  181.4 109.4 %reduce-scatter.6.cloned.1.call-start = ((), (), s32[]{:S(2)}) async-start(), calls=%async_computation.4 | async-start | bytes 4423680 | tf_op jit(solution)/shard_map/reduce_scatter | solution.py:297
  198.9 5.2 %copy-start.10 = (bf16[1024,4,32]{2,0,1:T(8,128)(2,1)S(1)}, bf16[1024,4,32]{2,0,1:T(8,128)(2,1)}, u32[]{:S(2)}) copy-start(bf16[1024,4,32]{2,0,1:T(8,128)(2,1)} %slice.379) | copy-start | bytes 786436
  199.4 3.9 %copy-start.22 = (bf16[1024,4,16,1]{0,1,3,2:T(4,128)(2,1)S(1)}, bf16[1024,4,16,1]{0,1,3,2:T(4,128)(2,1)}, u32[]{:S(2)}) copy-start(bf16[1024,4,16,1]{0,1,3,2:T(4,128)(2,1)} %get-tuple-element.55) | copy-start | bytes 393220
  205.0 3.8 %copy-start.8 = (bf16[4,8,32,1920]{3,2,1,0:T(8,128)(2,1)S(1)}, bf16[4,8,32,1920]{3,2,1,0:T(8,128)(2,1)}, u32[]{:S(2)}) copy-start(bf16[4,8,32,1920]{3,2,1,0:T(8,128)(2,1)} %copy-done.7) | copy-start | bytes 11796484
  205.0 3.8 %copy-start.27 = (bf16[1024,1024]{0,1:T(8,128)(2,1)S(1)}, bf16[1024,1024]{0,1:T(8,128)(2,1)}, u32[]{:S(2)}) copy-start(bf16[1024,1024]{0,1:T(8,128)(2,1)} %get-tuple-element.82) | copy-start | bytes 6291460
  211.2 4.0 %copy-start.4 = (bf16[4,256,2048]{2,1,0:T(8,128)(2,1)S(1)}, bf16[4,256,2048]{2,1,0:T(8,128)(2,1)}, u32[]{:S(2)}) copy-start(bf16[4,256,2048]{2,1,0:T(8,128)(2,1)} %copy-done) | copy-start | bytes 12582916
  211.2 4.0 %copy-start.26 = (f32[1024]{0:T(1024)S(1)}, f32[1024]{0:T(1024)}, u32[]{:S(2)}) copy-start(f32[1024]{0:T(1024)} %copy-done.25) | copy-start | bytes 12292
  211.7 9.3 %collective-permute-start.7 = (bf16[128,1024]{1,0:T(8,128)(2,1)S(1)}, bf16[128,1024]{1,0:T(8,128)(2,1)S(1)}, u32[]{:S(2)}, u32[]{:S(2)}) collective-permute-start(bf16[128,1024]{1,0:T(8,128)(2,1)S(1)} %get-tuple-element.44), channel_id=1, source_target_pairs={{0,8},{8,16},{16,24},{24,0},{1,9},{9,17},{17,25},{25,1},{2,10},{10... | collective-permute-start | bytes 786440 | tf_op jit(solution)/shard_map/ppermute | solution.py:56
  213.2 7.9 %collective-permute-start.9 = (bf16[128,1024]{1,0:T(8,128)(2,1)S(1)}, bf16[128,1024]{1,0:T(8,128)(2,1)S(1)}, u32[]{:S(2)}, u32[]{:S(2)}) collective-permute-start(bf16[128,1024]{1,0:T(8,128)(2,1)S(1)} %get-tuple-element.45), channel_id=1, source_target_pairs={{0,24},{8,0},{16,8},{24,16},{1,25},{9,1},{17,9},{25,17},{2,26},{10... | collective-permute-start | bytes 786440 | tf_op jit(solution)/shard_map/ppermute | solution.py:57
  217.9 6.6 %copy-start.20 = (bf16[1024,4,64]{0,2,1:T(8,128)(2,1)S(1)}, bf16[1024,4,64]{0,2,1:T(8,128)(2,1)}, u32[]{:S(2)}) copy-start(bf16[1024,4,64]{0,2,1:T(8,128)(2,1)} %copy.188) | copy-start | bytes 1572868
  217.9 6.6 %copy-start.21 = (bf16[1024,4,64]{0,2,1:T(8,128)(2,1)S(1)}, bf16[1024,4,64]{0,2,1:T(8,128)(2,1)}, u32[]{:S(2)}) copy-start(bf16[1024,4,64]{0,2,1:T(8,128)(2,1)} %copy.187) | copy-start | bytes 1572868
  221.3 13.2 %collective-permute-start.10 = (bf16[256,1024]{1,0:T(8,128)(2,1)S(1)}, bf16[256,1024]{1,0:T(8,128)(2,1)S(1)}, u32[]{:S(2)}, u32[]{:S(2)}) collective-permute-start(bf16[256,1024]{1,0:T(8,128)(2,1)S(1)} %pad_maximum_fusion.11), channel_id=1, source_target_pairs={{0,24},{8,0},{16,8},{24,16},{1,25},{9,1},{17,9},{25,17},{2,26},{10... | collective-permute-start | bytes 1572872 | tf_op jit(solution)/shard_map/ppermute | solution.py:61
  224.5 13.6 %collective-permute-start.8 = (bf16[256,1024]{1,0:T(8,128)(2,1)S(1)}, bf16[256,1024]{1,0:T(8,128)(2,1)S(1)}, u32[]{:S(2)}, u32[]{:S(2)}) collective-permute-start(bf16[256,1024]{1,0:T(8,128)(2,1)S(1)} %pad_maximum_fusion.10), channel_id=1, source_target_pairs={{0,8},{8,16},{16,24},{24,0},{1,9},{9,17},{17,25},{25,1},{2,10},{10... | collective-permute-start | bytes 1572872 | tf_op jit(solution)/shard_map/ppermute | solution.py:60
  244.0 4.8 %copy-start.12 = (bf16[1024,4,64]{0,2,1:T(8,128)(2,1)S(1)}, bf16[1024,4,64]{0,2,1:T(8,128)(2,1)}, u32[]{:S(2)}) copy-start(bf16[1024,4,64]{0,2,1:T(8,128)(2,1)} %copy-done.11) | copy-start | bytes 1572868
  244.0 4.8 %copy-start.14 = (bf16[8,32,1024]{2,1,0:T(8,128)(2,1)S(1)}, bf16[8,32,1024]{2,1,0:T(8,128)(2,1)}, u32[]{:S(2)}) copy-start(bf16[8,32,1024]{2,1,0:T(8,128)(2,1)} %copy-done.13) | copy-start | bytes 1572868
  244.0 77.7 %reduce-scatter.4.cloned.1.call-start = ((), (), s32[]{:S(2)}) async-start(), calls=%async_computation.3 | async-start | bytes 2621440 | tf_op jit(solution)/shard_map/reduce_scatter | solution.py:254
  249.6 72.1 %copy-start.17 = (bf16[1,256,1024]{2,1,0:T(8,128)(2,1)S(1)}, bf16[1,256,1024]{2,1,0:T(8,128)(2,1)}, u32[]{:S(2)}) copy-start(bf16[1,256,1024]{2,1,0:T(8,128)(2,1)} %param.14) | copy-start | bytes 1572868
  251.9 71.9 %copy-start.23 = (bf16[1,176,1024]{2,1,0:T(8,128)(2,1)S(1)}, bf16[1,176,1024]{2,1,0:T(8,128)(2,1)}, u32[]{:S(2)}) copy-start(bf16[1,176,1024]{2,1,0:T(8,128)(2,1)} %reduce-scatter.8.cloned.1.call-done) | copy-start | bytes 1081348
  251.9 71.9 %collective-permute-start.16 = (bf16[1,176,1024]{2,1,0:T(8,128)(2,1)}, bf16[1,176,1024]{2,1,0:T(8,128)(2,1)S(1)}, u32[]{:S(2)}, u32[]{:S(2)}) collective-permute-start(bf16[1,176,1024]{2,1,0:T(8,128)(2,1)} %reduce-scatter.8.cloned.1.call-done), channel_id=1, source_target_pairs={{0,32},{32,0},{64,96},{96,64},{1,33},{33,1},{65,97},{97,65},{2,34}... | collective-permute-start | bytes 1081352 | tf_op jit(solution)/shard_map/ppermute | solution.py:83
  290.8 36.3 %collective-permute-start.11 = (bf16[128,1920]{1,0:T(8,128)(2,1)}, bf16[128,1920]{1,0:T(8,128)(2,1)S(1)}, u32[]{:S(2)}, u32[]{:S(2)}) collective-permute-start(bf16[128,1920]{1,0:T(8,128)(2,1)} %reduce-scatter.6.cloned.1.call-done), channel_id=1, source_target_pairs={{0,32},{32,0},{64,96},{96,64},{1,33},{33,1},{65,97},{97,65},{2,34}... | collective-permute-start | bytes 1474568 | tf_op jit(solution)/shard_map/ppermute | solution.py:83
  323.9 12.9 %collective-permute-start.17 = (bf16[1,176,1024]{2,1,0:T(8,128)(2,1)S(1)}, bf16[1,176,1024]{2,1,0:T(8,128)(2,1)S(1)}, u32[]{:S(2)}, u32[]{:S(2)}) collective-permute-start(bf16[1,176,1024]{2,1,0:T(8,128)(2,1)S(1)} %add_convert_fusion.5), channel_id=1, source_target_pairs={{0,64},{32,96},{64,0},{96,32},{1,65},{33,97},{65,1},{97,33},{2,66}... | collective-permute-start | bytes 1081352 | tf_op jit(solution)/shard_map/ppermute | solution.py:85
  328.2 17.9 %collective-permute-start.12 = (bf16[128,1920]{1,0:T(8,128)(2,1)S(1)}, bf16[128,1920]{1,0:T(8,128)(2,1)S(1)}, u32[]{:S(2)}, u32[]{:S(2)}) collective-permute-start(bf16[128,1920]{1,0:T(8,128)(2,1)S(1)} %add_convert_fusion.4), channel_id=1, source_target_pairs={{0,64},{32,96},{64,0},{96,32},{1,65},{33,97},{65,1},{97,33},{2,66}... | collective-permute-start | bytes 1474568 | tf_op jit(solution)/shard_map/ppermute | solution.py:85
  346.4 4.9 %collective-permute-start.13 = (bf16[32,1920]{1,0:T(8,128)(2,1)S(1)}, bf16[32,1920]{1,0:T(8,128)(2,1)S(1)}, u32[]{:S(2)}, u32[]{:S(2)}) collective-permute-start(bf16[32,1920]{1,0:T(8,128)(2,1)S(1)} %get-tuple-element.65), channel_id=1, source_target_pairs={{0,24},{8,0},{16,8},{24,16},{1,25},{9,1},{17,9},{25,17},{2,26},{10... | collective-permute-start | bytes 368648 | tf_op jit(solution)/shard_map/ppermute | solution.py:70
  348.4 8.0 %collective-permute-start.15 = (bf16[32,1920]{1,0:T(8,128)(2,1)S(1)}, bf16[32,1920]{1,0:T(8,128)(2,1)S(1)}, u32[]{:S(2)}, u32[]{:S(2)}) collective-permute-start(bf16[32,1920]{1,0:T(8,128)(2,1)S(1)} %get-tuple-element.62), channel_id=1, source_target_pairs={{0,8},{8,16},{16,24},{24,0},{1,9},{9,17},{17,25},{25,1},{2,10},{10... | collective-permute-start | bytes 368648 | tf_op jit(solution)/shard_map/ppermute | solution.py:70
  349.6 6.6 %collective-permute-start.14 = (bf16[32,1920]{1,0:T(8,128)(2,1)S(1)}, bf16[32,1920]{1,0:T(8,128)(2,1)S(1)}, u32[]{:S(2)}, u32[]{:S(2)}) collective-permute-start(bf16[32,1920]{1,0:T(8,128)(2,1)S(1)} %get-tuple-element.64), channel_id=1, source_target_pairs={{0,16},{8,24},{16,0},{24,8},{1,17},{9,25},{17,1},{25,9},{2,18},{10... | collective-permute-start | bytes 368648 | tf_op jit(solution)/shard_map/ppermute | solution.py:70
  (4 other events, 7.5 us)
Sparse Core Ops, SparseCore 0:
  10.2 45.4 all-gather.6
  57.4 49.5 all-gather.4
  181.5 44.4 reduce-scatter.7
  244.1 46.6 reduce-scatter.5
  293.0 28.6 reduce-scatter.3
where the time goes:
time: 373 us; the launch traced here: 367 us
  waiting for transfers between devices  163 us (44%)
  local copies, waits for them, and re-layouts  55 us (15%)
  other arithmetic  39.5 us (11%)
  matrix products  37.4 us (10%)
  Pallas kernels  31 us (8%)
  starting transfers between devices  23.8 us (6%)
  between operations  16.7 us (4%)
    reduce_scatter x1, waiting for transfers between devices, local(): lax.psum_scatter(column_grads, 'fsdp', scatter_dimension=0, tiled=True)  36.5 us
    pallas_call x1, Pallas kernels, fused_attention(): pl.pallas_call(attention_kernel, out_shape=(jax.ShapeDtypeStruct((heads,...  31 us
    reduce_scatter x1, waiting for transfers between devices, local(): lax.psum_scatter(block_sum, 'ctx', scatter_dimension=0, tiled=True)[0]  30.6 us
    ppermute x1, waiting for transfers between devices, ring_gather(): from_right = lax.ppermute(block, axis, ring_pairs(n, -1))  22.1 us
    all_gather x1, waiting for transfers between devices, local(): column_block = lax.all_gather(column_payload, 'fsdp', axis=0, tiled=False)  21.2 us
    ppermute x2, waiting for transfers between devices, replica_sum(): lax.ppermute(pair, axis, [(i, i ^ 2) for i in range(n)]).astype(f32)  15.8 us
    ppermute x6, waiting for transfers between devices, ring_all_to_all(): lax.ppermute(pick(me + s), axis, ring_pairs(n, s))  12.2 us
    unnamed x75, local copies, waits for them, and re-layouts  10.8 us
  transfers between devices with their start and end apart: 23, of which 18 were waited for; matrix products, arithmetic and copies ran while one was open for 22% of the time, Pallas kernels for 0%

commit v1 on v0

--- a/solution.py
+++ b/solution.py
@@ -249,9 +249,7 @@
     preact = jnp.dot(normed, inner_here, preferred_element_type=f32) + ibias_here
     gelu_result = jax.nn.gelu(preact, approximate=True).astype(bf16)
     feedforward = jnp.dot(gelu_result, outer_here, preferred_element_type=f32)
-    block_sum = (attention + feedforward).astype(bf16).reshape(nc, own_rows, width)
-    block_sum = lax.dynamic_slice_in_dim(jnp.concatenate([block_sum, block_sum], 0), nc - me, nc, 0)
-    block_sum = lax.psum_scatter(block_sum, "ctx", scatter_dimension=0, tiled=True)[0].astype(f32)
+    block_sum = ring_scatter((attention + feedforward).reshape(nc, own_rows, width), "ctx")
     layer_output = (tokens[0].astype(f32) + block_sum + obias).astype(bf16)
 
     ones_block = jnp.ones((length, 16), bf16)
@@ -274,12 +272,12 @@
     grad_triple_weight = jnp.dot(normed.T, grad_query_key_value, preferred_element_type=f32)
     grad_normed = jnp.dot(grad_query_key_value, triple_here.T, preferred_element_type=f32)
     grad_normed = grad_normed + jnp.dot(grad_before_gelu, inner_here.T, preferred_element_type=f32)
+    grad_norm_gain = jnp.sum(grad_normed * whitened, 0)
+    grad_norm_shift = jnp.sum(grad_normed, 0)
     grad_normed = ring_scatter(grad_normed.reshape(nc, own_rows, width), "ctx")
 
     own_whitened = whitened[:own_rows]
     own_scaling = scaling[:own_rows]
-    grad_norm_gain = jnp.sum(grad_normed * own_whitened, 0)
-    grad_norm_shift = jnp.sum(grad_normed, 0)
     grad_white = grad_normed * gain
     grad_inputs = own_scaling * (
         grad_white

time: 373 us -> 333 us (0.89)
  waiting for transfers between devices: 163 us -> 110 us
  starting transfers between devices: 23.8 us -> 30.7 us
  local copies, waits for them, and re-layouts: 55 us -> 61.7 us
    reduce_scatter x1 -> x0, waiting for transfers between devices: 30.6 us -> none  [local(): lax.psum_scatter(block_sum, 'ctx', scatter_dimension=0, tiled=True)[0]]
    reduce_scatter x1, waiting for transfers between devices: 36.5 us -> 8.05 us  [local(): lax.psum_scatter(column_grads, 'fsdp', scatter_dimension=0, tiled=True)]
    ppermute x1 -> x2, waiting for transfers between devices: 6.54 us -> 12.3 us  [ring_scatter(): from_right = lax.ppermute(to_left.astype(wire), axis, ring_pairs(n, -1))]
    another operation x4 -> x6, other arithmetic: 2.88 us -> 8.13 us
    mul x1 -> x0, other arithmetic: 4.25 us -> none  [local(): whitened = center * scaling]
    unnamed x75 -> x83, local copies, waits for them, and re-layouts: 10.8 us -> 13.4 us
  transfers between devices with their start and end apart: 23 -> 26, of which waited for: 18 -> 18; matrix products, arithmetic and copies ran while one was open for 22% -> 26% of each run, Pallas kernels for 0% -> 0%
where the time goes in v1:
time: 333 us; the launch traced here: 327 us
  waiting for transfers between devices  110 us (33%)
  local copies, waits for them, and re-layouts  61.7 us (19%)
  matrix products  39.1 us (12%)
  other arithmetic  38 us (11%)
  Pallas kernels  31.2 us (9%)
  starting transfers between devices  30.7 us (9%)
  between operations  16.3 us (5%)
    pallas_call x1, Pallas kernels, fused_attention(): pl.pallas_call(attention_kernel, out_shape=(jax.ShapeDtypeStruct((heads,...  31.2 us
    ppermute x1, waiting for transfers between devices, ring_gather(): from_right = lax.ppermute(block, axis, ring_pairs(n, -1))  22.1 us
    all_gather x1, waiting for transfers between devices, local(): column_block = lax.all_gather(column_payload, 'fsdp', axis=0, tiled=False)  21.4 us
    ppermute x2, waiting for transfers between devices, replica_sum(): lax.ppermute(pair, axis, [(i, i ^ 2) for i in range(n)]).astype(f32)  17.4 us
    unnamed x83, local copies, waits for them, and re-layouts  13.4 us
    ppermute x6, waiting for transfers between devices, ring_all_to_all(): lax.ppermute(pick(me + s), axis, ring_pairs(n, s))  13 us
    ppermute x2, waiting for transfers between devices, ring_scatter(): from_right = lax.ppermute(to_left.astype(wire), axis, ring_pairs(n, -1))  12.3 us
    ppermute x6, starting transfers between devices, ring_all_to_all(): lax.ppermute(pick(me + s), axis, ring_pairs(n, s))  10 us
  transfers between devices with their start and end apart: 26, of which 18 were waited for; matrix products, arithmetic and copies ran while one was open for 26% of the time, Pallas kernels for 0%

profile of v1, /device:TPU:0, one launch (start us, length us, event | category | flops | bytes accessed | tf_op | source)
XLA Modules:
  0.0 326.9 jit_solution(13501484469528198634)
XLA Ops:
  7.2 1.7 fusion.52
  14.0 3.2 collective-permute-start.4
  18.9 3.4 %collective-permute-done.4 = bf16[32,1920]{1,0:T(8,128)(2,1)S(1)} collective-permute-done((bf16[32,1920]{1,0:T(8,128)(2,1)S(1)}, bf16[32,1920]{1,0:T(8,128)(2,1)S(1)}, u32[]{:S(2)}, u32[]{:S(2)}) %collective-permute-start.4) | collective-permute-done | bytes 122912 | tf_op jit(solution)/shard_map/ppermute | solution.py:70
  22.5 2.3 collective-permute-done.5
  26.3 3.0 concatenate.78
  34.3 22.1 %collective-permute-done = bf16[256,2048]{1,0:T(8,128)(2,1)S(1)} collective-permute-done((bf16[256,2048]{1,0:T(8,128)(2,1)S(1)}, bf16[256,2048]{1,0:T(8,128)(2,1)S(1)}, u32[]{:S(2)}, u32[]{:S(2)}) %collective-permute-start) | collective-permute-done | bytes 1048608 | tf_op jit(solution)/shard_map/ppermute | solution.py:45
  61.6 8.8 %collective-permute-done.3 = bf16[128,2048]{1,0:T(8,128)(2,1)} collective-permute-done((bf16[128,2048]{1,0:T(8,128)(2,1)}, bf16[128,2048]{1,0:T(8,128)(2,1)}, u32[]{:S(2)}, u32[]{:S(2)}) %collective-permute-start.3) | collective-permute-done | bytes 524320 | tf_op jit(solution)/shard_map/ppermute | solution.py:47
  70.4 2.8 collective-permute-done.2
  79.3 3.5 %slice.303 = bf16[8,128,1024]{2,1,0:T(8,128)(2,1)} slice(bf16[8,176,1024]{2,1,0:T(8,128)(2,1)} %bitcast.211), slice={[0:8], [32:160], [0:1024]} | slice | bytes 4194304 | tf_op jit(solution)/shard_map/slice | solution.py:209
  85.6 21.4 %all-gather.5.cloned.1.call-done = bf16[32,32,1920]{2,1,0:T(8,128)(2,1)} async-done(((bf16[4,32,1920]{2,1,0:T(8,128)(2,1)}), bf16[32,32,1920]{2,1,0:T(8,128)(2,1)}) %all-gather.5.cloned.1.call-update) | async-done | bytes 3932176 | tf_op jit(solution)/shard_map/all_gather | solution.py:197
  107.0 2.6 copy.171
  110.4 2.3 fusion.27
  119.1 1.7 copy.174
  120.7 3.0 copy.203
  123.8 3.0 maximum_bitcast_fusion.1.k_ref
  128.4 31.2 %shard_map.195 = (bf16[4,1024,64]{2,1,0:T(8,128)(2,1)}, f32[4,1024,64]{2,1,0:T(8,128)}, f32[4,1024,64]{2,1,0:T(8,128)}, f32[4,1024,64]{2,1,0:T(8,128)}) custom-call(s32[1]{0:T(128)S(6)} %copy.228.span_ref, bf16[4,1024,64]{2,1,0:T(8,128)(2,1)} %fusion.33.q_ref, bf16[4,1024,64]{2,1,0:T(8,128)(2,1)} %maximum_bitcast_fusion.1.k_ref, ...), custom_call_target="tpu_custom_call" | custom-call | flops 3221225472 | bytes 5767168 | tf_op jit(solution)/shard_map/pallas_call | solution.py:133
  161.2 6.3 %multiply_convert_fusion = (bf16[1024,1024]{0,1:T(8,128)(2,1)S(1)}, f32[1024,1024]{0,1:T(8,128)S(1)}) fusion(f32[1024]{0:T(1024)S(1)} %bitcast.259, bf16[1024,1920]{1,0:T(8,128)(2,1)} %bitcast.198, f32[1024]{0:T(1024)S(1)} %get-tuple-element.33, f32[1024]{0:T(1024)S(1)} %get-tuple-element.34, f32[1024]{0:T(1024)S(1)} %add_rsqrt_fusion, ...), kind=kOutput, calls=%fused_computation.16 | convolution fusion | flops 2164260864 | bytes 10506240 | tf_op jit(solution)/shard_map/dot_general | solution.py:249
  167.5 4.0 %convolution_convert_fusion = bf16[1296,1024]{1,0:T(8,128)(2,1)S(1)} fusion(bf16[1024,1024]{0,1:T(8,128)(2,1)S(1)} %get-tuple-element.86, bf16[1024,256]{0,1:T(8,128)(2,1)S(1)} %bitcast.215, bf16[1024,2048]{1,0:T(8,128)(2,1)S(1)} %bitcast.188, bf16[1296]{0:T(1024)(128)(2,1)S(1)} %pad.25.clone), kind=kOutput, calls=%fused_computation.19 | convolution fusion | flops 2727198720 | bytes 7376896 | tf_op jit(solution)/shard_map/dot_general | solution.py:257
  173.1 6.3 %fusion.67 = (bf16[1024]{0:T(1024)(128)(2,1)S(1)}, bf16[1024,1024]{0,1:T(8,128)(2,1)}) fusion(f32[1024,1024]{0,1:T(8,128)S(1)} %get-tuple-element.87, f32[1024]{0:T(1024)S(1)} %bitcast.260, bf16[1024,1024]{1,0:T(8,128)(2,1)S(1)} %bitcast.224, bf16[1024,2048]{1,0:T(8,128)(2,1)S(1)} %bitcast.189), kind=kOutput, calls=%fused_computation.176 | convolution fusion | flops 2170551296 | bytes 10491904 | tf_op jit(solution)/shard_map/dot_general | solution.py:258
  181.7 1.9 slice.446
  183.6 3.0 copy.185
  186.7 3.5 %multiply_bitcast_fusion = (f32[1024,4,64]{2,0,1:T(8,128)S(1)}, bf16[1024,4,64]{2,0,1:T(8,128)(2,1)}) fusion(f32[4,1024,64]{2,1,0:T(8,128)} %get-tuple-element.27, f32[4,1024,64]{2,1,0:T(8,128)} %get-tuple-element.29), kind=kLoop, calls=%fused_computation.30 | loop fusion | flops 524288 | bytes 3670016 | tf_op jit(solution)/shard_map/mul | solution.py:266
  190.2 2.3 copy.188
  195.3 2.1 subtract_convert_fusion.1
  199.8 2.4 copy.187
  204.6 3.9 %fusion.25 = f32[1024,1024]{1,0:T(8,128)S(1)} fusion(bf16[1024,1920]{1,0:T(8,128)(2,1)} %bitcast.199, bf16[1024,256]{0,1:T(8,128)(2,1)} %bitcast.241, bf16[1024,256]{0,1:T(8,128)(2,1)} %bitcast.243, bf16[1024,256]{0,1:T(8,128)(2,1)} %bitcast.245), kind=kOutput, calls=%fused_computation.43 | convolution fusion | flops 1615331328 | bytes 7340032 | tf_op jit(solution)/shard_map/dot_general | solution.py:273
  209.7 5.6 %multiply_reduce_fusion = (bf16[1024]{0:T(1024)(128)(2,1)S(1)}, bf16[1024]{0:T(1024)(128)(2,1)S(1)}, f32[1024,1024]{1,0:T(8,128)}, f32[1024,1024]{1,0:T(8,128)}) fusion(f32[1024]{0:T(1024)S(1)} %add_rsqrt_fusion, f32[1024]{0:T(1024)S(1)} %broadcast_multiply_fusion, bf16[1024,2048]{1,0:T(8,128)(2,1)S(1)} %bitcast.190, f32[1024,1024]{1,0:T(8,128)S(1)} %fusion.25, ...), kind=kOutput, calls=%fused_computation.15 | convolution fusion | flops 2154821632 | bytes 18886656 | tf_op jit(solution)/shard_map/dot_general | solution.py:274
  215.6 4.1 %convolution_convert_fusion.2 = bf16[1024,768]{1,0:T(8,128)(2,1)S(1)} fusion(bf16[1024,256]{0,1:T(8,128)(2,1)S(1)} %bitcast.242, bf16[1024,256]{0,1:T(8,128)(2,1)S(1)} %bitcast.244, bf16[1024,256]{0,1:T(8,128)(2,1)} %bitcast.246, f32[1024]{0:T(1024)S(1)} %copy-done.30, f32[1024]{0:T(1024)S(1)} %get-tuple-element.34, f32[1024]{0:T(1024)S(1)} %add_rsqrt_fusion, ...), kind=kOutput, calls=%fused_computation.36 | convolution fusion | flops 1622409216 | bytes 5259264 | tf_op jit(solution)/shard_map/dot_general | solution.py:272
  219.7 2.7 convolution_convert_fusion.1
  222.8 2.3 copy.199
  225.1 2.7 convert.120
  229.4 1.8 collective-permute-start.13
  231.2 2.4 fusion.68
  236.7 3.2 collective-permute-start.9
  242.4 1.7 collective-permute-start.12
  248.0 3.8 %collective-permute-start.10 = (bf16[256,1024]{1,0:T(8,128)(2,1)S(1)}, bf16[256,1024]{1,0:T(8,128)(2,1)S(1)}, u32[]{:S(2)}, u32[]{:S(2)}) collective-permute-start(bf16[256,1024]{1,0:T(8,128)(2,1)S(1)} %pad_maximum_fusion.11), channel_id=1, source_target_pairs={{0,24},{8,0},{16,8},{24,16},{1,25},{9,1},{17,9},{25,17},{2,26},{10... | collective-permute-start | bytes 1572872 | tf_op jit(solution)/shard_map/ppermute | solution.py:61
  251.9 5.9 %collective-permute-done.14 = bf16[256,1024]{1,0:T(8,128)(2,1)S(1)} collective-permute-done((bf16[256,1024]{1,0:T(8,128)(2,1)S(1)}, bf16[256,1024]{1,0:T(8,128)(2,1)S(1)}, u32[]{:S(2)}, u32[]{:S(2)}) %collective-permute-start.14) | collective-permute-done | bytes 524320 | tf_op jit(solution)/shard_map/ppermute | solution.py:61
  258.7 1.9 fusion.63
  260.7 6.3 %collective-permute-done.10 = bf16[256,1024]{1,0:T(8,128)(2,1)S(1)} collective-permute-done((bf16[256,1024]{1,0:T(8,128)(2,1)S(1)}, bf16[256,1024]{1,0:T(8,128)(2,1)S(1)}, u32[]{:S(2)}, u32[]{:S(2)}) %collective-permute-start.10) | collective-permute-done | bytes 524320 | tf_op jit(solution)/shard_map/ppermute | solution.py:61
  267.5 2.4 fusion.43
  269.9 8.0 %reduce-scatter.3.cloned.1.call-done = bf16[128,1920]{1,0:T(8,128)(2,1)} async-done(((bf16[1024,1920]{1,0:T(8,128)(2,1)}), bf16[128,1920]{1,0:T(8,128)(2,1)}) %reduce-scatter.3.cloned.1.call-update) | async-done | bytes 491536 | tf_op jit(solution)/shard_map/reduce_scatter | solution.py:295
  278.0 2.4 fusion.42
  281.5 2.9 collective-permute-start.21
  285.3 9.0 %collective-permute-done.21 = bf16[1,176,1024]{2,1,0:T(8,128)(2,1)S(1)} collective-permute-done((bf16[1,176,1024]{2,1,0:T(8,128)(2,1)S(1)}, bf16[1,176,1024]{2,1,0:T(8,128)(2,1)S(1)}, u32[]{:S(2)}, u32[]{:S(2)}) %collective-permute-start.21) | collective-permute-done | bytes 360480 | tf_op jit(solution)/shard_map/ppermute | solution.py:85
  296.0 8.4 %collective-permute-done.16 = bf16[128,1920]{1,0:T(8,128)(2,1)S(1)} collective-permute-done((bf16[128,1920]{1,0:T(8,128)(2,1)S(1)}, bf16[128,1920]{1,0:T(8,128)(2,1)S(1)}, u32[]{:S(2)}, u32[]{:S(2)}) %collective-permute-start.16) | collective-permute-done | bytes 491552 | tf_op jit(solution)/shard_map/ppermute | solution.py:85
  304.5 2.8 collective-permute-start.17
  308.5 2.3 collective-permute-start.18
  310.7 5.3 %collective-permute-done.18 = bf16[32,1920]{1,0:T(8,128)(2,1)S(1)} collective-permute-done((bf16[32,1920]{1,0:T(8,128)(2,1)S(1)}, bf16[32,1920]{1,0:T(8,128)(2,1)S(1)}, u32[]{:S(2)}, u32[]{:S(2)}) %collective-permute-start.18) | collective-permute-done | bytes 122912 | tf_op jit(solution)/shard_map/ppermute | solution.py:70
  (221 shorter events, 70.7 us)
Async XLA Ops:
  7.2 70.8 %all-gather.7.cloned.1.call-start = ((), (), s32[]{:S(2)}) async-start(), calls=%async_computation.5 | async-start | bytes 3244032 | tf_op jit(solution)/shard_map/all_gather | solution.py:207
  9.0 98.0 %all-gather.5.cloned.1.call-start = ((), (), s32[]{:S(2)}) async-start(), calls=%async_computation.4 | async-start | bytes 4423680 | tf_op jit(solution)/shard_map/all_gather | solution.py:197
  13.9 17.3 %copy-start.21 = (bf16[1,256,1024]{2,1,0:T(8,128)(2,1)S(1)}, bf16[1,256,1024]{2,1,0:T(8,128)(2,1)}, u32[]{:S(2)}) copy-start(bf16[1,256,1024]{2,1,0:T(8,128)(2,1)} %param.25) | copy-start | bytes 1572868
  13.9 17.4 %copy-start.19 = (bf16[1,256,1024]{2,1,0:T(8,128)(2,1)S(1)}, bf16[1,256,1024]{2,1,0:T(8,128)(2,1)}, u32[]{:S(2)}) copy-start(bf16[1,256,1024]{2,1,0:T(8,128)(2,1)} %param.14) | copy-start | bytes 1572868
  14.0 8.4 %collective-permute-start.4 = (bf16[32,1920]{1,0:T(8,128)(2,1)S(1)}, bf16[32,1920]{1,0:T(8,128)(2,1)S(1)}, u32[]{:S(2)}, u32[]{:S(2)}) collective-permute-start(bf16[32,1920]{1,0:T(8,128)(2,1)S(1)} %bitcast.250), channel_id=1, source_target_pairs={{0,24},{8,0},{16,8},{24,16},{1,25},{9,1},{17,9},{25,17},{2,26},{10... | collective-permute-start | bytes 368648 | tf_op jit(solution)/shard_map/ppermute | solution.py:70
  17.1 7.7 %collective-permute-start.5 = (bf16[32,1920]{1,0:T(8,128)(2,1)S(1)}, bf16[32,1920]{1,0:T(8,128)(2,1)S(1)}, u32[]{:S(2)}, u32[]{:S(2)}) collective-permute-start(bf16[32,1920]{1,0:T(8,128)(2,1)S(1)} %bitcast.252), channel_id=1, source_target_pairs={{0,16},{8,24},{16,0},{24,8},{1,17},{9,25},{17,1},{25,9},{2,18},{10... | collective-permute-start | bytes 368648 | tf_op jit(solution)/shard_map/ppermute | solution.py:70
  17.9 8.3 %collective-permute-start.6 = (bf16[32,1920]{1,0:T(8,128)(2,1)S(1)}, bf16[32,1920]{1,0:T(8,128)(2,1)S(1)}, u32[]{:S(2)}, u32[]{:S(2)}) collective-permute-start(bf16[32,1920]{1,0:T(8,128)(2,1)S(1)} %bitcast.254), channel_id=1, source_target_pairs={{0,8},{8,16},{16,24},{24,0},{1,9},{9,17},{17,25},{25,1},{2,10},{10... | collective-permute-start | bytes 368648 | tf_op jit(solution)/shard_map/ppermute | solution.py:70
  30.5 239.4 %reduce-scatter.5.cloned.1.call-start = ((), (), s32[]{:S(2)}) async-start(), calls=%async_computation.3 | async-start | bytes 3244032 | tf_op jit(solution)/shard_map/reduce_scatter | solution.py:320
  31.5 24.9 %collective-permute-start = (bf16[256,2048]{1,0:T(8,128)(2,1)S(1)}, bf16[256,2048]{1,0:T(8,128)(2,1)S(1)}, u32[]{:S(2)}, u32[]{:S(2)}) collective-permute-start(bf16[256,2048]{1,0:T(8,128)(2,1)S(1)} %get-tuple-element.58), channel_id=1, source_target_pairs={{0,24},{8,0},{16,8},{24,16},{1,25},{9,1},{17,9},{25,17},{2,26},{10... | collective-permute-start | bytes 3145736 | tf_op jit(solution)/shard_map/ppermute | solution.py:45
  32.1 26.6 %collective-permute-start.1 = (bf16[256,2048]{1,0:T(8,128)(2,1)S(1)}, bf16[256,2048]{1,0:T(8,128)(2,1)S(1)}, u32[]{:S(2)}, u32[]{:S(2)}) collective-permute-start(bf16[256,2048]{1,0:T(8,128)(2,1)S(1)} %get-tuple-element.58), channel_id=1, source_target_pairs={{0,8},{8,16},{16,24},{24,0},{1,9},{9,17},{17,25},{25,1},{2,10},{10... | collective-permute-start | bytes 3145736 | tf_op jit(solution)/shard_map/ppermute | solution.py:44
  57.3 13.1 %collective-permute-start.3 = (bf16[128,2048]{1,0:T(8,128)(2,1)}, bf16[128,2048]{1,0:T(8,128)(2,1)}, u32[]{:S(2)}, u32[]{:S(2)}) collective-permute-start(bf16[128,2048]{1,0:T(8,128)(2,1)} %slice.283), channel_id=1, source_target_pairs={{0,24},{8,0},{16,8},{24,16},{1,25},{9,1},{17,9},{25,17},{2,26},{10... | collective-permute-start | bytes 1572872 | tf_op jit(solution)/shard_map/ppermute | solution.py:47
  59.6 13.6 %collective-permute-start.2 = (bf16[128,2048]{1,0:T(8,128)(2,1)}, bf16[128,2048]{1,0:T(8,128)(2,1)}, u32[]{:S(2)}, u32[]{:S(2)}) collective-permute-start(bf16[128,2048]{1,0:T(8,128)(2,1)} %slice.282), channel_id=1, source_target_pairs={{0,8},{8,16},{16,24},{24,0},{1,9},{9,17},{17,25},{25,1},{2,10},{10... | collective-permute-start | bytes 1572872 | tf_op jit(solution)/shard_map/ppermute | solution.py:46
  60.2 15.1 %copy-start.28 = (s32[1,1,4,256]{3,1,2,0:T(1,128)}, s32[1,1,4,256]{3,1,2,0:T(1,128)S(1)}, u32[]{:S(2)}) copy-start(s32[1,1,4,256]{3,1,2,0:T(1,128)S(1)} %copy.209) | copy-start | bytes 12292
  78.0 166.2 %copy-start.27 = (f32[1024]{0:T(1024)}, f32[1024]{0:T(1024)S(1)}, u32[]{:S(2)}) copy-start(f32[1024]{0:T(1024)S(1)} %add_rsqrt_fusion) | copy-start | bytes 12292
  78.0 4.8 %copy-start.1 = (bf16[4,256,2048]{2,1,0:T(8,128)(2,1)S(1)}, bf16[4,256,2048]{2,1,0:T(8,128)(2,1)}, u32[]{:S(2)}) copy-start(bf16[4,256,2048]{2,1,0:T(8,128)(2,1)} %copy-done) | copy-start | bytes 12582916
  79.2 4.3 %copy-start.15 = (bf16[8,32,1024]{2,1,0:T(8,128)(2,1)}, bf16[8,32,1024]{2,1,0:T(8,128)(2,1)S(1)}, u32[]{:S(2)}) copy-start(bf16[8,32,1024]{2,1,0:T(8,128)(2,1)S(1)} %slice.300) | copy-start | bytes 1572868
  110.1 51.0 %copy-start.29 = (f32[1024]{0:T(1024)}, f32[1024]{0:T(1024)S(1)}, u32[]{:S(2)}) copy-start(f32[1024]{0:T(1024)S(1)} %get-tuple-element.33) | copy-start | bytes 12292
  161.1 6.3 %copy-start.13 = (bf16[1024,4,64]{0,2,1:T(8,128)(2,1)}, bf16[1024,4,64]{0,2,1:T(8,128)(2,1)S(1)}, u32[]{:S(2)}) copy-start(bf16[1024,4,64]{0,2,1:T(8,128)(2,1)S(1)} %copy.181) | copy-start | bytes 1572868
  161.2 6.3 %copy-start.3 = (bf16[4,256,2048]{2,1,0:T(8,128)(2,1)S(1)}, bf16[4,256,2048]{2,1,0:T(8,128)(2,1)}, u32[]{:S(2)}) copy-start(bf16[4,256,2048]{2,1,0:T(8,128)(2,1)} %copy-done) | copy-start | bytes 12582916
  181.7 96.3 %reduce-scatter.3.cloned.1.call-start = ((), (), s32[]{:S(2)}) async-start(), calls=%async_computation.2 | async-start | bytes 4423680 | tf_op jit(solution)/shard_map/reduce_scatter | solution.py:295
  197.5 5.4 %copy-start.11 = (bf16[1024,4,32]{2,0,1:T(8,128)(2,1)S(1)}, bf16[1024,4,32]{2,0,1:T(8,128)(2,1)}, u32[]{:S(2)}) copy-start(bf16[1024,4,32]{2,0,1:T(8,128)(2,1)} %slice.447) | copy-start | bytes 786436
  204.5 4.5 %copy-start.8 = (bf16[4,8,32,1920]{3,2,1,0:T(8,128)(2,1)S(1)}, bf16[4,8,32,1920]{3,2,1,0:T(8,128)(2,1)}, u32[]{:S(2)}) copy-start(bf16[4,8,32,1920]{3,2,1,0:T(8,128)(2,1)} %copy-done.7) | copy-start | bytes 11796484
  204.6 5.1 %copy-start.12 = (bf16[1024,1024]{0,1:T(8,128)(2,1)S(1)}, bf16[1024,1024]{0,1:T(8,128)(2,1)}, u32[]{:S(2)}) copy-start(bf16[1024,1024]{0,1:T(8,128)(2,1)} %get-tuple-element.90) | copy-start | bytes 6291460
  209.6 5.9 %copy-start.23 = (bf16[1024,4,64]{0,2,1:T(8,128)(2,1)S(1)}, bf16[1024,4,64]{0,2,1:T(8,128)(2,1)}, u32[]{:S(2)}) copy-start(bf16[1024,4,64]{0,2,1:T(8,128)(2,1)} %copy.188) | copy-start | bytes 1572868
  209.7 5.9 %copy-start.24 = (bf16[1024,4,64]{0,2,1:T(8,128)(2,1)S(1)}, bf16[1024,4,64]{0,2,1:T(8,128)(2,1)}, u32[]{:S(2)}) copy-start(bf16[1024,4,64]{0,2,1:T(8,128)(2,1)} %copy.187) | copy-start | bytes 1572868
  209.7 5.9 %copy-start.30 = (f32[1024]{0:T(1024)S(1)}, f32[1024]{0:T(1024)}, u32[]{:S(2)}) copy-start(f32[1024]{0:T(1024)} %copy-done.29) | copy-start | bytes 12292
  225.1 6.1 %copy-start.18 = (bf16[8,128,1024]{2,1,0:T(8,128)(2,1)S(1)}, bf16[8,128,1024]{2,1,0:T(8,128)(2,1)}, u32[]{:S(2)}) copy-start(bf16[8,128,1024]{2,1,0:T(8,128)(2,1)} %slice.303) | copy-start | bytes 6291460
  225.1 6.1 %copy-start.32 = (bf16[1024,1024]{0,1:T(8,128)(2,1)S(1)}, bf16[1024,1024]{0,1:T(8,128)(2,1)}, u32[]{:S(2)}) copy-start(bf16[1024,1024]{0,1:T(8,128)(2,1)} %copy-done.31) | copy-start | bytes 6291460
  227.9 11.9 %collective-permute-start.11 = (bf16[128,1024]{1,0:T(8,128)(2,1)S(1)}, bf16[128,1024]{1,0:T(8,128)(2,1)S(1)}, u32[]{:S(2)}, u32[]{:S(2)}) collective-permute-start(bf16[128,1024]{1,0:T(8,128)(2,1)S(1)} %get-tuple-element.47), channel_id=1, source_target_pairs={{0,8},{8,16},{16,24},{24,0},{1,9},{9,17},{17,25},{25,1},{2,10},{10... | collective-permute-start | bytes 786440 | tf_op jit(solution)/shard_map/ppermute | solution.py:56
  229.4 4.2 %copy-start.16 = (bf16[8,32,1024]{2,1,0:T(8,128)(2,1)S(1)}, bf16[8,32,1024]{2,1,0:T(8,128)(2,1)}, u32[]{:S(2)}) copy-start(bf16[8,32,1024]{2,1,0:T(8,128)(2,1)} %copy-done.15) | copy-start | bytes 1572868
  229.4 10.4 %collective-permute-start.13 = (bf16[128,1024]{1,0:T(8,128)(2,1)S(1)}, bf16[128,1024]{1,0:T(8,128)(2,1)S(1)}, u32[]{:S(2)}, u32[]{:S(2)}) collective-permute-start(bf16[128,1024]{1,0:T(8,128)(2,1)S(1)} %get-tuple-element.48), channel_id=1, source_target_pairs={{0,24},{8,0},{16,8},{24,16},{1,25},{9,1},{17,9},{25,17},{2,26},{10... | collective-permute-start | bytes 786440 | tf_op jit(solution)/shard_map/ppermute | solution.py:57
  236.4 8.7 %collective-permute-start.7 = (bf16[128,1024]{1,0:T(8,128)(2,1)S(1)}, bf16[128,1024]{1,0:T(8,128)(2,1)S(1)}, u32[]{:S(2)}, u32[]{:S(2)}) collective-permute-start(bf16[128,1024]{1,0:T(8,128)(2,1)S(1)} %get-tuple-element.51), channel_id=1, source_target_pairs={{0,8},{8,16},{16,24},{24,0},{1,9},{9,17},{17,25},{25,1},{2,10},{10... | collective-permute-start | bytes 786440 | tf_op jit(solution)/shard_map/ppermute | solution.py:56
  236.7 9.9 %collective-permute-start.9 = (bf16[128,1024]{1,0:T(8,128)(2,1)S(1)}, bf16[128,1024]{1,0:T(8,128)(2,1)S(1)}, u32[]{:S(2)}, u32[]{:S(2)}) collective-permute-start(bf16[128,1024]{1,0:T(8,128)(2,1)S(1)} %get-tuple-element.52), channel_id=1, source_target_pairs={{0,24},{8,0},{16,8},{24,16},{1,25},{9,1},{17,9},{25,17},{2,26},{10... | collective-permute-start | bytes 786440 | tf_op jit(solution)/shard_map/ppermute | solution.py:57
  241.2 16.6 %collective-permute-start.14 = (bf16[256,1024]{1,0:T(8,128)(2,1)S(1)}, bf16[256,1024]{1,0:T(8,128)(2,1)S(1)}, u32[]{:S(2)}, u32[]{:S(2)}) collective-permute-start(bf16[256,1024]{1,0:T(8,128)(2,1)S(1)} %pad_maximum_fusion.13), channel_id=1, source_target_pairs={{0,24},{8,0},{16,8},{24,16},{1,25},{9,1},{17,9},{25,17},{2,26},{10... | collective-permute-start | bytes 1572872 | tf_op jit(solution)/shard_map/ppermute | solution.py:61
  242.4 16.3 %collective-permute-start.12 = (bf16[256,1024]{1,0:T(8,128)(2,1)}, bf16[256,1024]{1,0:T(8,128)(2,1)S(1)}, u32[]{:S(2)}, u32[]{:S(2)}) collective-permute-start(bf16[256,1024]{1,0:T(8,128)(2,1)} %pad_maximum_fusion.12), channel_id=1, source_target_pairs={{0,8},{8,16},{16,24},{24,0},{1,9},{9,17},{17,25},{25,1},{2,10},{10... | collective-permute-start | bytes 1572872 | tf_op jit(solution)/shard_map/ppermute | solution.py:60
  244.1 23.4 %copy-start.20 = (bf16[1,256,1024]{2,1,0:T(8,128)(2,1)S(1)}, bf16[1,256,1024]{2,1,0:T(8,128)(2,1)}, u32[]{:S(2)}) copy-start(bf16[1,256,1024]{2,1,0:T(8,128)(2,1)} %param.14) | copy-start | bytes 1572868
  248.0 19.0 %collective-permute-start.10 = (bf16[256,1024]{1,0:T(8,128)(2,1)S(1)}, bf16[256,1024]{1,0:T(8,128)(2,1)S(1)}, u32[]{:S(2)}, u32[]{:S(2)}) collective-permute-start(bf16[256,1024]{1,0:T(8,128)(2,1)S(1)} %pad_maximum_fusion.11), channel_id=1, source_target_pairs={{0,24},{8,0},{16,8},{24,16},{1,25},{9,1},{17,9},{25,17},{2,26},{10... | collective-permute-start | bytes 1572872 | tf_op jit(solution)/shard_map/ppermute | solution.py:61
  251.7 26.2 %copy-start.22 = (bf16[1,256,1024]{2,1,0:T(8,128)(2,1)S(1)}, bf16[1,256,1024]{2,1,0:T(8,128)(2,1)}, u32[]{:S(2)}) copy-start(bf16[1,256,1024]{2,1,0:T(8,128)(2,1)} %param.25) | copy-start | bytes 1572868
  251.8 26.2 %slice-start = ((f32[1024]{0:T(1024)}), f32[256]{0:T(256)S(1)}, s32[]{:S(2)}) async-start(f32[1024]{0:T(1024)} %copy-done.27), calls=%async_computation.6 | async-start | bytes 2048 | tf_op jit(solution)/shard_map/slice | solution.py:280
  251.8 15.7 %collective-permute-start.8 = (bf16[256,1024]{1,0:T(8,128)(2,1)S(1)}, bf16[256,1024]{1,0:T(8,128)(2,1)S(1)}, u32[]{:S(2)}, u32[]{:S(2)}) collective-permute-start(bf16[256,1024]{1,0:T(8,128)(2,1)S(1)} %pad_maximum_fusion.10), channel_id=1, source_target_pairs={{0,8},{8,16},{16,24},{24,0},{1,9},{9,17},{17,25},{25,1},{2,10},{10... | collective-permute-start | bytes 1572872 | tf_op jit(solution)/shard_map/ppermute | solution.py:60
  269.9 10.5 %collective-permute-start.20 = (bf16[1,176,1024]{2,1,0:T(8,128)(2,1)}, bf16[1,176,1024]{2,1,0:T(8,128)(2,1)S(1)}, u32[]{:S(2)}, u32[]{:S(2)}) collective-permute-start(bf16[1,176,1024]{2,1,0:T(8,128)(2,1)} %reduce-scatter.5.cloned.1.call-done), channel_id=1, source_target_pairs={{0,32},{32,0},{64,96},{96,64},{1,33},{33,1},{65,97},{97,65},{2,34}... | collective-permute-start | bytes 1081352 | tf_op jit(solution)/shard_map/ppermute | solution.py:83
  278.0 6.4 %copy-start.26 = (bf16[128,1920]{1,0:T(8,128)(2,1)S(1)}, bf16[128,1920]{1,0:T(8,128)(2,1)}, u32[]{:S(2)}) copy-start(bf16[128,1920]{1,0:T(8,128)(2,1)} %reduce-scatter.3.cloned.1.call-done) | copy-start | bytes 1474564
  278.0 6.4 %collective-permute-start.15 = (bf16[128,1920]{1,0:T(8,128)(2,1)}, bf16[128,1920]{1,0:T(8,128)(2,1)S(1)}, u32[]{:S(2)}, u32[]{:S(2)}) collective-permute-start(bf16[128,1920]{1,0:T(8,128)(2,1)} %reduce-scatter.3.cloned.1.call-done), channel_id=1, source_target_pairs={{0,32},{32,0},{64,96},{96,64},{1,33},{33,1},{65,97},{97,65},{2,34}... | collective-permute-start | bytes 1474568 | tf_op jit(solution)/shard_map/ppermute | solution.py:83
  281.5 12.8 %collective-permute-start.21 = (bf16[1,176,1024]{2,1,0:T(8,128)(2,1)S(1)}, bf16[1,176,1024]{2,1,0:T(8,128)(2,1)S(1)}, u32[]{:S(2)}, u32[]{:S(2)}) collective-permute-start(bf16[1,176,1024]{2,1,0:T(8,128)(2,1)S(1)} %add_convert_fusion.3), channel_id=1, source_target_pairs={{0,64},{32,96},{64,0},{96,32},{1,65},{33,97},{65,1},{97,33},{2,66}... | collective-permute-start | bytes 1081352 | tf_op jit(solution)/shard_map/ppermute | solution.py:85
  284.5 19.8 %collective-permute-start.16 = (bf16[128,1920]{1,0:T(8,128)(2,1)S(1)}, bf16[128,1920]{1,0:T(8,128)(2,1)S(1)}, u32[]{:S(2)}, u32[]{:S(2)}) collective-permute-start(bf16[128,1920]{1,0:T(8,128)(2,1)S(1)} %add_convert_fusion.2), channel_id=1, source_target_pairs={{0,64},{32,96},{64,0},{96,32},{1,65},{33,97},{65,1},{97,33},{2,66}... | collective-permute-start | bytes 1474568 | tf_op jit(solution)/shard_map/ppermute | solution.py:85
  304.5 6.2 %collective-permute-start.17 = (bf16[32,1920]{1,0:T(8,128)(2,1)S(1)}, bf16[32,1920]{1,0:T(8,128)(2,1)S(1)}, u32[]{:S(2)}, u32[]{:S(2)}) collective-permute-start(bf16[32,1920]{1,0:T(8,128)(2,1)S(1)} %get-tuple-element.72), channel_id=1, source_target_pairs={{0,24},{8,0},{16,8},{24,16},{1,25},{9,1},{17,9},{25,17},{2,26},{10... | collective-permute-start | bytes 368648 | tf_op jit(solution)/shard_map/ppermute | solution.py:70
  308.4 8.5 %collective-permute-start.19 = (bf16[32,1920]{1,0:T(8,128)(2,1)S(1)}, bf16[32,1920]{1,0:T(8,128)(2,1)S(1)}, u32[]{:S(2)}, u32[]{:S(2)}) collective-permute-start(bf16[32,1920]{1,0:T(8,128)(2,1)S(1)} %get-tuple-element.69), channel_id=1, source_target_pairs={{0,8},{8,16},{16,24},{24,0},{1,9},{9,17},{17,25},{25,1},{2,10},{10... | collective-permute-start | bytes 368648 | tf_op jit(solution)/shard_map/ppermute | solution.py:70
  308.5 7.5 %collective-permute-start.18 = (bf16[32,1920]{1,0:T(8,128)(2,1)S(1)}, bf16[32,1920]{1,0:T(8,128)(2,1)S(1)}, u32[]{:S(2)}, u32[]{:S(2)}) collective-permute-start(bf16[32,1920]{1,0:T(8,128)(2,1)S(1)} %get-tuple-element.71), channel_id=1, source_target_pairs={{0,16},{8,24},{16,0},{24,8},{1,17},{9,25},{17,1},{25,9},{2,18},{10... | collective-permute-start | bytes 368648 | tf_op jit(solution)/shard_map/ppermute | solution.py:70
  (12 other events, 36.7 us)
Sparse Core Ops, SparseCore 0:
  10.2 45.4 all-gather.6
  57.4 49.5 all-gather.4
  181.8 44.3 reduce-scatter.4
  228.5 49.4 reduce-scatter.2

commit v2 on v1

--- a/solution.py
+++ b/solution.py
@@ -86,18 +86,22 @@
 
 
 def attention_kernel(span_ref, q_ref, k_ref, v_ref, gm_ref, qpos_ref, kpos_ref,
-                     mix_ref, gq_ref, gk_ref, gv_ref):
+                     mix_ref, gq_ref, gk_ref, gv_ref, bias_ref):
     f32, bf16 = jnp.float32, jnp.bfloat16
-    block = pl.program_id(1)
+    block = pl.program_id(0)
+    head = pl.program_id(1)
+
+    @pl.when(head == 0)
+    def _():
+        allowed = (kpos_ref[...] <= qpos_ref[...]) | (kpos_ref[...] < span_ref[0])
+        bias_ref[...] = jnp.where(allowed, 0.0, -1e30).astype(f32)
+
     q = q_ref[...]
     k = k_ref[...]
     v = v_ref[...]
     gm = gm_ref[...]
     scores = lax.dot_general(q, k, (((1,), (1,)), ((), ())), preferred_element_type=f32)
-    qpos = qpos_ref[...]
-    kpos = kpos_ref[...]
-    allowed = (kpos <= qpos) | (kpos < span_ref[0])
-    scores = jnp.where(allowed, scores, -1e30)
+    scores = scores + bias_ref[...]
     peak = jnp.max(scores, axis=1, keepdims=True)
     exps = jnp.exp(scores - peak)
     total = jnp.sum(exps, axis=1, keepdims=True)
@@ -113,13 +117,13 @@
 
     @pl.when(block == 0)
     def _():
-        gk_ref[...] = gk_part
-        gv_ref[...] = gv_part
+        gk_ref[head] = gk_part
+        gv_ref[head] = gv_part
 
     @pl.when(block != 0)
     def _():
-        gk_ref[...] += gk_part
-        gv_ref[...] += gv_part
+        gk_ref[head] += gk_part
+        gv_ref[head] += gv_part
 
 
 def fused_attention(span, queries, keys, values, grad_mixture, positions, rows=256):
@@ -127,8 +131,9 @@
     blocks = length // rows
     qpos = positions.reshape(length, 1).astype(jnp.int32)
     kpos = positions.reshape(1, length).astype(jnp.int32)
-    row_block = pl.BlockSpec((None, rows, dim), lambda h, b, s: (h, b, 0))
-    whole = pl.BlockSpec((None, length, dim), lambda h, b, s: (h, 0, 0))
+    row_block = pl.BlockSpec((None, rows, dim), lambda b, h, s: (h, b, 0))
+    whole_head = pl.BlockSpec((None, length, dim), lambda b, h, s: (h, 0, 0))
+    resident = pl.BlockSpec((heads, length, dim), lambda b, h, s: (0, 0, 0))
     f32 = jnp.float32
     return pl.pallas_call(
         attention_kernel,
@@ -140,13 +145,14 @@
         ),
         grid_spec=pltpu.PrefetchScalarGridSpec(
             num_scalar_prefetch=1,
-            grid=(heads, blocks),
+            grid=(blocks, heads),
             in_specs=[
-                row_block, whole, whole, row_block,
-                pl.BlockSpec((rows, 1), lambda h, b, s: (b, 0)),
-                pl.BlockSpec((1, length), lambda h, b, s: (0, 0)),
+                row_block, whole_head, whole_head, row_block,
+                pl.BlockSpec((rows, 1), lambda b, h, s: (b, 0)),
+                pl.BlockSpec((1, length), lambda b, h, s: (0, 0)),
             ],
-            out_specs=[row_block, row_block, whole, whole],
+            out_specs=[row_block, row_block, resident, resident],
+            scratch_shapes=[pltpu.VMEM((rows, length), f32)],
         ),
         compiler_params=pltpu.CompilerParams(dimension_semantics=("arbitrary", "arbitrary")),
         cost_estimate=pl.CostEstimate(

time: 333 us -> 333 us (level)
  no operation moved by 1% of the time
where the time goes in v2:
time: 333 us; the launch traced here: 327 us
  waiting for transfers between devices  110 us (33%)
  local copies, waits for them, and re-layouts  61.7 us (19%)
  matrix products  39.1 us (12%)
  other arithmetic  38 us (11%)
  Pallas kernels  31 us (9%)
  starting transfers between devices  30.7 us (9%)
  between operations  16.3 us (5%)
    pallas_call x1, Pallas kernels, fused_attention(): pl.pallas_call(attention_kernel, out_shape=(jax.ShapeDtypeStruct((heads,...  31 us
    ppermute x1, waiting for transfers between devices, ring_gather(): from_right = lax.ppermute(block, axis, ring_pairs(n, -1))  22.1 us
    all_gather x1, waiting for transfers between devices, local(): column_block = lax.all_gather(column_payload, 'fsdp', axis=0, tiled=False)  21.4 us
    ppermute x2, waiting for transfers between devices, replica_sum(): lax.ppermute(pair, axis, [(i, i ^ 2) for i in range(n)]).astype(f32)  17.4 us
    unnamed x83, local copies, waits for them, and re-layouts  13.5 us
    ppermute x6, waiting for transfers between devices, ring_all_to_all(): lax.ppermute(pick(me + s), axis, ring_pairs(n, s))  13 us
    ppermute x2, waiting for transfers between devices, ring_scatter(): from_right = lax.ppermute(to_left.astype(wire), axis, ring_pairs(n, -1))  12.2 us
    ppermute x6, starting transfers between devices, ring_all_to_all(): lax.ppermute(pick(me + s), axis, ring_pairs(n, s))  10 us
  transfers between devices with their start and end apart: 26, of which 18 were waited for; matrix products, arithmetic and copies ran while one was open for 26% of the time, Pallas kernels for 0%

profile of v2, /device:TPU:0, one launch (start us, length us, event | category | flops | bytes accessed | tf_op | source)
XLA Modules:
  0.0 326.8 jit_solution(4805807311827820070)
XLA Ops:
  7.2 1.7 fusion.52
  14.0 3.2 collective-permute-start.4
  18.9 3.4 %collective-permute-done.4 = bf16[32,1920]{1,0:T(8,128)(2,1)S(1)} collective-permute-done((bf16[32,1920]{1,0:T(8,128)(2,1)S(1)}, bf16[32,1920]{1,0:T(8,128)(2,1)S(1)}, u32[]{:S(2)}, u32[]{:S(2)}) %collective-permute-start.4) | collective-permute-done | bytes 122912 | tf_op jit(solution)/shard_map/ppermute | solution.py:70
  22.5 2.3 collective-permute-done.5
  26.3 3.0 concatenate.78
  34.3 22.1 %collective-permute-done = bf16[256,2048]{1,0:T(8,128)(2,1)S(1)} collective-permute-done((bf16[256,2048]{1,0:T(8,128)(2,1)S(1)}, bf16[256,2048]{1,0:T(8,128)(2,1)S(1)}, u32[]{:S(2)}, u32[]{:S(2)}) %collective-permute-start) | collective-permute-done | bytes 1048608 | tf_op jit(solution)/shard_map/ppermute | solution.py:45
  61.6 8.8 %collective-permute-done.3 = bf16[128,2048]{1,0:T(8,128)(2,1)} collective-permute-done((bf16[128,2048]{1,0:T(8,128)(2,1)}, bf16[128,2048]{1,0:T(8,128)(2,1)}, u32[]{:S(2)}, u32[]{:S(2)}) %collective-permute-start.3) | collective-permute-done | bytes 524320 | tf_op jit(solution)/shard_map/ppermute | solution.py:47
  70.4 2.8 collective-permute-done.2
  79.3 3.5 %slice.303 = bf16[8,128,1024]{2,1,0:T(8,128)(2,1)} slice(bf16[8,176,1024]{2,1,0:T(8,128)(2,1)} %bitcast.211), slice={[0:8], [32:160], [0:1024]} | slice | bytes 4194304 | tf_op jit(solution)/shard_map/slice | solution.py:215
  85.6 21.4 %all-gather.5.cloned.1.call-done = bf16[32,32,1920]{2,1,0:T(8,128)(2,1)} async-done(((bf16[4,32,1920]{2,1,0:T(8,128)(2,1)}), bf16[32,32,1920]{2,1,0:T(8,128)(2,1)}) %all-gather.5.cloned.1.call-update) | async-done | bytes 3932176 | tf_op jit(solution)/shard_map/all_gather | solution.py:203
  107.0 2.6 copy.171
  110.4 2.3 fusion.27
  119.1 1.7 copy.174
  120.7 3.0 copy.203
  123.8 3.0 maximum_bitcast_fusion.1.k_ref
  128.4 31.0 %shard_map.195 = (bf16[4,1024,64]{2,1,0:T(8,128)(2,1)}, f32[4,1024,64]{2,1,0:T(8,128)}, f32[4,1024,64]{2,1,0:T(8,128)}, f32[4,1024,64]{2,1,0:T(8,128)}) custom-call(s32[1]{0:T(128)S(6)} %copy.228.span_ref, bf16[4,1024,64]{2,1,0:T(8,128)(2,1)} %fusion.33.q_ref, bf16[4,1024,64]{2,1,0:T(8,128)(2,1)} %maximum_bitcast_fusion.1.k_ref, ...), custom_call_target="tpu_custom_call" | custom-call | flops 3221225472 | bytes 5767168 | tf_op jit(solution)/shard_map/pallas_call | solution.py:138
  161.0 6.3 %multiply_convert_fusion = (bf16[1024,1024]{0,1:T(8,128)(2,1)S(1)}, f32[1024,1024]{0,1:T(8,128)S(1)}) fusion(f32[1024]{0:T(1024)S(1)} %bitcast.259, bf16[1024,1920]{1,0:T(8,128)(2,1)} %bitcast.198, f32[1024]{0:T(1024)S(1)} %get-tuple-element.33, f32[1024]{0:T(1024)S(1)} %get-tuple-element.34, f32[1024]{0:T(1024)S(1)} %add_rsqrt_fusion, ...), kind=kOutput, calls=%fused_computation.16 | convolution fusion | flops 2164260864 | bytes 10506240 | tf_op jit(solution)/shard_map/dot_general | solution.py:255
  167.3 4.0 %convolution_convert_fusion = bf16[1296,1024]{1,0:T(8,128)(2,1)S(1)} fusion(bf16[1024,1024]{0,1:T(8,128)(2,1)S(1)} %get-tuple-element.86, bf16[1024,256]{0,1:T(8,128)(2,1)S(1)} %bitcast.215, bf16[1024,2048]{1,0:T(8,128)(2,1)S(1)} %bitcast.188, bf16[1296]{0:T(1024)(128)(2,1)S(1)} %pad.25.clone), kind=kOutput, calls=%fused_computation.19 | convolution fusion | flops 2727198720 | bytes 7376896 | tf_op jit(solution)/shard_map/dot_general | solution.py:263
  173.0 6.3 %fusion.67 = (bf16[1024]{0:T(1024)(128)(2,1)S(1)}, bf16[1024,1024]{0,1:T(8,128)(2,1)}) fusion(f32[1024,1024]{0,1:T(8,128)S(1)} %get-tuple-element.87, f32[1024]{0:T(1024)S(1)} %bitcast.260, bf16[1024,1024]{1,0:T(8,128)(2,1)S(1)} %bitcast.224, bf16[1024,2048]{1,0:T(8,128)(2,1)S(1)} %bitcast.189), kind=kOutput, calls=%fused_computation.176 | convolution fusion | flops 2170551296 | bytes 10491904 | tf_op jit(solution)/shard_map/dot_general | solution.py:264
  181.6 1.9 slice.446
  183.5 3.0 copy.185
  186.5 3.5 %multiply_bitcast_fusion = (f32[1024,4,64]{2,0,1:T(8,128)S(1)}, bf16[1024,4,64]{2,0,1:T(8,128)(2,1)}) fusion(f32[4,1024,64]{2,1,0:T(8,128)} %get-tuple-element.27, f32[4,1024,64]{2,1,0:T(8,128)} %get-tuple-element.29), kind=kLoop, calls=%fused_computation.30 | loop fusion | flops 524288 | bytes 3670016 | tf_op jit(solution)/shard_map/mul | solution.py:272
  190.1 2.3 copy.188
  195.2 2.1 subtract_convert_fusion.1
  199.6 2.4 copy.187
  204.4 3.9 %fusion.25 = f32[1024,1024]{1,0:T(8,128)S(1)} fusion(bf16[1024,1920]{1,0:T(8,128)(2,1)} %bitcast.199, bf16[1024,256]{0,1:T(8,128)(2,1)} %bitcast.241, bf16[1024,256]{0,1:T(8,128)(2,1)} %bitcast.243, bf16[1024,256]{0,1:T(8,128)(2,1)} %bitcast.245), kind=kOutput, calls=%fused_computation.43 | convolution fusion | flops 1615331328 | bytes 7340032 | tf_op jit(solution)/shard_map/dot_general | solution.py:279
  209.5 5.6 %multiply_reduce_fusion = (bf16[1024]{0:T(1024)(128)(2,1)S(1)}, bf16[1024]{0:T(1024)(128)(2,1)S(1)}, f32[1024,1024]{1,0:T(8,128)}, f32[1024,1024]{1,0:T(8,128)}) fusion(f32[1024]{0:T(1024)S(1)} %add_rsqrt_fusion, f32[1024]{0:T(1024)S(1)} %broadcast_multiply_fusion, bf16[1024,2048]{1,0:T(8,128)(2,1)S(1)} %bitcast.190, f32[1024,1024]{1,0:T(8,128)S(1)} %fusion.25, ...), kind=kOutput, calls=%fused_computation.15 | convolution fusion | flops 2154821632 | bytes 18886656 | tf_op jit(solution)/shard_map/dot_general | solution.py:280
  215.4 4.1 %convolution_convert_fusion.2 = bf16[1024,768]{1,0:T(8,128)(2,1)S(1)} fusion(bf16[1024,256]{0,1:T(8,128)(2,1)S(1)} %bitcast.242, bf16[1024,256]{0,1:T(8,128)(2,1)S(1)} %bitcast.244, bf16[1024,256]{0,1:T(8,128)(2,1)} %bitcast.246, f32[1024]{0:T(1024)S(1)} %copy-done.30, f32[1024]{0:T(1024)S(1)} %get-tuple-element.34, f32[1024]{0:T(1024)S(1)} %add_rsqrt_fusion, ...), kind=kOutput, calls=%fused_computation.36 | convolution fusion | flops 1622409216 | bytes 5259264 | tf_op jit(solution)/shard_map/dot_general | solution.py:278
  219.5 2.7 convolution_convert_fusion.1
  222.6 2.3 copy.199
  224.9 2.7 convert.120
  229.3 1.8 collective-permute-start.13
  231.0 2.4 fusion.68
  236.5 3.2 collective-permute-start.9
  242.3 1.7 collective-permute-start.12
  247.8 3.8 %collective-permute-start.10 = (bf16[256,1024]{1,0:T(8,128)(2,1)S(1)}, bf16[256,1024]{1,0:T(8,128)(2,1)S(1)}, u32[]{:S(2)}, u32[]{:S(2)}) collective-permute-start(bf16[256,1024]{1,0:T(8,128)(2,1)S(1)} %pad_maximum_fusion.11), channel_id=1, source_target_pairs={{0,24},{8,0},{16,8},{24,16},{1,25},{9,1},{17,9},{25,17},{2,26},{10... | collective-permute-start | bytes 1572872 | tf_op jit(solution)/shard_map/ppermute | solution.py:61
  251.7 5.9 %collective-permute-done.14 = bf16[256,1024]{1,0:T(8,128)(2,1)S(1)} collective-permute-done((bf16[256,1024]{1,0:T(8,128)(2,1)S(1)}, bf16[256,1024]{1,0:T(8,128)(2,1)S(1)}, u32[]{:S(2)}, u32[]{:S(2)}) %collective-permute-start.14) | collective-permute-done | bytes 524320 | tf_op jit(solution)/shard_map/ppermute | solution.py:61
  258.6 1.9 fusion.63
  260.5 6.3 %collective-permute-done.10 = bf16[256,1024]{1,0:T(8,128)(2,1)S(1)} collective-permute-done((bf16[256,1024]{1,0:T(8,128)(2,1)S(1)}, bf16[256,1024]{1,0:T(8,128)(2,1)S(1)}, u32[]{:S(2)}, u32[]{:S(2)}) %collective-permute-start.10) | collective-permute-done | bytes 524320 | tf_op jit(solution)/shard_map/ppermute | solution.py:61
  267.3 2.4 fusion.43
  269.7 8.2 %reduce-scatter.3.cloned.1.call-done = bf16[128,1920]{1,0:T(8,128)(2,1)} async-done(((bf16[1024,1920]{1,0:T(8,128)(2,1)}), bf16[128,1920]{1,0:T(8,128)(2,1)}) %reduce-scatter.3.cloned.1.call-update) | async-done | bytes 491536 | tf_op jit(solution)/shard_map/reduce_scatter | solution.py:301
  277.9 2.4 fusion.42
  281.4 2.9 collective-permute-start.21
  285.2 9.0 %collective-permute-done.21 = bf16[1,176,1024]{2,1,0:T(8,128)(2,1)S(1)} collective-permute-done((bf16[1,176,1024]{2,1,0:T(8,128)(2,1)S(1)}, bf16[1,176,1024]{2,1,0:T(8,128)(2,1)S(1)}, u32[]{:S(2)}, u32[]{:S(2)}) %collective-permute-start.21) | collective-permute-done | bytes 360480 | tf_op jit(solution)/shard_map/ppermute | solution.py:85
  295.9 8.4 %collective-permute-done.16 = bf16[128,1920]{1,0:T(8,128)(2,1)S(1)} collective-permute-done((bf16[128,1920]{1,0:T(8,128)(2,1)S(1)}, bf16[128,1920]{1,0:T(8,128)(2,1)S(1)}, u32[]{:S(2)}, u32[]{:S(2)}) %collective-permute-start.16) | collective-permute-done | bytes 491552 | tf_op jit(solution)/shard_map/ppermute | solution.py:85
  304.5 2.8 collective-permute-start.17
  308.4 2.3 collective-permute-start.18
  310.7 5.3 %collective-permute-done.18 = bf16[32,1920]{1,0:T(8,128)(2,1)S(1)} collective-permute-done((bf16[32,1920]{1,0:T(8,128)(2,1)S(1)}, bf16[32,1920]{1,0:T(8,128)(2,1)S(1)}, u32[]{:S(2)}, u32[]{:S(2)}) %collective-permute-start.18) | collective-permute-done | bytes 122912 | tf_op jit(solution)/shard_map/ppermute | solution.py:70
  (221 shorter events, 70.7 us)
Async XLA Ops:
  7.2 70.8 %all-gather.7.cloned.1.call-start = ((), (), s32[]{:S(2)}) async-start(), calls=%async_computation.5 | async-start | bytes 3244032 | tf_op jit(solution)/shard_map/all_gather | solution.py:213
  9.0 98.0 %all-gather.5.cloned.1.call-start = ((), (), s32[]{:S(2)}) async-start(), calls=%async_computation.4 | async-start | bytes 4423680 | tf_op jit(solution)/shard_map/all_gather | solution.py:203
  13.9 17.3 %copy-start.21 = (bf16[1,256,1024]{2,1,0:T(8,128)(2,1)S(1)}, bf16[1,256,1024]{2,1,0:T(8,128)(2,1)}, u32[]{:S(2)}) copy-start(bf16[1,256,1024]{2,1,0:T(8,128)(2,1)} %param.25) | copy-start | bytes 1572868
  13.9 17.4 %copy-start.19 = (bf16[1,256,1024]{2,1,0:T(8,128)(2,1)S(1)}, bf16[1,256,1024]{2,1,0:T(8,128)(2,1)}, u32[]{:S(2)}) copy-start(bf16[1,256,1024]{2,1,0:T(8,128)(2,1)} %param.14) | copy-start | bytes 1572868
  14.0 8.4 %collective-permute-start.4 = (bf16[32,1920]{1,0:T(8,128)(2,1)S(1)}, bf16[32,1920]{1,0:T(8,128)(2,1)S(1)}, u32[]{:S(2)}, u32[]{:S(2)}) collective-permute-start(bf16[32,1920]{1,0:T(8,128)(2,1)S(1)} %bitcast.250), channel_id=1, source_target_pairs={{0,24},{8,0},{16,8},{24,16},{1,25},{9,1},{17,9},{25,17},{2,26},{10... | collective-permute-start | bytes 368648 | tf_op jit(solution)/shard_map/ppermute | solution.py:70
  17.1 7.7 %collective-permute-start.5 = (bf16[32,1920]{1,0:T(8,128)(2,1)S(1)}, bf16[32,1920]{1,0:T(8,128)(2,1)S(1)}, u32[]{:S(2)}, u32[]{:S(2)}) collective-permute-start(bf16[32,1920]{1,0:T(8,128)(2,1)S(1)} %bitcast.252), channel_id=1, source_target_pairs={{0,16},{8,24},{16,0},{24,8},{1,17},{9,25},{17,1},{25,9},{2,18},{10... | collective-permute-start | bytes 368648 | tf_op jit(solution)/shard_map/ppermute | solution.py:70
  17.9 8.3 %collective-permute-start.6 = (bf16[32,1920]{1,0:T(8,128)(2,1)S(1)}, bf16[32,1920]{1,0:T(8,128)(2,1)S(1)}, u32[]{:S(2)}, u32[]{:S(2)}) collective-permute-start(bf16[32,1920]{1,0:T(8,128)(2,1)S(1)} %bitcast.254), channel_id=1, source_target_pairs={{0,8},{8,16},{16,24},{24,0},{1,9},{9,17},{17,25},{25,1},{2,10},{10... | collective-permute-start | bytes 368648 | tf_op jit(solution)/shard_map/ppermute | solution.py:70
  30.5 239.2 %reduce-scatter.5.cloned.1.call-start = ((), (), s32[]{:S(2)}) async-start(), calls=%async_computation.3 | async-start | bytes 3244032 | tf_op jit(solution)/shard_map/reduce_scatter | solution.py:326
  31.5 24.9 %collective-permute-start = (bf16[256,2048]{1,0:T(8,128)(2,1)S(1)}, bf16[256,2048]{1,0:T(8,128)(2,1)S(1)}, u32[]{:S(2)}, u32[]{:S(2)}) collective-permute-start(bf16[256,2048]{1,0:T(8,128)(2,1)S(1)} %get-tuple-element.58), channel_id=1, source_target_pairs={{0,24},{8,0},{16,8},{24,16},{1,25},{9,1},{17,9},{25,17},{2,26},{10... | collective-permute-start | bytes 3145736 | tf_op jit(solution)/shard_map/ppermute | solution.py:45
  32.1 26.6 %collective-permute-start.1 = (bf16[256,2048]{1,0:T(8,128)(2,1)S(1)}, bf16[256,2048]{1,0:T(8,128)(2,1)S(1)}, u32[]{:S(2)}, u32[]{:S(2)}) collective-permute-start(bf16[256,2048]{1,0:T(8,128)(2,1)S(1)} %get-tuple-element.58), channel_id=1, source_target_pairs={{0,8},{8,16},{16,24},{24,0},{1,9},{9,17},{17,25},{25,1},{2,10},{10... | collective-permute-start | bytes 3145736 | tf_op jit(solution)/shard_map/ppermute | solution.py:44
  57.3 13.1 %collective-permute-start.3 = (bf16[128,2048]{1,0:T(8,128)(2,1)}, bf16[128,2048]{1,0:T(8,128)(2,1)}, u32[]{:S(2)}, u32[]{:S(2)}) collective-permute-start(bf16[128,2048]{1,0:T(8,128)(2,1)} %slice.283), channel_id=1, source_target_pairs={{0,24},{8,0},{16,8},{24,16},{1,25},{9,1},{17,9},{25,17},{2,26},{10... | collective-permute-start | bytes 1572872 | tf_op jit(solution)/shard_map/ppermute | solution.py:47
  59.6 13.6 %collective-permute-start.2 = (bf16[128,2048]{1,0:T(8,128)(2,1)}, bf16[128,2048]{1,0:T(8,128)(2,1)}, u32[]{:S(2)}, u32[]{:S(2)}) collective-permute-start(bf16[128,2048]{1,0:T(8,128)(2,1)} %slice.282), channel_id=1, source_target_pairs={{0,8},{8,16},{16,24},{24,0},{1,9},{9,17},{17,25},{25,1},{2,10},{10... | collective-permute-start | bytes 1572872 | tf_op jit(solution)/shard_map/ppermute | solution.py:46
  60.2 15.1 %copy-start.28 = (s32[1,1,4,256]{3,1,2,0:T(1,128)}, s32[1,1,4,256]{3,1,2,0:T(1,128)S(1)}, u32[]{:S(2)}) copy-start(s32[1,1,4,256]{3,1,2,0:T(1,128)S(1)} %copy.209) | copy-start | bytes 12292
  78.0 166.0 %copy-start.27 = (f32[1024]{0:T(1024)}, f32[1024]{0:T(1024)S(1)}, u32[]{:S(2)}) copy-start(f32[1024]{0:T(1024)S(1)} %add_rsqrt_fusion) | copy-start | bytes 12292
  78.0 4.8 %copy-start.1 = (bf16[4,256,2048]{2,1,0:T(8,128)(2,1)S(1)}, bf16[4,256,2048]{2,1,0:T(8,128)(2,1)}, u32[]{:S(2)}) copy-start(bf16[4,256,2048]{2,1,0:T(8,128)(2,1)} %copy-done) | copy-start | bytes 12582916
  79.2 4.3 %copy-start.15 = (bf16[8,32,1024]{2,1,0:T(8,128)(2,1)}, bf16[8,32,1024]{2,1,0:T(8,128)(2,1)S(1)}, u32[]{:S(2)}) copy-start(bf16[8,32,1024]{2,1,0:T(8,128)(2,1)S(1)} %slice.300) | copy-start | bytes 1572868
  110.1 50.9 %copy-start.29 = (f32[1024]{0:T(1024)}, f32[1024]{0:T(1024)S(1)}, u32[]{:S(2)}) copy-start(f32[1024]{0:T(1024)S(1)} %get-tuple-element.33) | copy-start | bytes 12292
  161.0 6.3 %copy-start.13 = (bf16[1024,4,64]{0,2,1:T(8,128)(2,1)}, bf16[1024,4,64]{0,2,1:T(8,128)(2,1)S(1)}, u32[]{:S(2)}) copy-start(bf16[1024,4,64]{0,2,1:T(8,128)(2,1)S(1)} %copy.181) | copy-start | bytes 1572868
  161.0 6.3 %copy-start.3 = (bf16[4,256,2048]{2,1,0:T(8,128)(2,1)S(1)}, bf16[4,256,2048]{2,1,0:T(8,128)(2,1)}, u32[]{:S(2)}) copy-start(bf16[4,256,2048]{2,1,0:T(8,128)(2,1)} %copy-done) | copy-start | bytes 12582916
  181.5 96.4 %reduce-scatter.3.cloned.1.call-start = ((), (), s32[]{:S(2)}) async-start(), calls=%async_computation.2 | async-start | bytes 4423680 | tf_op jit(solution)/shard_map/reduce_scatter | solution.py:301
  197.3 5.4 %copy-start.11 = (bf16[1024,4,32]{2,0,1:T(8,128)(2,1)S(1)}, bf16[1024,4,32]{2,0,1:T(8,128)(2,1)}, u32[]{:S(2)}) copy-start(bf16[1024,4,32]{2,0,1:T(8,128)(2,1)} %slice.447) | copy-start | bytes 786436
  204.4 4.5 %copy-start.8 = (bf16[4,8,32,1920]{3,2,1,0:T(8,128)(2,1)S(1)}, bf16[4,8,32,1920]{3,2,1,0:T(8,128)(2,1)}, u32[]{:S(2)}) copy-start(bf16[4,8,32,1920]{3,2,1,0:T(8,128)(2,1)} %copy-done.7) | copy-start | bytes 11796484
  204.4 5.1 %copy-start.12 = (bf16[1024,1024]{0,1:T(8,128)(2,1)S(1)}, bf16[1024,1024]{0,1:T(8,128)(2,1)}, u32[]{:S(2)}) copy-start(bf16[1024,1024]{0,1:T(8,128)(2,1)} %get-tuple-element.90) | copy-start | bytes 6291460
  209.5 5.9 %copy-start.23 = (bf16[1024,4,64]{0,2,1:T(8,128)(2,1)S(1)}, bf16[1024,4,64]{0,2,1:T(8,128)(2,1)}, u32[]{:S(2)}) copy-start(bf16[1024,4,64]{0,2,1:T(8,128)(2,1)} %copy.188) | copy-start | bytes 1572868
  209.5 5.9 %copy-start.24 = (bf16[1024,4,64]{0,2,1:T(8,128)(2,1)S(1)}, bf16[1024,4,64]{0,2,1:T(8,128)(2,1)}, u32[]{:S(2)}) copy-start(bf16[1024,4,64]{0,2,1:T(8,128)(2,1)} %copy.187) | copy-start | bytes 1572868
  209.5 5.9 %copy-start.30 = (f32[1024]{0:T(1024)S(1)}, f32[1024]{0:T(1024)}, u32[]{:S(2)}) copy-start(f32[1024]{0:T(1024)} %copy-done.29) | copy-start | bytes 12292
  224.9 6.1 %copy-start.18 = (bf16[8,128,1024]{2,1,0:T(8,128)(2,1)S(1)}, bf16[8,128,1024]{2,1,0:T(8,128)(2,1)}, u32[]{:S(2)}) copy-start(bf16[8,128,1024]{2,1,0:T(8,128)(2,1)} %slice.303) | copy-start | bytes 6291460
  224.9 6.1 %copy-start.32 = (bf16[1024,1024]{0,1:T(8,128)(2,1)S(1)}, bf16[1024,1024]{0,1:T(8,128)(2,1)}, u32[]{:S(2)}) copy-start(bf16[1024,1024]{0,1:T(8,128)(2,1)} %copy-done.31) | copy-start | bytes 6291460
  227.7 11.9 %collective-permute-start.11 = (bf16[128,1024]{1,0:T(8,128)(2,1)S(1)}, bf16[128,1024]{1,0:T(8,128)(2,1)S(1)}, u32[]{:S(2)}, u32[]{:S(2)}) collective-permute-start(bf16[128,1024]{1,0:T(8,128)(2,1)S(1)} %get-tuple-element.47), channel_id=1, source_target_pairs={{0,8},{8,16},{16,24},{24,0},{1,9},{9,17},{17,25},{25,1},{2,10},{10... | collective-permute-start | bytes 786440 | tf_op jit(solution)/shard_map/ppermute | solution.py:56
  229.3 4.2 %copy-start.16 = (bf16[8,32,1024]{2,1,0:T(8,128)(2,1)S(1)}, bf16[8,32,1024]{2,1,0:T(8,128)(2,1)}, u32[]{:S(2)}) copy-start(bf16[8,32,1024]{2,1,0:T(8,128)(2,1)} %copy-done.15) | copy-start | bytes 1572868
  229.3 10.4 %collective-permute-start.13 = (bf16[128,1024]{1,0:T(8,128)(2,1)S(1)}, bf16[128,1024]{1,0:T(8,128)(2,1)S(1)}, u32[]{:S(2)}, u32[]{:S(2)}) collective-permute-start(bf16[128,1024]{1,0:T(8,128)(2,1)S(1)} %get-tuple-element.48), channel_id=1, source_target_pairs={{0,24},{8,0},{16,8},{24,16},{1,25},{9,1},{17,9},{25,17},{2,26},{10... | collective-permute-start | bytes 786440 | tf_op jit(solution)/shard_map/ppermute | solution.py:57
  236.2 8.6 %collective-permute-start.7 = (bf16[128,1024]{1,0:T(8,128)(2,1)S(1)}, bf16[128,1024]{1,0:T(8,128)(2,1)S(1)}, u32[]{:S(2)}, u32[]{:S(2)}) collective-permute-start(bf16[128,1024]{1,0:T(8,128)(2,1)S(1)} %get-tuple-element.51), channel_id=1, source_target_pairs={{0,8},{8,16},{16,24},{24,0},{1,9},{9,17},{17,25},{25,1},{2,10},{10... | collective-permute-start | bytes 786440 | tf_op jit(solution)/shard_map/ppermute | solution.py:56
  236.5 9.9 %collective-permute-start.9 = (bf16[128,1024]{1,0:T(8,128)(2,1)S(1)}, bf16[128,1024]{1,0:T(8,128)(2,1)S(1)}, u32[]{:S(2)}, u32[]{:S(2)}) collective-permute-start(bf16[128,1024]{1,0:T(8,128)(2,1)S(1)} %get-tuple-element.52), channel_id=1, source_target_pairs={{0,24},{8,0},{16,8},{24,16},{1,25},{9,1},{17,9},{25,17},{2,26},{10... | collective-permute-start | bytes 786440 | tf_op jit(solution)/shard_map/ppermute | solution.py:57
  241.0 16.6 %collective-permute-start.14 = (bf16[256,1024]{1,0:T(8,128)(2,1)S(1)}, bf16[256,1024]{1,0:T(8,128)(2,1)S(1)}, u32[]{:S(2)}, u32[]{:S(2)}) collective-permute-start(bf16[256,1024]{1,0:T(8,128)(2,1)S(1)} %pad_maximum_fusion.13), channel_id=1, source_target_pairs={{0,24},{8,0},{16,8},{24,16},{1,25},{9,1},{17,9},{25,17},{2,26},{10... | collective-permute-start | bytes 1572872 | tf_op jit(solution)/shard_map/ppermute | solution.py:61
  242.3 16.3 %collective-permute-start.12 = (bf16[256,1024]{1,0:T(8,128)(2,1)}, bf16[256,1024]{1,0:T(8,128)(2,1)S(1)}, u32[]{:S(2)}, u32[]{:S(2)}) collective-permute-start(bf16[256,1024]{1,0:T(8,128)(2,1)} %pad_maximum_fusion.12), channel_id=1, source_target_pairs={{0,8},{8,16},{16,24},{24,0},{1,9},{9,17},{17,25},{25,1},{2,10},{10... | collective-permute-start | bytes 1572872 | tf_op jit(solution)/shard_map/ppermute | solution.py:60
  244.0 23.3 %copy-start.20 = (bf16[1,256,1024]{2,1,0:T(8,128)(2,1)S(1)}, bf16[1,256,1024]{2,1,0:T(8,128)(2,1)}, u32[]{:S(2)}) copy-start(bf16[1,256,1024]{2,1,0:T(8,128)(2,1)} %param.14) | copy-start | bytes 1572868
  247.8 19.0 %collective-permute-start.10 = (bf16[256,1024]{1,0:T(8,128)(2,1)S(1)}, bf16[256,1024]{1,0:T(8,128)(2,1)S(1)}, u32[]{:S(2)}, u32[]{:S(2)}) collective-permute-start(bf16[256,1024]{1,0:T(8,128)(2,1)S(1)} %pad_maximum_fusion.11), channel_id=1, source_target_pairs={{0,24},{8,0},{16,8},{24,16},{1,25},{9,1},{17,9},{25,17},{2,26},{10... | collective-permute-start | bytes 1572872 | tf_op jit(solution)/shard_map/ppermute | solution.py:61
  251.6 26.3 %copy-start.22 = (bf16[1,256,1024]{2,1,0:T(8,128)(2,1)S(1)}, bf16[1,256,1024]{2,1,0:T(8,128)(2,1)}, u32[]{:S(2)}) copy-start(bf16[1,256,1024]{2,1,0:T(8,128)(2,1)} %param.25) | copy-start | bytes 1572868
  251.6 26.3 %slice-start = ((f32[1024]{0:T(1024)}), f32[256]{0:T(256)S(1)}, s32[]{:S(2)}) async-start(f32[1024]{0:T(1024)} %copy-done.27), calls=%async_computation.6 | async-start | bytes 2048 | tf_op jit(solution)/shard_map/slice | solution.py:286
  251.6 15.7 %collective-permute-start.8 = (bf16[256,1024]{1,0:T(8,128)(2,1)S(1)}, bf16[256,1024]{1,0:T(8,128)(2,1)S(1)}, u32[]{:S(2)}, u32[]{:S(2)}) collective-permute-start(bf16[256,1024]{1,0:T(8,128)(2,1)S(1)} %pad_maximum_fusion.10), channel_id=1, source_target_pairs={{0,8},{8,16},{16,24},{24,0},{1,9},{9,17},{17,25},{25,1},{2,10},{10... | collective-permute-start | bytes 1572872 | tf_op jit(solution)/shard_map/ppermute | solution.py:60
  269.7 10.6 %collective-permute-start.20 = (bf16[1,176,1024]{2,1,0:T(8,128)(2,1)}, bf16[1,176,1024]{2,1,0:T(8,128)(2,1)S(1)}, u32[]{:S(2)}, u32[]{:S(2)}) collective-permute-start(bf16[1,176,1024]{2,1,0:T(8,128)(2,1)} %reduce-scatter.5.cloned.1.call-done), channel_id=1, source_target_pairs={{0,32},{32,0},{64,96},{96,64},{1,33},{33,1},{65,97},{97,65},{2,34}... | collective-permute-start | bytes 1081352 | tf_op jit(solution)/shard_map/ppermute | solution.py:83
  277.9 6.4 %copy-start.26 = (bf16[128,1920]{1,0:T(8,128)(2,1)S(1)}, bf16[128,1920]{1,0:T(8,128)(2,1)}, u32[]{:S(2)}) copy-start(bf16[128,1920]{1,0:T(8,128)(2,1)} %reduce-scatter.3.cloned.1.call-done) | copy-start | bytes 1474564
  277.9 6.4 %collective-permute-start.15 = (bf16[128,1920]{1,0:T(8,128)(2,1)}, bf16[128,1920]{1,0:T(8,128)(2,1)S(1)}, u32[]{:S(2)}, u32[]{:S(2)}) collective-permute-start(bf16[128,1920]{1,0:T(8,128)(2,1)} %reduce-scatter.3.cloned.1.call-done), channel_id=1, source_target_pairs={{0,32},{32,0},{64,96},{96,64},{1,33},{33,1},{65,97},{97,65},{2,34}... | collective-permute-start | bytes 1474568 | tf_op jit(solution)/shard_map/ppermute | solution.py:83
  281.4 12.8 %collective-permute-start.21 = (bf16[1,176,1024]{2,1,0:T(8,128)(2,1)S(1)}, bf16[1,176,1024]{2,1,0:T(8,128)(2,1)S(1)}, u32[]{:S(2)}, u32[]{:S(2)}) collective-permute-start(bf16[1,176,1024]{2,1,0:T(8,128)(2,1)S(1)} %add_convert_fusion.3), channel_id=1, source_target_pairs={{0,64},{32,96},{64,0},{96,32},{1,65},{33,97},{65,1},{97,33},{2,66}... | collective-permute-start | bytes 1081352 | tf_op jit(solution)/shard_map/ppermute | solution.py:85
  284.5 19.8 %collective-permute-start.16 = (bf16[128,1920]{1,0:T(8,128)(2,1)S(1)}, bf16[128,1920]{1,0:T(8,128)(2,1)S(1)}, u32[]{:S(2)}, u32[]{:S(2)}) collective-permute-start(bf16[128,1920]{1,0:T(8,128)(2,1)S(1)} %add_convert_fusion.2), channel_id=1, source_target_pairs={{0,64},{32,96},{64,0},{96,32},{1,65},{33,97},{65,1},{97,33},{2,66}... | collective-permute-start | bytes 1474568 | tf_op jit(solution)/shard_map/ppermute | solution.py:85
  304.5 6.2 %collective-permute-start.17 = (bf16[32,1920]{1,0:T(8,128)(2,1)S(1)}, bf16[32,1920]{1,0:T(8,128)(2,1)S(1)}, u32[]{:S(2)}, u32[]{:S(2)}) collective-permute-start(bf16[32,1920]{1,0:T(8,128)(2,1)S(1)} %get-tuple-element.72), channel_id=1, source_target_pairs={{0,24},{8,0},{16,8},{24,16},{1,25},{9,1},{17,9},{25,17},{2,26},{10... | collective-permute-start | bytes 368648 | tf_op jit(solution)/shard_map/ppermute | solution.py:70
  308.4 8.5 %collective-permute-start.19 = (bf16[32,1920]{1,0:T(8,128)(2,1)S(1)}, bf16[32,1920]{1,0:T(8,128)(2,1)S(1)}, u32[]{:S(2)}, u32[]{:S(2)}) collective-permute-start(bf16[32,1920]{1,0:T(8,128)(2,1)S(1)} %get-tuple-element.69), channel_id=1, source_target_pairs={{0,8},{8,16},{16,24},{24,0},{1,9},{9,17},{17,25},{25,1},{2,10},{10... | collective-permute-start | bytes 368648 | tf_op jit(solution)/shard_map/ppermute | solution.py:70
  308.4 7.6 %collective-permute-start.18 = (bf16[32,1920]{1,0:T(8,128)(2,1)S(1)}, bf16[32,1920]{1,0:T(8,128)(2,1)S(1)}, u32[]{:S(2)}, u32[]{:S(2)}) collective-permute-start(bf16[32,1920]{1,0:T(8,128)(2,1)S(1)} %get-tuple-element.71), channel_id=1, source_target_pairs={{0,16},{8,24},{16,0},{24,8},{1,17},{9,25},{17,1},{25,9},{2,18},{10... | collective-permute-start | bytes 368648 | tf_op jit(solution)/shard_map/ppermute | solution.py:70
  (12 other events, 36.7 us)
Sparse Core Ops, SparseCore 0:
  10.2 45.4 all-gather.6
  57.4 49.5 all-gather.4
  181.6 44.2 reduce-scatter.4
  228.2 49.6 reduce-scatter.2

commit v3 on v2

--- a/solution.py
+++ b/solution.py
@@ -282,6 +282,16 @@
     grad_norm_shift = jnp.sum(grad_normed, 0)
     grad_normed = ring_scatter(grad_normed.reshape(nc, own_rows, width), "ctx")
 
+    mixer_part = row_product[:head_cols].reshape(nf, shard_rows, width)
+    outer_part = row_product[head_cols : head_cols + ff_here].reshape(nf, ff_rows, width)
+    sums_part = jnp.broadcast_to(row_product[head_cols + ff_here :][None], (nf, 16, width))
+    row_grads = jnp.concatenate([mixer_part, outer_part, sums_part], 1)
+    row_grads = row_grads.at[:, ff_rows + shard_rows + 1, :ff_rows].set(
+        grad_inner_bias.reshape(nf, ff_rows).astype(bf16)
+    )
+    row_grads = lax.psum_scatter(row_grads, "fsdp", scatter_dimension=0, tiled=True)
+    row_grads = replica_sum(row_grads, "rep")[0]
+    row_grads, grad_normed = lax.optimization_barrier((row_grads, grad_normed))
     own_whitened = whitened[:own_rows]
     own_scaling = scaling[:own_rows]
     grad_white = grad_normed * gain
@@ -316,15 +326,6 @@
     grad_gain_out = jnp.sum(column_grads[:, :, 3 * head_cols + ff_here], 0)
     grad_shift_out = jnp.sum(column_grads[:, :, 3 * head_cols + ff_here + 1], 0)
 
-    mixer_part = row_product[:head_cols].reshape(nf, shard_rows, width)
-    outer_part = row_product[head_cols : head_cols + ff_here].reshape(nf, ff_rows, width)
-    sums_part = jnp.broadcast_to(row_product[head_cols + ff_here :][None], (nf, 16, width))
-    row_grads = jnp.concatenate([mixer_part, outer_part, sums_part], 1)
-    row_grads = row_grads.at[:, ff_rows + shard_rows + 1, :ff_rows].set(
-        grad_inner_bias.reshape(nf, ff_rows).astype(bf16)
-    )
-    row_grads = lax.psum_scatter(row_grads, "fsdp", scatter_dimension=0, tiled=True)
-    row_grads = replica_sum(row_grads, "rep")[0]
     grad_mixer_out = row_grads[:shard_rows]
     grad_outer_out = row_grads[shard_rows : shard_rows + ff_rows]
     grad_ibias_out = row_grads[shard_rows + ff_rows + 1, :ff_rows]

time: 333 us -> 335 us (level)
    unnamed x83 -> x85, local copies, waits for them, and re-layouts: 13.5 us -> 14.2 us
  transfers between devices with their start and end apart: 26 -> 26, of which waited for: 18 -> 17; matrix products, arithmetic and copies ran while one was open for 26% -> 26% of each run, Pallas kernels for 0% -> 0%
where the time goes in v3:
time: 335 us; the launch traced here: 328 us
  waiting for transfers between devices  109 us (33%)
  local copies, waits for them, and re-layouts  62.4 us (19%)
  other arithmetic  39.4 us (12%)
  matrix products  39.1 us (12%)
  Pallas kernels  31 us (9%)
  starting transfers between devices  30.5 us (9%)
  between operations  16.4 us (5%)
    pallas_call x1, Pallas kernels, fused_attention(): pl.pallas_call(attention_kernel, out_shape=(jax.ShapeDtypeStruct((heads,...  31 us
    ppermute x1, waiting for transfers between devices, ring_gather(): from_right = lax.ppermute(block, axis, ring_pairs(n, -1))  22.1 us
    all_gather x1, waiting for transfers between devices, local(): column_block = lax.all_gather(column_payload, 'fsdp', axis=0, tiled=False)  21.4 us
    ppermute x2, waiting for transfers between devices, replica_sum(): lax.ppermute(pair, axis, [(i, i ^ 2) for i in range(n)]).astype(f32)  20.2 us
    unnamed x85, local copies, waits for them, and re-layouts  14.2 us
    ppermute x6, waiting for transfers between devices, ring_all_to_all(): lax.ppermute(pick(me + s), axis, ring_pairs(n, s))  12.5 us
    ppermute x6, starting transfers between devices, ring_all_to_all(): lax.ppermute(pick(me + s), axis, ring_pairs(n, s))  10 us
    ppermute x2, waiting for transfers between devices, ring_scatter(): from_right = lax.ppermute(to_left.astype(wire), axis, ring_pairs(n, -1))  10 us
  transfers between devices with their start and end apart: 26, of which 17 were waited for; matrix products, arithmetic and copies ran while one was open for 26% of the time, Pallas kernels for 0%

profile of v3, /device:TPU:0, one launch (start us, length us, event | category | flops | bytes accessed | tf_op | source)
XLA Modules:
  0.0 328.2 jit_solution(15466291662431572151)
XLA Ops:
  7.2 1.7 fusion.51
  14.0 3.2 collective-permute-start.4
  18.9 3.4 %collective-permute-done.4 = bf16[32,1920]{1,0:T(8,128)(2,1)S(1)} collective-permute-done((bf16[32,1920]{1,0:T(8,128)(2,1)S(1)}, bf16[32,1920]{1,0:T(8,128)(2,1)S(1)}, u32[]{:S(2)}, u32[]{:S(2)}) %collective-permute-start.4) | collective-permute-done | bytes 122912 | tf_op jit(solution)/shard_map/ppermute | solution.py:70
  22.5 2.3 collective-permute-done.5
  26.3 3.0 concatenate.78
  34.3 22.1 %collective-permute-done = bf16[256,2048]{1,0:T(8,128)(2,1)S(1)} collective-permute-done((bf16[256,2048]{1,0:T(8,128)(2,1)S(1)}, bf16[256,2048]{1,0:T(8,128)(2,1)S(1)}, u32[]{:S(2)}, u32[]{:S(2)}) %collective-permute-start) | collective-permute-done | bytes 1048608 | tf_op jit(solution)/shard_map/ppermute | solution.py:45
  61.6 8.8 %collective-permute-done.3 = bf16[128,2048]{1,0:T(8,128)(2,1)} collective-permute-done((bf16[128,2048]{1,0:T(8,128)(2,1)}, bf16[128,2048]{1,0:T(8,128)(2,1)}, u32[]{:S(2)}, u32[]{:S(2)}) %collective-permute-start.3) | collective-permute-done | bytes 524320 | tf_op jit(solution)/shard_map/ppermute | solution.py:47
  70.4 2.8 collective-permute-done.2
  79.3 3.5 %slice.294 = bf16[8,128,1024]{2,1,0:T(8,128)(2,1)} slice(bf16[8,176,1024]{2,1,0:T(8,128)(2,1)} %bitcast.207), slice={[0:8], [32:160], [0:1024]} | slice | bytes 4194304 | tf_op jit(solution)/shard_map/slice | solution.py:215
  85.6 21.4 %all-gather.5.cloned.1.call-done = bf16[32,32,1920]{2,1,0:T(8,128)(2,1)} async-done(((bf16[4,32,1920]{2,1,0:T(8,128)(2,1)}), bf16[32,32,1920]{2,1,0:T(8,128)(2,1)}) %all-gather.5.cloned.1.call-update) | async-done | bytes 3932176 | tf_op jit(solution)/shard_map/all_gather | solution.py:203
  107.0 2.6 copy.171
  110.4 2.3 fusion.27
  119.1 1.7 copy.174
  120.7 3.0 copy.203
  123.7 3.0 maximum_bitcast_fusion.1.k_ref
  128.4 31.0 %shard_map.195 = (bf16[4,1024,64]{2,1,0:T(8,128)(2,1)}, f32[4,1024,64]{2,1,0:T(8,128)}, f32[4,1024,64]{2,1,0:T(8,128)}, f32[4,1024,64]{2,1,0:T(8,128)}) custom-call(s32[1]{0:T(128)S(6)} %copy.228.span_ref, bf16[4,1024,64]{2,1,0:T(8,128)(2,1)} %fusion.33.q_ref, bf16[4,1024,64]{2,1,0:T(8,128)(2,1)} %maximum_bitcast_fusion.1.k_ref, ...), custom_call_target="tpu_custom_call" | custom-call | flops 3221225472 | bytes 5767168 | tf_op jit(solution)/shard_map/pallas_call | solution.py:138
  161.0 6.3 %multiply_convert_fusion = (bf16[1024,1024]{0,1:T(8,128)(2,1)S(1)}, f32[1024,1024]{0,1:T(8,128)S(1)}) fusion(f32[1024]{0:T(1024)S(1)} %bitcast.255, bf16[1024,1920]{1,0:T(8,128)(2,1)} %bitcast.194, f32[1024]{0:T(1024)S(1)} %get-tuple-element.37, f32[1024]{0:T(1024)S(1)} %get-tuple-element.38, f32[1024]{0:T(1024)S(1)} %add_rsqrt_fusion, ...), kind=kOutput, calls=%fused_computation.16 | convolution fusion | flops 2164260864 | bytes 10506240 | tf_op jit(solution)/shard_map/dot_general | solution.py:255
  167.3 4.0 %convolution_convert_fusion = bf16[1296,1024]{1,0:T(8,128)(2,1)S(1)} fusion(bf16[1024,1024]{0,1:T(8,128)(2,1)S(1)} %get-tuple-element.87, bf16[1024,256]{0,1:T(8,128)(2,1)S(1)} %bitcast.211, bf16[1024,2048]{1,0:T(8,128)(2,1)S(1)} %bitcast.184, bf16[1296]{0:T(1024)(128)(2,1)S(1)} %pad.45.clone), kind=kOutput, calls=%fused_computation.19 | convolution fusion | flops 2727198720 | bytes 7376896 | tf_op jit(solution)/shard_map/dot_general | solution.py:263
  173.0 6.3 %fusion.63 = (bf16[1024]{0:T(1024)(128)(2,1)S(1)}, bf16[1024,1024]{0,1:T(8,128)(2,1)}) fusion(f32[1024,1024]{0,1:T(8,128)S(1)} %get-tuple-element.88, f32[1024]{0:T(1024)S(1)} %bitcast.256, bf16[1024,1024]{1,0:T(8,128)(2,1)S(1)} %bitcast.220, bf16[1024,2048]{1,0:T(8,128)(2,1)S(1)} %bitcast.185), kind=kOutput, calls=%fused_computation.172 | convolution fusion | flops 2170551296 | bytes 10491904 | tf_op jit(solution)/shard_map/dot_general | solution.py:264
  181.5 1.9 slice.429
  183.5 3.0 copy.188
  186.5 3.5 %multiply_bitcast_fusion = (f32[1024,4,64]{2,0,1:T(8,128)S(1)}, bf16[1024,4,64]{2,0,1:T(8,128)(2,1)}) fusion(f32[4,1024,64]{2,1,0:T(8,128)} %get-tuple-element.29, f32[4,1024,64]{2,1,0:T(8,128)} %get-tuple-element.31), kind=kLoop, calls=%fused_computation.30 | loop fusion | flops 524288 | bytes 3670016 | tf_op jit(solution)/shard_map/mul | solution.py:272
  190.0 2.3 copy.191
  195.1 2.1 subtract_convert_fusion.1
  199.6 2.4 copy.190
  204.4 3.9 %fusion.25 = f32[1024,1024]{1,0:T(8,128)S(1)} fusion(bf16[1024,1920]{1,0:T(8,128)(2,1)} %bitcast.195, bf16[1024,256]{0,1:T(8,128)(2,1)} %bitcast.237, bf16[1024,256]{0,1:T(8,128)(2,1)} %bitcast.239, bf16[1024,256]{0,1:T(8,128)(2,1)} %bitcast.241), kind=kOutput, calls=%fused_computation.43 | convolution fusion | flops 1615331328 | bytes 7340032 | tf_op jit(solution)/shard_map/dot_general | solution.py:279
  209.5 5.5 %multiply_reduce_fusion = (bf16[1024]{0:T(1024)(128)(2,1)S(1)}, bf16[1024]{0:T(1024)(128)(2,1)S(1)}, f32[1024,1024]{1,0:T(8,128)}, f32[1024,1024]{1,0:T(8,128)}) fusion(f32[1024]{0:T(1024)S(1)} %add_rsqrt_fusion, f32[1024]{0:T(1024)S(1)} %broadcast_multiply_fusion, bf16[1024,2048]{1,0:T(8,128)(2,1)S(1)} %bitcast.186, f32[1024,1024]{1,0:T(8,128)S(1)} %fusion.25, ...), kind=kOutput, calls=%fused_computation.15 | convolution fusion | flops 2154821632 | bytes 18886656 | tf_op jit(solution)/shard_map/dot_general | solution.py:280
  215.4 4.1 %convolution_convert_fusion.2 = bf16[1024,768]{1,0:T(8,128)(2,1)S(1)} fusion(bf16[1024,256]{0,1:T(8,128)(2,1)S(1)} %bitcast.238, bf16[1024,256]{0,1:T(8,128)(2,1)S(1)} %bitcast.240, bf16[1024,256]{0,1:T(8,128)(2,1)} %bitcast.242, f32[1024]{0:T(1024)S(1)} %copy-done.31, f32[1024]{0:T(1024)S(1)} %get-tuple-element.38, f32[1024]{0:T(1024)S(1)} %add_rsqrt_fusion, ...), kind=kOutput, calls=%fused_computation.36 | convolution fusion | flops 1622409216 | bytes 5259264 | tf_op jit(solution)/shard_map/dot_general | solution.py:278
  219.5 2.7 convolution_convert_fusion.1
  222.6 2.3 copy.199
  224.9 2.7 convert.120
  229.3 1.8 collective-permute-start.15
  231.0 2.4 fusion.64
  236.5 3.2 collective-permute-start.9
  241.5 1.8 collective-permute-start.14
  243.3 2.6 collective-permute-done.7
  248.1 3.7 %collective-permute-start.10 = (bf16[256,1024]{1,0:T(8,128)(2,1)S(1)}, bf16[256,1024]{1,0:T(8,128)(2,1)S(1)}, u32[]{:S(2)}, u32[]{:S(2)}) collective-permute-start(bf16[256,1024]{1,0:T(8,128)(2,1)S(1)} %pad_maximum_fusion.11), channel_id=1, source_target_pairs={{0,24},{8,0},{16,8},{24,16},{1,25},{9,1},{17,9},{25,17},{2,26},{10... | collective-permute-start | bytes 1572872 | tf_op jit(solution)/shard_map/ppermute | solution.py:61
  252.1 3.0 collective-permute-start.12
  255.1 2.6 collective-permute-done.16
  259.4 7.5 %collective-permute-done.10 = bf16[256,1024]{1,0:T(8,128)(2,1)S(1)} collective-permute-done((bf16[256,1024]{1,0:T(8,128)(2,1)S(1)}, bf16[256,1024]{1,0:T(8,128)(2,1)S(1)}, u32[]{:S(2)}, u32[]{:S(2)}) %collective-permute-start.10) | collective-permute-done | bytes 524320 | tf_op jit(solution)/shard_map/ppermute | solution.py:61
  267.4 2.4 fusion.42
  269.7 8.2 %reduce-scatter.5.cloned.1.call-done = bf16[128,1920]{1,0:T(8,128)(2,1)} async-done(((bf16[1024,1920]{1,0:T(8,128)(2,1)}), bf16[128,1920]{1,0:T(8,128)(2,1)}) %reduce-scatter.5.cloned.1.call-update) | async-done | bytes 491536 | tf_op jit(solution)/shard_map/reduce_scatter | solution.py:311
  277.9 8.3 %collective-permute-done.12 = bf16[1,176,1024]{2,1,0:T(8,128)(2,1)} collective-permute-done((bf16[1,176,1024]{2,1,0:T(8,128)(2,1)S(1)}, bf16[1,176,1024]{2,1,0:T(8,128)(2,1)}, u32[]{:S(2)}, u32[]{:S(2)}) %collective-permute-start.12) | collective-permute-done | bytes 360480 | tf_op jit(solution)/shard_map/ppermute | solution.py:85
  290.3 2.3 fusion.41
  292.7 11.9 %collective-permute-done.18 = bf16[128,1920]{1,0:T(8,128)(2,1)S(1)} collective-permute-done((bf16[128,1920]{1,0:T(8,128)(2,1)S(1)}, bf16[128,1920]{1,0:T(8,128)(2,1)S(1)}, u32[]{:S(2)}, u32[]{:S(2)}) %collective-permute-start.18) | collective-permute-done | bytes 491552 | tf_op jit(solution)/shard_map/ppermute | solution.py:85
  304.8 2.8 collective-permute-start.19
  310.2 2.3 collective-permute-start.20
  312.5 4.8 %collective-permute-done.20 = bf16[32,1920]{1,0:T(8,128)(2,1)S(1)} collective-permute-done((bf16[32,1920]{1,0:T(8,128)(2,1)S(1)}, bf16[32,1920]{1,0:T(8,128)(2,1)S(1)}, u32[]{:S(2)}, u32[]{:S(2)}) %collective-permute-start.20) | collective-permute-done | bytes 122912 | tf_op jit(solution)/shard_map/ppermute | solution.py:70
  (224 shorter events, 71.3 us)
Async XLA Ops:
  7.2 70.8 %all-gather.7.cloned.1.call-start = ((), (), s32[]{:S(2)}) async-start(), calls=%async_computation.5 | async-start | bytes 3244032 | tf_op jit(solution)/shard_map/all_gather | solution.py:213
  9.0 98.0 %all-gather.5.cloned.1.call-start = ((), (), s32[]{:S(2)}) async-start(), calls=%async_computation.4 | async-start | bytes 4423680 | tf_op jit(solution)/shard_map/all_gather | solution.py:203
  13.9 17.3 %copy-start.21 = (bf16[1,256,1024]{2,1,0:T(8,128)(2,1)S(1)}, bf16[1,256,1024]{2,1,0:T(8,128)(2,1)}, u32[]{:S(2)}) copy-start(bf16[1,256,1024]{2,1,0:T(8,128)(2,1)} %param.25) | copy-start | bytes 1572868
  13.9 17.4 %copy-start.19 = (bf16[1,256,1024]{2,1,0:T(8,128)(2,1)S(1)}, bf16[1,256,1024]{2,1,0:T(8,128)(2,1)}, u32[]{:S(2)}) copy-start(bf16[1,256,1024]{2,1,0:T(8,128)(2,1)} %param.14) | copy-start | bytes 1572868
  14.0 8.4 %collective-permute-start.4 = (bf16[32,1920]{1,0:T(8,128)(2,1)S(1)}, bf16[32,1920]{1,0:T(8,128)(2,1)S(1)}, u32[]{:S(2)}, u32[]{:S(2)}) collective-permute-start(bf16[32,1920]{1,0:T(8,128)(2,1)S(1)} %bitcast.246), channel_id=1, source_target_pairs={{0,24},{8,0},{16,8},{24,16},{1,25},{9,1},{17,9},{25,17},{2,26},{10... | collective-permute-start | bytes 368648 | tf_op jit(solution)/shard_map/ppermute | solution.py:70
  17.1 7.7 %collective-permute-start.5 = (bf16[32,1920]{1,0:T(8,128)(2,1)S(1)}, bf16[32,1920]{1,0:T(8,128)(2,1)S(1)}, u32[]{:S(2)}, u32[]{:S(2)}) collective-permute-start(bf16[32,1920]{1,0:T(8,128)(2,1)S(1)} %bitcast.248), channel_id=1, source_target_pairs={{0,16},{8,24},{16,0},{24,8},{1,17},{9,25},{17,1},{25,9},{2,18},{10... | collective-permute-start | bytes 368648 | tf_op jit(solution)/shard_map/ppermute | solution.py:70
  17.9 8.3 %collective-permute-start.6 = (bf16[32,1920]{1,0:T(8,128)(2,1)S(1)}, bf16[32,1920]{1,0:T(8,128)(2,1)S(1)}, u32[]{:S(2)}, u32[]{:S(2)}) collective-permute-start(bf16[32,1920]{1,0:T(8,128)(2,1)S(1)} %bitcast.250), channel_id=1, source_target_pairs={{0,8},{8,16},{16,24},{24,0},{1,9},{9,17},{17,25},{25,1},{2,10},{10... | collective-permute-start | bytes 368648 | tf_op jit(solution)/shard_map/ppermute | solution.py:70
  30.5 212.7 %reduce-scatter.3.cloned.1.call-start = ((), (), s32[]{:S(2)}) async-start(), calls=%async_computation.2 | async-start | bytes 3244032 | tf_op jit(solution)/shard_map/reduce_scatter | solution.py:292
  31.5 24.9 %collective-permute-start = (bf16[256,2048]{1,0:T(8,128)(2,1)S(1)}, bf16[256,2048]{1,0:T(8,128)(2,1)S(1)}, u32[]{:S(2)}, u32[]{:S(2)}) collective-permute-start(bf16[256,2048]{1,0:T(8,128)(2,1)S(1)} %get-tuple-element.61), channel_id=1, source_target_pairs={{0,24},{8,0},{16,8},{24,16},{1,25},{9,1},{17,9},{25,17},{2,26},{10... | collective-permute-start | bytes 3145736 | tf_op jit(solution)/shard_map/ppermute | solution.py:45
  32.1 26.6 %collective-permute-start.1 = (bf16[256,2048]{1,0:T(8,128)(2,1)S(1)}, bf16[256,2048]{1,0:T(8,128)(2,1)S(1)}, u32[]{:S(2)}, u32[]{:S(2)}) collective-permute-start(bf16[256,2048]{1,0:T(8,128)(2,1)S(1)} %get-tuple-element.61), channel_id=1, source_target_pairs={{0,8},{8,16},{16,24},{24,0},{1,9},{9,17},{17,25},{25,1},{2,10},{10... | collective-permute-start | bytes 3145736 | tf_op jit(solution)/shard_map/ppermute | solution.py:44
  57.3 13.1 %collective-permute-start.3 = (bf16[128,2048]{1,0:T(8,128)(2,1)}, bf16[128,2048]{1,0:T(8,128)(2,1)}, u32[]{:S(2)}, u32[]{:S(2)}) collective-permute-start(bf16[128,2048]{1,0:T(8,128)(2,1)} %slice.274), channel_id=1, source_target_pairs={{0,24},{8,0},{16,8},{24,16},{1,25},{9,1},{17,9},{25,17},{2,26},{10... | collective-permute-start | bytes 1572872 | tf_op jit(solution)/shard_map/ppermute | solution.py:47
  59.6 13.6 %collective-permute-start.2 = (bf16[128,2048]{1,0:T(8,128)(2,1)}, bf16[128,2048]{1,0:T(8,128)(2,1)}, u32[]{:S(2)}, u32[]{:S(2)}) collective-permute-start(bf16[128,2048]{1,0:T(8,128)(2,1)} %slice.273), channel_id=1, source_target_pairs={{0,8},{8,16},{16,24},{24,0},{1,9},{9,17},{17,25},{25,1},{2,10},{10... | collective-permute-start | bytes 1572872 | tf_op jit(solution)/shard_map/ppermute | solution.py:46
  60.2 15.1 %copy-start.29 = (s32[1,1,4,256]{3,1,2,0:T(1,128)}, s32[1,1,4,256]{3,1,2,0:T(1,128)S(1)}, u32[]{:S(2)}) copy-start(s32[1,1,4,256]{3,1,2,0:T(1,128)S(1)} %copy.209) | copy-start | bytes 12292
  78.0 146.9 %copy-start.28 = (f32[1024]{0:T(1024)}, f32[1024]{0:T(1024)S(1)}, u32[]{:S(2)}) copy-start(f32[1024]{0:T(1024)S(1)} %add_rsqrt_fusion) | copy-start | bytes 12292
  78.0 4.8 %copy-start.1 = (bf16[4,256,2048]{2,1,0:T(8,128)(2,1)S(1)}, bf16[4,256,2048]{2,1,0:T(8,128)(2,1)}, u32[]{:S(2)}) copy-start(bf16[4,256,2048]{2,1,0:T(8,128)(2,1)} %copy-done) | copy-start | bytes 12582916
  79.2 4.3 %copy-start.15 = (bf16[8,32,1024]{2,1,0:T(8,128)(2,1)}, bf16[8,32,1024]{2,1,0:T(8,128)(2,1)S(1)}, u32[]{:S(2)}) copy-start(bf16[8,32,1024]{2,1,0:T(8,128)(2,1)S(1)} %slice.291) | copy-start | bytes 1572868
  110.1 50.9 %copy-start.30 = (f32[1024]{0:T(1024)}, f32[1024]{0:T(1024)S(1)}, u32[]{:S(2)}) copy-start(f32[1024]{0:T(1024)S(1)} %get-tuple-element.37) | copy-start | bytes 12292
  161.0 6.3 %copy-start.13 = (bf16[1024,4,64]{0,2,1:T(8,128)(2,1)}, bf16[1024,4,64]{0,2,1:T(8,128)(2,1)S(1)}, u32[]{:S(2)}) copy-start(bf16[1024,4,64]{0,2,1:T(8,128)(2,1)S(1)} %copy.181) | copy-start | bytes 1572868
  161.0 6.3 %copy-start.3 = (bf16[4,256,2048]{2,1,0:T(8,128)(2,1)S(1)}, bf16[4,256,2048]{2,1,0:T(8,128)(2,1)}, u32[]{:S(2)}) copy-start(bf16[4,256,2048]{2,1,0:T(8,128)(2,1)} %copy-done) | copy-start | bytes 12582916
  181.5 96.4 %reduce-scatter.5.cloned.1.call-start = ((), (), s32[]{:S(2)}) async-start(), calls=%async_computation.3 | async-start | bytes 4423680 | tf_op jit(solution)/shard_map/reduce_scatter | solution.py:311
  197.3 5.4 %copy-start.11 = (bf16[1024,4,32]{2,0,1:T(8,128)(2,1)S(1)}, bf16[1024,4,32]{2,0,1:T(8,128)(2,1)}, u32[]{:S(2)}) copy-start(bf16[1024,4,32]{2,0,1:T(8,128)(2,1)} %slice.430) | copy-start | bytes 786436
  204.4 4.5 %copy-start.8 = (bf16[4,8,32,1920]{3,2,1,0:T(8,128)(2,1)S(1)}, bf16[4,8,32,1920]{3,2,1,0:T(8,128)(2,1)}, u32[]{:S(2)}) copy-start(bf16[4,8,32,1920]{3,2,1,0:T(8,128)(2,1)} %copy-done.7) | copy-start | bytes 11796484
  204.4 5.1 %copy-start.12 = (bf16[1024,1024]{0,1:T(8,128)(2,1)S(1)}, bf16[1024,1024]{0,1:T(8,128)(2,1)}, u32[]{:S(2)}) copy-start(bf16[1024,1024]{0,1:T(8,128)(2,1)} %get-tuple-element.91) | copy-start | bytes 6291460
  209.5 5.9 %copy-start.23 = (bf16[1024,4,64]{0,2,1:T(8,128)(2,1)S(1)}, bf16[1024,4,64]{0,2,1:T(8,128)(2,1)}, u32[]{:S(2)}) copy-start(bf16[1024,4,64]{0,2,1:T(8,128)(2,1)} %copy.191) | copy-start | bytes 1572868
  209.5 5.9 %copy-start.24 = (bf16[1024,4,64]{0,2,1:T(8,128)(2,1)S(1)}, bf16[1024,4,64]{0,2,1:T(8,128)(2,1)}, u32[]{:S(2)}) copy-start(bf16[1024,4,64]{0,2,1:T(8,128)(2,1)} %copy.190) | copy-start | bytes 1572868
  209.5 5.9 %copy-start.31 = (f32[1024]{0:T(1024)S(1)}, f32[1024]{0:T(1024)}, u32[]{:S(2)}) copy-start(f32[1024]{0:T(1024)} %copy-done.30) | copy-start | bytes 12292
  224.9 6.1 %copy-start.18 = (bf16[8,128,1024]{2,1,0:T(8,128)(2,1)S(1)}, bf16[8,128,1024]{2,1,0:T(8,128)(2,1)}, u32[]{:S(2)}) copy-start(bf16[8,128,1024]{2,1,0:T(8,128)(2,1)} %slice.294) | copy-start | bytes 6291460
  224.9 6.1 %copy-start.33 = (bf16[1024,1024]{0,1:T(8,128)(2,1)S(1)}, bf16[1024,1024]{0,1:T(8,128)(2,1)}, u32[]{:S(2)}) copy-start(bf16[1024,1024]{0,1:T(8,128)(2,1)} %copy-done.32) | copy-start | bytes 6291460
  227.7 11.9 %collective-permute-start.13 = (bf16[128,1024]{1,0:T(8,128)(2,1)S(1)}, bf16[128,1024]{1,0:T(8,128)(2,1)S(1)}, u32[]{:S(2)}, u32[]{:S(2)}) collective-permute-start(bf16[128,1024]{1,0:T(8,128)(2,1)S(1)} %get-tuple-element.50), channel_id=1, source_target_pairs={{0,8},{8,16},{16,24},{24,0},{1,9},{9,17},{17,25},{25,1},{2,10},{10... | collective-permute-start | bytes 786440 | tf_op jit(solution)/shard_map/ppermute | solution.py:56
  229.3 4.2 %copy-start.16 = (bf16[8,32,1024]{2,1,0:T(8,128)(2,1)S(1)}, bf16[8,32,1024]{2,1,0:T(8,128)(2,1)}, u32[]{:S(2)}) copy-start(bf16[8,32,1024]{2,1,0:T(8,128)(2,1)} %copy-done.15) | copy-start | bytes 1572868
  229.3 10.4 %collective-permute-start.15 = (bf16[128,1024]{1,0:T(8,128)(2,1)S(1)}, bf16[128,1024]{1,0:T(8,128)(2,1)S(1)}, u32[]{:S(2)}, u32[]{:S(2)}) collective-permute-start(bf16[128,1024]{1,0:T(8,128)(2,1)S(1)} %get-tuple-element.51), channel_id=1, source_target_pairs={{0,24},{8,0},{16,8},{24,16},{1,25},{9,1},{17,9},{25,17},{2,26},{10... | collective-permute-start | bytes 786440 | tf_op jit(solution)/shard_map/ppermute | solution.py:57
  236.2 9.6 %collective-permute-start.7 = (bf16[128,1024]{1,0:T(8,128)(2,1)S(1)}, bf16[128,1024]{1,0:T(8,128)(2,1)S(1)}, u32[]{:S(2)}, u32[]{:S(2)}) collective-permute-start(bf16[128,1024]{1,0:T(8,128)(2,1)S(1)} %get-tuple-element.54), channel_id=1, source_target_pairs={{0,8},{8,16},{16,24},{24,0},{1,9},{9,17},{17,25},{25,1},{2,10},{10... | collective-permute-start | bytes 786440 | tf_op jit(solution)/shard_map/ppermute | solution.py:56
  236.5 10.1 %collective-permute-start.9 = (bf16[128,1024]{1,0:T(8,128)(2,1)S(1)}, bf16[128,1024]{1,0:T(8,128)(2,1)}, u32[]{:S(2)}, u32[]{:S(2)}) collective-permute-start(bf16[128,1024]{1,0:T(8,128)(2,1)S(1)} %get-tuple-element.55), channel_id=1, source_target_pairs={{0,24},{8,0},{16,8},{24,16},{1,25},{9,1},{17,9},{25,17},{2,26},{10... | collective-permute-start | bytes 786440 | tf_op jit(solution)/shard_map/ppermute | solution.py:57
  241.0 16.6 %collective-permute-start.16 = (bf16[256,1024]{1,0:T(8,128)(2,1)S(1)}, bf16[256,1024]{1,0:T(8,128)(2,1)S(1)}, u32[]{:S(2)}, u32[]{:S(2)}) collective-permute-start(bf16[256,1024]{1,0:T(8,128)(2,1)S(1)} %pad_maximum_fusion.13), channel_id=1, source_target_pairs={{0,24},{8,0},{16,8},{24,16},{1,25},{9,1},{17,9},{25,17},{2,26},{10... | collective-permute-start | bytes 1572872 | tf_op jit(solution)/shard_map/ppermute | solution.py:61
  241.5 25.9 %copy-start.20 = (bf16[1,256,1024]{2,1,0:T(8,128)(2,1)S(1)}, bf16[1,256,1024]{2,1,0:T(8,128)(2,1)}, u32[]{:S(2)}) copy-start(bf16[1,256,1024]{2,1,0:T(8,128)(2,1)} %param.14) | copy-start | bytes 1572868
  241.5 16.2 %collective-permute-start.14 = (bf16[256,1024]{1,0:T(8,128)(2,1)S(1)}, bf16[256,1024]{1,0:T(8,128)(2,1)}, u32[]{:S(2)}, u32[]{:S(2)}) collective-permute-start(bf16[256,1024]{1,0:T(8,128)(2,1)S(1)} %pad_maximum_fusion.12), channel_id=1, source_target_pairs={{0,8},{8,16},{16,24},{24,0},{1,9},{9,17},{17,25},{25,1},{2,10},{10... | collective-permute-start | bytes 1572872 | tf_op jit(solution)/shard_map/ppermute | solution.py:60
  243.3 8.7 %copy-start.26 = (bf16[1,176,1024]{2,1,0:T(8,128)(2,1)S(1)}, bf16[1,176,1024]{2,1,0:T(8,128)(2,1)}, u32[]{:S(2)}) copy-start(bf16[1,176,1024]{2,1,0:T(8,128)(2,1)} %reduce-scatter.3.cloned.1.call-done) | copy-start | bytes 1081348
  243.3 8.7 %collective-permute-start.11 = (bf16[1,176,1024]{2,1,0:T(8,128)(2,1)}, bf16[1,176,1024]{2,1,0:T(8,128)(2,1)S(1)}, u32[]{:S(2)}, u32[]{:S(2)}) collective-permute-start(bf16[1,176,1024]{2,1,0:T(8,128)(2,1)} %reduce-scatter.3.cloned.1.call-done), channel_id=1, source_target_pairs={{0,32},{32,0},{64,96},{96,64},{1,33},{33,1},{65,97},{97,65},{2,34}... | collective-permute-start | bytes 1081352 | tf_op jit(solution)/shard_map/ppermute | solution.py:83
  248.1 18.7 %collective-permute-start.10 = (bf16[256,1024]{1,0:T(8,128)(2,1)S(1)}, bf16[256,1024]{1,0:T(8,128)(2,1)S(1)}, u32[]{:S(2)}, u32[]{:S(2)}) collective-permute-start(bf16[256,1024]{1,0:T(8,128)(2,1)S(1)} %pad_maximum_fusion.11), channel_id=1, source_target_pairs={{0,24},{8,0},{16,8},{24,16},{1,25},{9,1},{17,9},{25,17},{2,26},{10... | collective-permute-start | bytes 1572872 | tf_op jit(solution)/shard_map/ppermute | solution.py:61
  251.9 15.5 %collective-permute-start.8 = (bf16[256,1024]{1,0:T(8,128)(2,1)S(1)}, bf16[256,1024]{1,0:T(8,128)(2,1)S(1)}, u32[]{:S(2)}, u32[]{:S(2)}) collective-permute-start(bf16[256,1024]{1,0:T(8,128)(2,1)S(1)} %pad_maximum_fusion.10), channel_id=1, source_target_pairs={{0,8},{8,16},{16,24},{24,0},{1,9},{9,17},{17,25},{25,1},{2,10},{10... | collective-permute-start | bytes 1572872 | tf_op jit(solution)/shard_map/ppermute | solution.py:60
  252.1 34.0 %collective-permute-start.12 = (bf16[1,176,1024]{2,1,0:T(8,128)(2,1)S(1)}, bf16[1,176,1024]{2,1,0:T(8,128)(2,1)}, u32[]{:S(2)}, u32[]{:S(2)}) collective-permute-start(bf16[1,176,1024]{2,1,0:T(8,128)(2,1)S(1)} %add_convert_fusion.3), channel_id=1, source_target_pairs={{0,64},{32,96},{64,0},{96,32},{1,65},{33,97},{65,1},{97,33},{2,66}... | collective-permute-start | bytes 1081352 | tf_op jit(solution)/shard_map/ppermute | solution.py:85
  259.3 31.0 %copy-start.22 = (bf16[1,256,1024]{2,1,0:T(8,128)(2,1)S(1)}, bf16[1,256,1024]{2,1,0:T(8,128)(2,1)}, u32[]{:S(2)}) copy-start(bf16[1,256,1024]{2,1,0:T(8,128)(2,1)} %param.25) | copy-start | bytes 1572868
  259.3 31.0 %slice-start = ((f32[1024]{0:T(1024)}), f32[256]{0:T(256)S(1)}, s32[]{:S(2)}) async-start(f32[1024]{0:T(1024)} %copy-done.28), calls=%async_computation.6 | async-start | bytes 2048 | tf_op jit(solution)/shard_map/slice | solution.py:296
  277.9 10.8 %collective-permute-start.17 = (bf16[128,1920]{1,0:T(8,128)(2,1)}, bf16[128,1920]{1,0:T(8,128)(2,1)S(1)}, u32[]{:S(2)}, u32[]{:S(2)}) collective-permute-start(bf16[128,1920]{1,0:T(8,128)(2,1)} %reduce-scatter.5.cloned.1.call-done), channel_id=1, source_target_pairs={{0,32},{32,0},{64,96},{96,64},{1,33},{33,1},{65,97},{97,65},{2,34}... | collective-permute-start | bytes 1474568 | tf_op jit(solution)/shard_map/ppermute | solution.py:83
  289.9 14.7 %collective-permute-start.18 = (bf16[128,1920]{1,0:T(8,128)(2,1)S(1)}, bf16[128,1920]{1,0:T(8,128)(2,1)S(1)}, u32[]{:S(2)}, u32[]{:S(2)}) collective-permute-start(bf16[128,1920]{1,0:T(8,128)(2,1)S(1)} %add_convert_fusion.2), channel_id=1, source_target_pairs={{0,64},{32,96},{64,0},{96,32},{1,65},{33,97},{65,1},{97,33},{2,66}... | collective-permute-start | bytes 1474568 | tf_op jit(solution)/shard_map/ppermute | solution.py:85
  304.8 7.7 %collective-permute-start.19 = (bf16[32,1920]{1,0:T(8,128)(2,1)S(1)}, bf16[32,1920]{1,0:T(8,128)(2,1)S(1)}, u32[]{:S(2)}, u32[]{:S(2)}) collective-permute-start(bf16[32,1920]{1,0:T(8,128)(2,1)S(1)} %get-tuple-element.73), channel_id=1, source_target_pairs={{0,24},{8,0},{16,8},{24,16},{1,25},{9,1},{17,9},{25,17},{2,26},{10... | collective-permute-start | bytes 368648 | tf_op jit(solution)/shard_map/ppermute | solution.py:70
  310.2 8.0 %collective-permute-start.21 = (bf16[32,1920]{1,0:T(8,128)(2,1)S(1)}, bf16[32,1920]{1,0:T(8,128)(2,1)S(1)}, u32[]{:S(2)}, u32[]{:S(2)}) collective-permute-start(bf16[32,1920]{1,0:T(8,128)(2,1)S(1)} %get-tuple-element.70), channel_id=1, source_target_pairs={{0,8},{8,16},{16,24},{24,0},{1,9},{9,17},{17,25},{25,1},{2,10},{10... | collective-permute-start | bytes 368648 | tf_op jit(solution)/shard_map/ppermute | solution.py:70
  310.2 7.1 %collective-permute-start.20 = (bf16[32,1920]{1,0:T(8,128)(2,1)S(1)}, bf16[32,1920]{1,0:T(8,128)(2,1)S(1)}, u32[]{:S(2)}, u32[]{:S(2)}) collective-permute-start(bf16[32,1920]{1,0:T(8,128)(2,1)S(1)} %get-tuple-element.72), channel_id=1, source_target_pairs={{0,16},{8,24},{16,0},{24,8},{1,17},{9,25},{17,1},{25,9},{2,18},{10... | collective-permute-start | bytes 368648 | tf_op jit(solution)/shard_map/ppermute | solution.py:70
  (13 other events, 37.4 us)
Sparse Core Ops, SparseCore 0:
  10.2 45.4 all-gather.6
  57.4 49.5 all-gather.4
  181.6 44.4 reduce-scatter.2
  228.4 49.4 reduce-scatter.4

commit v4 on v2

--- a/solution.py
+++ b/solution.py
@@ -251,13 +251,9 @@
         values.swapaxes(0, 1) for values in (grad_queries, grad_keys, grad_values)
     )
     mixture = mixture.swapaxes(0, 1).reshape(length, head_cols)
-    attention = jnp.dot(mixture, mixer_here, preferred_element_type=f32)
     preact = jnp.dot(normed, inner_here, preferred_element_type=f32) + ibias_here
     gelu_result = jax.nn.gelu(preact, approximate=True).astype(bf16)
     feedforward = jnp.dot(gelu_result, outer_here, preferred_element_type=f32)
-    block_sum = ring_scatter((attention + feedforward).reshape(nc, own_rows, width), "ctx")
-    layer_output = (tokens[0].astype(f32) + block_sum + obias).astype(bf16)
-
     ones_block = jnp.ones((length, 16), bf16)
     row_lhs = jnp.concatenate([mixture, gelu_result, ones_block], -1)
     row_product = jnp.dot(row_lhs.T, all_upstream, preferred_element_type=f32).astype(bf16)
@@ -298,6 +294,11 @@
         [grad_triple_weight, grad_inner_weight, small_grads], -1
     ).astype(bf16)
     column_grads = column_grads.reshape(nc, nf, shard_rows, -1).swapaxes(0, 1).reshape(width, -1)
+    column_grads, mixture_late = lax.optimization_barrier((column_grads, mixture))
+    attention = jnp.dot(mixture_late, mixer_here, preferred_element_type=f32)
+    block_sum = ring_scatter((attention + feedforward).reshape(nc, own_rows, width), "ctx")
+    layer_output = (tokens[0].astype(f32) + block_sum + obias).astype(bf16)
+
     column_grads = lax.psum_scatter(column_grads, "fsdp", scatter_dimension=0, tiled=True)
     column_grads = replica_sum(column_grads, "rep").astype(bf16)
     column_grads = column_grads.reshape(nc, shard_rows, -1)

time: 333 us -> 333 us (level)
    unnamed x83 -> x79, local copies, waits for them, and re-layouts: 13.5 us -> 13.4 us
  transfers between devices with their start and end apart: 26 -> 26, of which waited for: 18 -> 18; matrix products, arithmetic and copies ran while one was open for 26% -> 27% of each run, Pallas kernels for 0% -> 0%
where the time goes in v4:
time: 333 us; the launch traced here: 327 us
  waiting for transfers between devices  109 us (33%)
  local copies, waits for them, and re-layouts  63.3 us (19%)
  other arithmetic  39.4 us (12%)
  matrix products  37 us (11%)
  Pallas kernels  31.1 us (9%)
  starting transfers between devices  30.8 us (9%)
  between operations  16.3 us (5%)
    pallas_call x1, Pallas kernels, fused_attention(): pl.pallas_call(attention_kernel, out_shape=(jax.ShapeDtypeStruct((heads,...  31.1 us
    ppermute x1, waiting for transfers between devices, ring_gather(): from_right = lax.ppermute(block, axis, ring_pairs(n, -1))  22.1 us
    all_gather x1, waiting for transfers between devices, local(): column_block = lax.all_gather(column_payload, 'fsdp', axis=0, tiled=False)  20.8 us
    ppermute x2, waiting for transfers between devices, replica_sum(): lax.ppermute(pair, axis, [(i, i ^ 2) for i in range(n)]).astype(f32)  17.4 us
    unnamed x79, local copies, waits for them, and re-layouts  13.4 us
    ppermute x6, waiting for transfers between devices, ring_all_to_all(): lax.ppermute(pick(me + s), axis, ring_pairs(n, s))  13 us
    ppermute x2, waiting for transfers between devices, ring_scatter(): from_right = lax.ppermute(to_left.astype(wire), axis, ring_pairs(n, -1))  11.6 us
    ppermute x6, starting transfers between devices, ring_all_to_all(): lax.ppermute(pick(me + s), axis, ring_pairs(n, s))  10 us
  transfers between devices with their start and end apart: 26, of which 18 were waited for; matrix products, arithmetic and copies ran while one was open for 27% of the time, Pallas kernels for 0%

profile of v4, /device:TPU:0, one launch (start us, length us, event | category | flops | bytes accessed | tf_op | source)
XLA Modules:
  0.0 326.5 jit_solution(14891131120358835969)
XLA Ops:
  7.2 1.7 fusion.52
  14.0 3.2 collective-permute-start.4
  18.9 3.4 %collective-permute-done.4 = bf16[32,1920]{1,0:T(8,128)(2,1)S(1)} collective-permute-done((bf16[32,1920]{1,0:T(8,128)(2,1)S(1)}, bf16[32,1920]{1,0:T(8,128)(2,1)S(1)}, u32[]{:S(2)}, u32[]{:S(2)}) %collective-permute-start.4) | collective-permute-done | bytes 122912 | tf_op jit(solution)/shard_map/ppermute | solution.py:70
  22.5 2.3 collective-permute-done.5
  26.3 3.0 concatenate.78
  34.3 22.1 %collective-permute-done = bf16[256,2048]{1,0:T(8,128)(2,1)S(1)} collective-permute-done((bf16[256,2048]{1,0:T(8,128)(2,1)S(1)}, bf16[256,2048]{1,0:T(8,128)(2,1)S(1)}, u32[]{:S(2)}, u32[]{:S(2)}) %collective-permute-start) | collective-permute-done | bytes 1048608 | tf_op jit(solution)/shard_map/ppermute | solution.py:45
  62.2 8.2 %collective-permute-done.3 = bf16[128,2048]{1,0:T(8,128)(2,1)} collective-permute-done((bf16[128,2048]{1,0:T(8,128)(2,1)}, bf16[128,2048]{1,0:T(8,128)(2,1)}, u32[]{:S(2)}, u32[]{:S(2)}) %collective-permute-start.3) | collective-permute-done | bytes 524320 | tf_op jit(solution)/shard_map/ppermute | solution.py:47
  70.4 2.8 collective-permute-done.2
  79.3 3.6 %slice.309 = bf16[8,128,1024]{2,1,0:T(8,128)(2,1)} slice(bf16[8,176,1024]{2,1,0:T(8,128)(2,1)} %bitcast.213), slice={[0:8], [32:160], [0:1024]} | slice | bytes 4194304 | tf_op jit(solution)/shard_map/slice | solution.py:215
  86.2 20.8 %all-gather.5.cloned.1.call-done = bf16[32,32,1920]{2,1,0:T(8,128)(2,1)} async-done(((bf16[4,32,1920]{2,1,0:T(8,128)(2,1)}), bf16[32,32,1920]{2,1,0:T(8,128)(2,1)}) %all-gather.5.cloned.1.call-update) | async-done | bytes 3932176 | tf_op jit(solution)/shard_map/all_gather | solution.py:203
  107.0 2.6 copy.170
  110.4 2.3 fusion.28
  119.1 1.7 copy.173
  120.8 3.0 copy.202
  123.8 2.9 maximum_bitcast_fusion.1.k_ref
  128.3 31.1 %shard_map.195 = (bf16[4,1024,64]{2,1,0:T(8,128)(2,1)}, f32[4,1024,64]{2,1,0:T(8,128)}, f32[4,1024,64]{2,1,0:T(8,128)}, f32[4,1024,64]{2,1,0:T(8,128)}) custom-call(s32[1]{0:T(128)S(6)} %copy.227.span_ref, bf16[4,1024,64]{2,1,0:T(8,128)(2,1)} %fusion.33.q_ref, bf16[4,1024,64]{2,1,0:T(8,128)(2,1)} %maximum_bitcast_fusion.1.k_ref, ...), custom_call_target="tpu_custom_call" | custom-call | flops 3221225472 | bytes 5767168 | tf_op jit(solution)/shard_map/pallas_call | solution.py:138
  161.2 5.6 %multiply_convert_fusion = (bf16[1024,1024]{1,0:T(8,128)(2,1)S(1)}, f32[1024,1024]{1,0:T(8,128)S(1)}) fusion(f32[1024]{0:T(1024)S(1)} %bitcast.259, bf16[1024,1920]{1,0:T(8,128)(2,1)} %bitcast.198, f32[1024]{0:T(1024)S(1)} %copy-done.25, f32[1024]{0:T(1024)S(1)} %get-tuple-element.38, f32[1024]{0:T(1024)S(1)} %add_rsqrt_fusion, ...), kind=kOutput, calls=%fused_computation.15 | convolution fusion | flops 2164260864 | bytes 10506240 | tf_op jit(solution)/shard_map/dot_general | solution.py:254
  166.8 3.2 convolution_convert_fusion
  171.6 6.0 %fusion.67 = (bf16[1024]{0:T(1024)(128)(2,1)S(1)}, bf16[1024,1024]{1,0:T(8,128)(2,1)}) fusion(f32[1024,1024]{1,0:T(8,128)S(1)} %get-tuple-element.91, f32[1024]{0:T(1024)S(1)} %bitcast.260, bf16[1024,1024]{1,0:T(8,128)(2,1)S(1)} %bitcast.224, bf16[1024,2048]{1,0:T(8,128)(2,1)S(1)} %bitcast.189), kind=kOutput, calls=%fused_computation.176 | convolution fusion | flops 2170551296 | bytes 10491904 | tf_op jit(solution)/shard_map/dot_general | solution.py:260
  181.1 3.5 %multiply_bitcast_fusion = (f32[1024,4,64]{2,0,1:T(8,128)S(1)}, bf16[1024,4,64]{2,0,1:T(8,128)(2,1)}) fusion(f32[4,1024,64]{2,1,0:T(8,128)} %get-tuple-element.28, f32[4,1024,64]{2,1,0:T(8,128)} %get-tuple-element.30), kind=kLoop, calls=%fused_computation.30 | loop fusion | flops 524288 | bytes 3670016 | tf_op jit(solution)/shard_map/mul | solution.py:268
  184.7 2.3 copy.186
  189.0 3.0 slice.446
  192.0 2.3 copy.183
  196.0 2.9 pad_maximum_fusion.6
  198.9 2.4 copy.185
  201.3 1.8 pad_maximum_fusion.5
  204.2 3.8 %fusion.26 = f32[1024,1024]{1,0:T(8,128)S(1)} fusion(bf16[1024,1920]{1,0:T(8,128)(2,1)} %bitcast.199, bf16[1024,256]{0,1:T(8,128)(2,1)S(1)} %bitcast.242, bf16[1024,256]{0,1:T(8,128)(2,1)} %bitcast.243, bf16[1024,256]{0,1:T(8,128)(2,1)} %bitcast.245), kind=kOutput, calls=%fused_computation.44 | convolution fusion | flops 1615331328 | bytes 7340032 | tf_op jit(solution)/shard_map/dot_general | solution.py:275
  209.2 5.2 %multiply_reduce_fusion = (bf16[1024]{0:T(1024)(128)(2,1)S(1)}, bf16[1024]{0:T(1024)(128)(2,1)S(1)}, f32[1024,1024]{1,0:T(8,128)}, f32[1024,1024]{1,0:T(8,128)}) fusion(f32[1024]{0:T(1024)S(1)} %add_rsqrt_fusion, f32[1024]{0:T(1024)S(1)} %broadcast_multiply_fusion, bf16[1024,2048]{1,0:T(8,128)(2,1)S(1)} %bitcast.190, f32[1024,1024]{1,0:T(8,128)S(1)} %fusion.26, ...), kind=kOutput, calls=%fused_computation.16 | convolution fusion | flops 2154821632 | bytes 18886656 | tf_op jit(solution)/shard_map/dot_general | solution.py:276
  214.7 4.4 %convolution_convert_fusion.2 = bf16[1024,768]{1,0:T(8,128)(2,1)S(1)} fusion(bf16[1024,256]{0,1:T(8,128)(2,1)} %bitcast.241, bf16[1024,256]{0,1:T(8,128)(2,1)} %bitcast.244, bf16[1024,256]{0,1:T(8,128)(2,1)} %bitcast.246, f32[1024]{0:T(1024)S(1)} %copy-done.26, f32[1024]{0:T(1024)S(1)} %get-tuple-element.38, f32[1024]{0:T(1024)S(1)} %add_rsqrt_fusion, ...), kind=kOutput, calls=%fused_computation.36 | convolution fusion | flops 1622409216 | bytes 5259264 | tf_op jit(solution)/shard_map/dot_general | solution.py:274
  219.2 2.7 convolution_convert_fusion.1
  222.3 2.3 copy.198
  224.6 2.7 convert.124
  228.9 1.8 collective-permute-start.13
  230.7 2.3 fusion.68
  236.1 3.0 collective-permute-start.9
  247.3 3.9 %collective-permute-start.10 = (bf16[256,1024]{1,0:T(8,128)(2,1)S(1)}, bf16[256,1024]{1,0:T(8,128)(2,1)S(1)}, u32[]{:S(2)}, u32[]{:S(2)}) collective-permute-start(bf16[256,1024]{1,0:T(8,128)(2,1)S(1)} %pad_maximum_fusion.11), channel_id=1, source_target_pairs={{0,24},{8,0},{16,8},{24,16},{1,25},{9,1},{17,9},{25,17},{2,26},{10... | collective-permute-start | bytes 1572872 | tf_op jit(solution)/shard_map/ppermute | solution.py:61
  251.3 5.8 %collective-permute-done.14 = bf16[256,1024]{1,0:T(8,128)(2,1)S(1)} collective-permute-done((bf16[256,1024]{1,0:T(8,128)(2,1)S(1)}, bf16[256,1024]{1,0:T(8,128)(2,1)S(1)}, u32[]{:S(2)}, u32[]{:S(2)}) %collective-permute-start.14) | collective-permute-done | bytes 524320 | tf_op jit(solution)/shard_map/ppermute | solution.py:61
  258.4 1.9 fusion.63
  260.4 5.8 %collective-permute-done.10 = bf16[256,1024]{1,0:T(8,128)(2,1)S(1)} collective-permute-done((bf16[256,1024]{1,0:T(8,128)(2,1)S(1)}, bf16[256,1024]{1,0:T(8,128)(2,1)S(1)}, u32[]{:S(2)}, u32[]{:S(2)}) %collective-permute-start.10) | collective-permute-done | bytes 524320 | tf_op jit(solution)/shard_map/ppermute | solution.py:61
  267.1 2.4 fusion.43
  269.5 8.1 %reduce-scatter.3.cloned.1.call-done = bf16[128,1920]{1,0:T(8,128)(2,1)} async-done(((bf16[1024,1920]{1,0:T(8,128)(2,1)}), bf16[128,1920]{1,0:T(8,128)(2,1)}) %reduce-scatter.3.cloned.1.call-update) | async-done | bytes 491536 | tf_op jit(solution)/shard_map/reduce_scatter | solution.py:302
  277.7 2.4 fusion.42
  281.1 2.9 collective-permute-start.21
  285.0 9.0 %collective-permute-done.21 = bf16[1,176,1024]{2,1,0:T(8,128)(2,1)S(1)} collective-permute-done((bf16[1,176,1024]{2,1,0:T(8,128)(2,1)S(1)}, bf16[1,176,1024]{2,1,0:T(8,128)(2,1)S(1)}, u32[]{:S(2)}, u32[]{:S(2)}) %collective-permute-start.21) | collective-permute-done | bytes 360480 | tf_op jit(solution)/shard_map/ppermute | solution.py:85
  295.6 8.4 %collective-permute-done.16 = bf16[128,1920]{1,0:T(8,128)(2,1)S(1)} collective-permute-done((bf16[128,1920]{1,0:T(8,128)(2,1)S(1)}, bf16[128,1920]{1,0:T(8,128)(2,1)S(1)}, u32[]{:S(2)}, u32[]{:S(2)}) %collective-permute-start.16) | collective-permute-done | bytes 491552 | tf_op jit(solution)/shard_map/ppermute | solution.py:85
  304.2 2.8 collective-permute-start.17
  308.1 2.3 collective-permute-start.18
  310.4 5.3 %collective-permute-done.18 = bf16[32,1920]{1,0:T(8,128)(2,1)S(1)} collective-permute-done((bf16[32,1920]{1,0:T(8,128)(2,1)S(1)}, bf16[32,1920]{1,0:T(8,128)(2,1)S(1)}, u32[]{:S(2)}, u32[]{:S(2)}) %collective-permute-start.18) | collective-permute-done | bytes 122912 | tf_op jit(solution)/shard_map/ppermute | solution.py:70
  (218 shorter events, 73.4 us)
Async XLA Ops:
  7.2 70.8 %all-gather.7.cloned.1.call-start = ((), (), s32[]{:S(2)}) async-start(), calls=%async_computation.5 | async-start | bytes 3244032 | tf_op jit(solution)/shard_map/all_gather | solution.py:213
  9.0 98.0 %all-gather.5.cloned.1.call-start = ((), (), s32[]{:S(2)}) async-start(), calls=%async_computation.4 | async-start | bytes 4423680 | tf_op jit(solution)/shard_map/all_gather | solution.py:203
  13.9 17.3 %copy-start.18 = (bf16[1,256,1024]{2,1,0:T(8,128)(2,1)S(1)}, bf16[1,256,1024]{2,1,0:T(8,128)(2,1)}, u32[]{:S(2)}) copy-start(bf16[1,256,1024]{2,1,0:T(8,128)(2,1)} %param.25) | copy-start | bytes 1572868
  13.9 17.4 %copy-start.16 = (bf16[1,256,1024]{2,1,0:T(8,128)(2,1)S(1)}, bf16[1,256,1024]{2,1,0:T(8,128)(2,1)}, u32[]{:S(2)}) copy-start(bf16[1,256,1024]{2,1,0:T(8,128)(2,1)} %param.14) | copy-start | bytes 1572868
  14.0 8.4 %collective-permute-start.4 = (bf16[32,1920]{1,0:T(8,128)(2,1)S(1)}, bf16[32,1920]{1,0:T(8,128)(2,1)S(1)}, u32[]{:S(2)}, u32[]{:S(2)}) collective-permute-start(bf16[32,1920]{1,0:T(8,128)(2,1)S(1)} %bitcast.250), channel_id=1, source_target_pairs={{0,24},{8,0},{16,8},{24,16},{1,25},{9,1},{17,9},{25,17},{2,26},{10... | collective-permute-start | bytes 368648 | tf_op jit(solution)/shard_map/ppermute | solution.py:70
  17.1 7.7 %collective-permute-start.5 = (bf16[32,1920]{1,0:T(8,128)(2,1)S(1)}, bf16[32,1920]{1,0:T(8,128)(2,1)S(1)}, u32[]{:S(2)}, u32[]{:S(2)}) collective-permute-start(bf16[32,1920]{1,0:T(8,128)(2,1)S(1)} %bitcast.252), channel_id=1, source_target_pairs={{0,16},{8,24},{16,0},{24,8},{1,17},{9,25},{17,1},{25,9},{2,18},{10... | collective-permute-start | bytes 368648 | tf_op jit(solution)/shard_map/ppermute | solution.py:70
  17.9 8.3 %collective-permute-start.6 = (bf16[32,1920]{1,0:T(8,128)(2,1)S(1)}, bf16[32,1920]{1,0:T(8,128)(2,1)S(1)}, u32[]{:S(2)}, u32[]{:S(2)}) collective-permute-start(bf16[32,1920]{1,0:T(8,128)(2,1)S(1)} %bitcast.254), channel_id=1, source_target_pairs={{0,8},{8,16},{16,24},{24,0},{1,9},{9,17},{17,25},{25,1},{2,10},{10... | collective-permute-start | bytes 368648 | tf_op jit(solution)/shard_map/ppermute | solution.py:70
  30.5 239.0 %reduce-scatter.5.cloned.1.call-start = ((), (), s32[]{:S(2)}) async-start(), calls=%async_computation.3 | async-start | bytes 3244032 | tf_op jit(solution)/shard_map/reduce_scatter | solution.py:327
  31.5 24.9 %collective-permute-start = (bf16[256,2048]{1,0:T(8,128)(2,1)S(1)}, bf16[256,2048]{1,0:T(8,128)(2,1)S(1)}, u32[]{:S(2)}, u32[]{:S(2)}) collective-permute-start(bf16[256,2048]{1,0:T(8,128)(2,1)S(1)} %get-tuple-element.62), channel_id=1, source_target_pairs={{0,24},{8,0},{16,8},{24,16},{1,25},{9,1},{17,9},{25,17},{2,26},{10... | collective-permute-start | bytes 3145736 | tf_op jit(solution)/shard_map/ppermute | solution.py:45
  32.1 26.6 %collective-permute-start.1 = (bf16[256,2048]{1,0:T(8,128)(2,1)S(1)}, bf16[256,2048]{1,0:T(8,128)(2,1)S(1)}, u32[]{:S(2)}, u32[]{:S(2)}) collective-permute-start(bf16[256,2048]{1,0:T(8,128)(2,1)S(1)} %get-tuple-element.62), channel_id=1, source_target_pairs={{0,8},{8,16},{16,24},{24,0},{1,9},{9,17},{17,25},{25,1},{2,10},{10... | collective-permute-start | bytes 3145736 | tf_op jit(solution)/shard_map/ppermute | solution.py:44
  57.2 13.1 %collective-permute-start.3 = (bf16[128,2048]{1,0:T(8,128)(2,1)}, bf16[128,2048]{1,0:T(8,128)(2,1)}, u32[]{:S(2)}, u32[]{:S(2)}) collective-permute-start(bf16[128,2048]{1,0:T(8,128)(2,1)} %slice.283), channel_id=1, source_target_pairs={{0,24},{8,0},{16,8},{24,16},{1,25},{9,1},{17,9},{25,17},{2,26},{10... | collective-permute-start | bytes 1572872 | tf_op jit(solution)/shard_map/ppermute | solution.py:47
  59.6 13.6 %collective-permute-start.2 = (bf16[128,2048]{1,0:T(8,128)(2,1)}, bf16[128,2048]{1,0:T(8,128)(2,1)}, u32[]{:S(2)}, u32[]{:S(2)}) collective-permute-start(bf16[128,2048]{1,0:T(8,128)(2,1)} %slice.282), channel_id=1, source_target_pairs={{0,8},{8,16},{16,24},{24,0},{1,9},{9,17},{17,25},{25,1},{2,10},{10... | collective-permute-start | bytes 1572872 | tf_op jit(solution)/shard_map/ppermute | solution.py:46
  60.2 15.1 %copy-start.23 = (s32[1,1,4,256]{3,1,2,0:T(1,128)}, s32[1,1,4,256]{3,1,2,0:T(1,128)S(1)}, u32[]{:S(2)}) copy-start(s32[1,1,4,256]{3,1,2,0:T(1,128)S(1)} %copy.208) | copy-start | bytes 12292
  78.0 165.6 %copy-start.22 = (f32[1024]{0:T(1024)}, f32[1024]{0:T(1024)S(1)}, u32[]{:S(2)}) copy-start(f32[1024]{0:T(1024)S(1)} %add_rsqrt_fusion) | copy-start | bytes 12292
  78.0 4.8 %copy-start.1 = (bf16[4,256,2048]{2,1,0:T(8,128)(2,1)S(1)}, bf16[4,256,2048]{2,1,0:T(8,128)(2,1)}, u32[]{:S(2)}) copy-start(bf16[4,256,2048]{2,1,0:T(8,128)(2,1)} %copy-done) | copy-start | bytes 12582916
  79.2 4.3 %copy-start.12 = (bf16[8,32,1024]{2,1,0:T(8,128)(2,1)}, bf16[8,32,1024]{2,1,0:T(8,128)(2,1)S(1)}, u32[]{:S(2)}) copy-start(bf16[8,32,1024]{2,1,0:T(8,128)(2,1)S(1)} %slice.300) | copy-start | bytes 1572868
  128.3 32.8 %copy-start.25 = (f32[1024]{0:T(1024)S(1)}, f32[1024]{0:T(1024)}, u32[]{:S(2)}) copy-start(f32[1024]{0:T(1024)} %copy-done.24) | copy-start | bytes 12292
  128.3 32.8 %copy-start.28 = (f32[8,1,128]{2,1,0:T(1,128)S(1)}, f32[8,1,128]{2,1,0:T(1,128)}, u32[]{:S(2)}) copy-start(f32[8,1,128]{2,1,0:T(1,128)} %slice_convert_fusion.4) | copy-start | bytes 12292
  161.2 5.6 %copy-start.3 = (bf16[4,256,2048]{2,1,0:T(8,128)(2,1)S(1)}, bf16[4,256,2048]{2,1,0:T(8,128)(2,1)}, u32[]{:S(2)}) copy-start(bf16[4,256,2048]{2,1,0:T(8,128)(2,1)} %copy-done) | copy-start | bytes 12582916
  161.2 5.6 %copy-start.27 = (bf16[1296]{0:T(1024)(128)(2,1)S(1)}, bf16[1296]{0:T(1024)(128)(2,1)}, u32[]{:S(2)}) copy-start(bf16[1296]{0:T(1024)(128)(2,1)} %pad.25.clone) | copy-start | bytes 7780
  181.1 96.6 %reduce-scatter.3.cloned.1.call-start = ((), (), s32[]{:S(2)}) async-start(), calls=%async_computation.2 | async-start | bytes 4423680 | tf_op jit(solution)/shard_map/reduce_scatter | solution.py:302
  196.0 8.2 %copy-start.20 = (bf16[1024,4,64]{0,2,1:T(8,128)(2,1)S(1)}, bf16[1024,4,64]{0,2,1:T(8,128)(2,1)}, u32[]{:S(2)}) copy-start(bf16[1024,4,64]{0,2,1:T(8,128)(2,1)} %copy.186) | copy-start | bytes 1572868
  204.2 4.3 %copy-start.8 = (bf16[4,8,32,1920]{3,2,1,0:T(8,128)(2,1)S(1)}, bf16[4,8,32,1920]{3,2,1,0:T(8,128)(2,1)}, u32[]{:S(2)}) copy-start(bf16[4,8,32,1920]{3,2,1,0:T(8,128)(2,1)} %copy-done.7) | copy-start | bytes 11796484
  204.2 4.9 %copy-start.11 = (bf16[1024,1024]{1,0:T(8,128)(2,1)S(1)}, bf16[1024,1024]{1,0:T(8,128)(2,1)}, u32[]{:S(2)}) copy-start(bf16[1024,1024]{1,0:T(8,128)(2,1)} %get-tuple-element.94) | copy-start | bytes 6291460
  209.2 5.5 %copy-start.26 = (f32[1024]{0:T(1024)S(1)}, f32[1024]{0:T(1024)}, u32[]{:S(2)}) copy-start(f32[1024]{0:T(1024)} %copy-done.24) | copy-start | bytes 12292
  214.7 4.4 %copy-start.5 = (bf16[4,256,2048]{2,1,0:T(8,128)(2,1)S(1)}, bf16[4,256,2048]{2,1,0:T(8,128)(2,1)}, u32[]{:S(2)}) copy-start(bf16[4,256,2048]{2,1,0:T(8,128)(2,1)} %copy-done) | copy-start | bytes 12582916
  224.6 6.1 %copy-start.15 = (bf16[8,128,1024]{2,1,0:T(8,128)(2,1)S(1)}, bf16[8,128,1024]{2,1,0:T(8,128)(2,1)}, u32[]{:S(2)}) copy-start(bf16[8,128,1024]{2,1,0:T(8,128)(2,1)} %slice.309) | copy-start | bytes 6291460
  224.6 6.1 %copy-start.30 = (bf16[1024,1024]{1,0:T(8,128)(2,1)S(1)}, bf16[1024,1024]{1,0:T(8,128)(2,1)}, u32[]{:S(2)}) copy-start(bf16[1024,1024]{1,0:T(8,128)(2,1)} %copy-done.29) | copy-start | bytes 6291460
  227.4 11.6 %collective-permute-start.11 = (bf16[128,1024]{1,0:T(8,128)(2,1)S(1)}, bf16[128,1024]{1,0:T(8,128)(2,1)S(1)}, u32[]{:S(2)}, u32[]{:S(2)}) collective-permute-start(bf16[128,1024]{1,0:T(8,128)(2,1)S(1)} %get-tuple-element.51), channel_id=1, source_target_pairs={{0,8},{8,16},{16,24},{24,0},{1,9},{9,17},{17,25},{25,1},{2,10},{10... | collective-permute-start | bytes 786440 | tf_op jit(solution)/shard_map/ppermute | solution.py:56
  228.9 4.1 %copy-start.13 = (bf16[8,32,1024]{2,1,0:T(8,128)(2,1)S(1)}, bf16[8,32,1024]{2,1,0:T(8,128)(2,1)}, u32[]{:S(2)}) copy-start(bf16[8,32,1024]{2,1,0:T(8,128)(2,1)} %copy-done.12) | copy-start | bytes 1572868
  228.9 10.1 %collective-permute-start.13 = (bf16[128,1024]{1,0:T(8,128)(2,1)S(1)}, bf16[128,1024]{1,0:T(8,128)(2,1)S(1)}, u32[]{:S(2)}, u32[]{:S(2)}) collective-permute-start(bf16[128,1024]{1,0:T(8,128)(2,1)S(1)} %get-tuple-element.52), channel_id=1, source_target_pairs={{0,24},{8,0},{16,8},{24,16},{1,25},{9,1},{17,9},{25,17},{2,26},{10... | collective-permute-start | bytes 786440 | tf_op jit(solution)/shard_map/ppermute | solution.py:57
  235.8 8.7 %collective-permute-start.7 = (bf16[128,1024]{1,0:T(8,128)(2,1)S(1)}, bf16[128,1024]{1,0:T(8,128)(2,1)S(1)}, u32[]{:S(2)}, u32[]{:S(2)}) collective-permute-start(bf16[128,1024]{1,0:T(8,128)(2,1)S(1)} %get-tuple-element.55), channel_id=1, source_target_pairs={{0,8},{8,16},{16,24},{24,0},{1,9},{9,17},{17,25},{25,1},{2,10},{10... | collective-permute-start | bytes 786440 | tf_op jit(solution)/shard_map/ppermute | solution.py:56
  236.1 9.7 %collective-permute-start.9 = (bf16[128,1024]{1,0:T(8,128)(2,1)S(1)}, bf16[128,1024]{1,0:T(8,128)(2,1)}, u32[]{:S(2)}, u32[]{:S(2)}) collective-permute-start(bf16[128,1024]{1,0:T(8,128)(2,1)S(1)} %get-tuple-element.56), channel_id=1, source_target_pairs={{0,24},{8,0},{16,8},{24,16},{1,25},{9,1},{17,9},{25,17},{2,26},{10... | collective-permute-start | bytes 786440 | tf_op jit(solution)/shard_map/ppermute | solution.py:57
  240.4 16.6 %collective-permute-start.14 = (bf16[256,1024]{1,0:T(8,128)(2,1)S(1)}, bf16[256,1024]{1,0:T(8,128)(2,1)S(1)}, u32[]{:S(2)}, u32[]{:S(2)}) collective-permute-start(bf16[256,1024]{1,0:T(8,128)(2,1)S(1)} %pad_maximum_fusion.13), channel_id=1, source_target_pairs={{0,24},{8,0},{16,8},{24,16},{1,25},{9,1},{17,9},{25,17},{2,26},{10... | collective-permute-start | bytes 1572872 | tf_op jit(solution)/shard_map/ppermute | solution.py:61
  242.0 16.5 %collective-permute-start.12 = (bf16[256,1024]{1,0:T(8,128)(2,1)}, bf16[256,1024]{1,0:T(8,128)(2,1)S(1)}, u32[]{:S(2)}, u32[]{:S(2)}) collective-permute-start(bf16[256,1024]{1,0:T(8,128)(2,1)} %pad_maximum_fusion.12), channel_id=1, source_target_pairs={{0,8},{8,16},{16,24},{24,0},{1,9},{9,17},{17,25},{25,1},{2,10},{10... | collective-permute-start | bytes 1572872 | tf_op jit(solution)/shard_map/ppermute | solution.py:60
  243.6 23.6 %copy-start.17 = (bf16[1,256,1024]{2,1,0:T(8,128)(2,1)S(1)}, bf16[1,256,1024]{2,1,0:T(8,128)(2,1)}, u32[]{:S(2)}) copy-start(bf16[1,256,1024]{2,1,0:T(8,128)(2,1)} %param.14) | copy-start | bytes 1572868
  247.3 18.9 %collective-permute-start.10 = (bf16[256,1024]{1,0:T(8,128)(2,1)S(1)}, bf16[256,1024]{1,0:T(8,128)(2,1)S(1)}, u32[]{:S(2)}, u32[]{:S(2)}) collective-permute-start(bf16[256,1024]{1,0:T(8,128)(2,1)S(1)} %pad_maximum_fusion.11), channel_id=1, source_target_pairs={{0,24},{8,0},{16,8},{24,16},{1,25},{9,1},{17,9},{25,17},{2,26},{10... | collective-permute-start | bytes 1572872 | tf_op jit(solution)/shard_map/ppermute | solution.py:61
  251.1 26.5 %copy-start.19 = (bf16[1,256,1024]{2,1,0:T(8,128)(2,1)S(1)}, bf16[1,256,1024]{2,1,0:T(8,128)(2,1)}, u32[]{:S(2)}) copy-start(bf16[1,256,1024]{2,1,0:T(8,128)(2,1)} %param.25) | copy-start | bytes 1572868
  251.1 26.5 %slice-start = ((f32[1024]{0:T(1024)}), f32[256]{0:T(256)S(1)}, s32[]{:S(2)}) async-start(f32[1024]{0:T(1024)} %copy-done.22), calls=%async_computation.6 | async-start | bytes 2048 | tf_op jit(solution)/shard_map/slice | solution.py:282
  251.2 16.0 %collective-permute-start.8 = (bf16[256,1024]{1,0:T(8,128)(2,1)S(1)}, bf16[256,1024]{1,0:T(8,128)(2,1)S(1)}, u32[]{:S(2)}, u32[]{:S(2)}) collective-permute-start(bf16[256,1024]{1,0:T(8,128)(2,1)S(1)} %pad_maximum_fusion.10), channel_id=1, source_target_pairs={{0,8},{8,16},{16,24},{24,0},{1,9},{9,17},{17,25},{25,1},{2,10},{10... | collective-permute-start | bytes 1572872 | tf_op jit(solution)/shard_map/ppermute | solution.py:60
  269.5 10.5 %collective-permute-start.20 = (bf16[1,176,1024]{2,1,0:T(8,128)(2,1)}, bf16[1,176,1024]{2,1,0:T(8,128)(2,1)S(1)}, u32[]{:S(2)}, u32[]{:S(2)}) collective-permute-start(bf16[1,176,1024]{2,1,0:T(8,128)(2,1)} %reduce-scatter.5.cloned.1.call-done), channel_id=1, source_target_pairs={{0,32},{32,0},{64,96},{96,64},{1,33},{33,1},{65,97},{97,65},{2,34}... | collective-permute-start | bytes 1081352 | tf_op jit(solution)/shard_map/ppermute | solution.py:83
  277.6 6.4 %copy-start.21 = (bf16[128,1920]{1,0:T(8,128)(2,1)S(1)}, bf16[128,1920]{1,0:T(8,128)(2,1)}, u32[]{:S(2)}) copy-start(bf16[128,1920]{1,0:T(8,128)(2,1)} %reduce-scatter.3.cloned.1.call-done) | copy-start | bytes 1474564
  277.7 6.4 %collective-permute-start.15 = (bf16[128,1920]{1,0:T(8,128)(2,1)}, bf16[128,1920]{1,0:T(8,128)(2,1)S(1)}, u32[]{:S(2)}, u32[]{:S(2)}) collective-permute-start(bf16[128,1920]{1,0:T(8,128)(2,1)} %reduce-scatter.3.cloned.1.call-done), channel_id=1, source_target_pairs={{0,32},{32,0},{64,96},{96,64},{1,33},{33,1},{65,97},{97,65},{2,34}... | collective-permute-start | bytes 1474568 | tf_op jit(solution)/shard_map/ppermute | solution.py:83
  281.1 12.8 %collective-permute-start.21 = (bf16[1,176,1024]{2,1,0:T(8,128)(2,1)S(1)}, bf16[1,176,1024]{2,1,0:T(8,128)(2,1)S(1)}, u32[]{:S(2)}, u32[]{:S(2)}) collective-permute-start(bf16[1,176,1024]{2,1,0:T(8,128)(2,1)S(1)} %add_convert_fusion.3), channel_id=1, source_target_pairs={{0,64},{32,96},{64,0},{96,32},{1,65},{33,97},{65,1},{97,33},{2,66}... | collective-permute-start | bytes 1081352 | tf_op jit(solution)/shard_map/ppermute | solution.py:85
  284.2 19.8 %collective-permute-start.16 = (bf16[128,1920]{1,0:T(8,128)(2,1)S(1)}, bf16[128,1920]{1,0:T(8,128)(2,1)S(1)}, u32[]{:S(2)}, u32[]{:S(2)}) collective-permute-start(bf16[128,1920]{1,0:T(8,128)(2,1)S(1)} %add_convert_fusion.2), channel_id=1, source_target_pairs={{0,64},{32,96},{64,0},{96,32},{1,65},{33,97},{65,1},{97,33},{2,66}... | collective-permute-start | bytes 1474568 | tf_op jit(solution)/shard_map/ppermute | solution.py:85
  304.2 6.2 %collective-permute-start.17 = (bf16[32,1920]{1,0:T(8,128)(2,1)S(1)}, bf16[32,1920]{1,0:T(8,128)(2,1)S(1)}, u32[]{:S(2)}, u32[]{:S(2)}) collective-permute-start(bf16[32,1920]{1,0:T(8,128)(2,1)S(1)} %get-tuple-element.76), channel_id=1, source_target_pairs={{0,24},{8,0},{16,8},{24,16},{1,25},{9,1},{17,9},{25,17},{2,26},{10... | collective-permute-start | bytes 368648 | tf_op jit(solution)/shard_map/ppermute | solution.py:70
  308.1 8.5 %collective-permute-start.19 = (bf16[32,1920]{1,0:T(8,128)(2,1)S(1)}, bf16[32,1920]{1,0:T(8,128)(2,1)S(1)}, u32[]{:S(2)}, u32[]{:S(2)}) collective-permute-start(bf16[32,1920]{1,0:T(8,128)(2,1)S(1)} %get-tuple-element.73), channel_id=1, source_target_pairs={{0,8},{8,16},{16,24},{24,0},{1,9},{9,17},{17,25},{25,1},{2,10},{10... | collective-permute-start | bytes 368648 | tf_op jit(solution)/shard_map/ppermute | solution.py:70
  308.1 7.6 %collective-permute-start.18 = (bf16[32,1920]{1,0:T(8,128)(2,1)S(1)}, bf16[32,1920]{1,0:T(8,128)(2,1)S(1)}, u32[]{:S(2)}, u32[]{:S(2)}) collective-permute-start(bf16[32,1920]{1,0:T(8,128)(2,1)S(1)} %get-tuple-element.75), channel_id=1, source_target_pairs={{0,16},{8,24},{16,0},{24,8},{1,17},{9,25},{17,1},{25,9},{2,18},{10... | collective-permute-start | bytes 368648 | tf_op jit(solution)/shard_map/ppermute | solution.py:70
  (10 other events, 25.9 us)
Sparse Core Ops, SparseCore 0:
  10.2 45.5 all-gather.6
  57.4 49.5 all-gather.4
  181.2 44.3 reduce-scatter.4
  227.9 49.6 reduce-scatter.2

commit v5 on v2

--- a/solution.py
+++ b/solution.py
@@ -32,6 +32,26 @@
         [even_part * cos_wide - odd_part * sin_wide, odd_part * cos_wide + even_part * sin_wide], -1
     )
     return jnp.concatenate([turned.reshape(leading + (ROT,)), field[..., ROT:]], -1)
+
+
+def pair_tables(positions, width):
+    f32 = jnp.float32
+    highest = lax.Precision.HIGHEST
+    cos_table, sin_table = angles(positions)
+    feature = jnp.arange(width) % HEAD_DIM
+    pick = (feature[None, :] // 2 == jnp.arange(ROT // 2)[:, None]) & (feature[None, :] < ROT)
+    pick = pick.astype(f32)
+    sign = jnp.where(feature % 2 == 0, -1.0, 1.0).astype(f32)
+    cos_full = jnp.dot(cos_table, pick, precision=highest) + (feature >= ROT).astype(f32)
+    sin_full = jnp.dot(sin_table, pick, precision=highest) * sign
+    return cos_full, sin_full
+
+
+def swap_pairs(values):
+    width = values.shape[-1]
+    index = jnp.arange(width)
+    swap = (index[:, None] == (index[None, :] ^ 1)).astype(jnp.float32)
+    return jnp.dot(values, swap, precision=lax.Precision.HIGHEST)
 
 
 def ring_pairs(n, step):
@@ -267,13 +287,13 @@
     grad_inner_weight = jnp.dot(normed.T, grad_before_gelu, preferred_element_type=f32)
     grad_inner_bias = jnp.sum(grad_before_gelu.astype(f32), 0)
     flat_shape = (length, head_cols)
+    cos_full, sin_full = pair_tables(positions, 2 * head_cols)
+    grad_turned = jnp.concatenate(
+        [(grad_queries * HEAD_DIM ** (-0.5)).reshape(flat_shape), grad_keys.reshape(flat_shape)], -1
+    )
+    grad_turned = grad_turned * cos_full - swap_pairs(grad_turned) * sin_full
     grad_query_key_value = jnp.concatenate(
-        [
-            rotate(grad_queries * HEAD_DIM ** (-0.5), cos_table, -sin_table).reshape(flat_shape),
-            rotate(grad_keys, cos_table, -sin_table).reshape(flat_shape),
-            grad_values.reshape(flat_shape),
-        ],
-        -1,
+        [grad_turned, grad_values.reshape(flat_shape)], -1
     ).astype(bf16)
     grad_triple_weight = jnp.dot(normed.T, grad_query_key_value, preferred_element_type=f32)
     grad_normed = jnp.dot(grad_query_key_value, triple_here.T, preferred_element_type=f32)

time: 333 us -> 333 us (level)
  waiting for transfers between devices: 110 us -> 119 us
  local copies, waits for them, and re-layouts: 61.7 us -> 53.1 us
  other arithmetic: 38 us -> 32.9 us
  matrix products: 39.1 us -> 43.4 us
    reduce_scatter x1, waiting for transfers between devices: 8.19 us -> 16.5 us  [local(): lax.psum_scatter(column_grads, 'fsdp', scatter_dimension=0, tiled=True)]
    dot_general x0 -> x3, matrix products: none -> 6.28 us  [the longest x1 2.64 us: pair_tables(): jnp.dot(cos_table, pick, precision=highest) + (feature >= ROT).astype(f32)]
    slice x6 -> x4, local copies, waits for them, and re-layouts: 6.08 us -> 1.58 us  [rotate(): paired = field[..., :ROT].reshape(leading + (ROT // 2, 2))]
    concatenate x2 -> x0, local copies, waits for them, and re-layouts: 3.49 us -> none  [rotate(): jnp.concatenate([turned.reshape(leading + (ROT,)), field[..., ROT:]], -1)]
    another operation x6 -> x5, other arithmetic: 8.14 us -> 6.08 us
    unnamed x83 -> x75, local copies, waits for them, and re-layouts: 13.5 us -> 13.9 us
  transfers between devices with their start and end apart: 26 -> 26, of which waited for: 18 -> 17; matrix products, arithmetic and copies ran while one was open for 26% -> 23% of each run, Pallas kernels for 0% -> 0%
where the time goes in v5:
time: 333 us; the launch traced here: 327 us
  waiting for transfers between devices  119 us (36%)
  local copies, waits for them, and re-layouts  53.1 us (16%)
  matrix products  43.4 us (13%)
  other arithmetic  32.9 us (10%)
  starting transfers between devices  31.3 us (9%)
  Pallas kernels  30.9 us (9%)
  between operations  16.3 us (5%)
    pallas_call x1, Pallas kernels, fused_attention(): pl.pallas_call(attention_kernel, out_shape=(jax.ShapeDtypeStruct((heads,...  30.9 us
    ppermute x1, waiting for transfers between devices, ring_gather(): from_right = lax.ppermute(block, axis, ring_pairs(n, -1))  22.1 us
    all_gather x1, waiting for transfers between devices, local(): column_block = lax.all_gather(column_payload, 'fsdp', axis=0, tiled=False)  21.4 us
    ppermute x2, waiting for transfers between devices, replica_sum(): lax.ppermute(pair, axis, [(i, i ^ 2) for i in range(n)]).astype(f32)  17.4 us
    reduce_scatter x1, waiting for transfers between devices, local(): lax.psum_scatter(column_grads, 'fsdp', scatter_dimension=0, tiled=True)  16.5 us
    unnamed x75, local copies, waits for them, and re-layouts  13.9 us
    ppermute x2, waiting for transfers between devices, ring_scatter(): from_right = lax.ppermute(to_left.astype(wire), axis, ring_pairs(n, -1))  13 us
    ppermute x6, waiting for transfers between devices, ring_all_to_all(): lax.ppermute(pick(me + s), axis, ring_pairs(n, s))  13 us
  transfers between devices with their start and end apart: 26, of which 17 were waited for; matrix products, arithmetic and copies ran while one was open for 23% of the time, Pallas kernels for 0%

profile of v5, /device:TPU:0, one launch (start us, length us, event | category | flops | bytes accessed | tf_op | source)
XLA Modules:
  0.0 326.6 jit_solution(7335293694115655386)
XLA Ops:
  7.2 1.7 fusion.54
  13.9 3.2 collective-permute-start.4
  18.9 3.4 %collective-permute-done.4 = bf16[32,1920]{1,0:T(8,128)(2,1)S(1)} collective-permute-done((bf16[32,1920]{1,0:T(8,128)(2,1)S(1)}, bf16[32,1920]{1,0:T(8,128)(2,1)S(1)}, u32[]{:S(2)}, u32[]{:S(2)}) %collective-permute-start.4) | collective-permute-done | bytes 122912 | tf_op jit(solution)/shard_map/ppermute | solution.py:90
  22.5 2.3 collective-permute-done.5
  26.3 3.0 concatenate.73
  34.2 22.1 %collective-permute-done = bf16[256,2048]{1,0:T(8,128)(2,1)S(1)} collective-permute-done((bf16[256,2048]{1,0:T(8,128)(2,1)S(1)}, bf16[256,2048]{1,0:T(8,128)(2,1)S(1)}, u32[]{:S(2)}, u32[]{:S(2)}) %collective-permute-start) | collective-permute-done | bytes 1048608 | tf_op jit(solution)/shard_map/ppermute | solution.py:65
  61.5 8.8 %collective-permute-done.3 = bf16[128,2048]{1,0:T(8,128)(2,1)} collective-permute-done((bf16[128,2048]{1,0:T(8,128)(2,1)}, bf16[128,2048]{1,0:T(8,128)(2,1)}, u32[]{:S(2)}, u32[]{:S(2)}) %collective-permute-start.3) | collective-permute-done | bytes 524320 | tf_op jit(solution)/shard_map/ppermute | solution.py:67
  70.4 2.8 collective-permute-done.2
  79.2 3.5 %slice.269 = bf16[8,128,1024]{2,1,0:T(8,128)(2,1)} slice(bf16[8,176,1024]{2,1,0:T(8,128)(2,1)} %bitcast.206), slice={[0:8], [32:160], [0:1024]} | slice | bytes 4194304 | tf_op jit(solution)/shard_map/slice | solution.py:235
  85.6 21.4 %all-gather.5.cloned.1.call-done = bf16[32,32,1920]{2,1,0:T(8,128)(2,1)} async-done(((bf16[4,32,1920]{2,1,0:T(8,128)(2,1)}), bf16[32,32,1920]{2,1,0:T(8,128)(2,1)}) %all-gather.5.cloned.1.call-update) | async-done | bytes 3932176 | tf_op jit(solution)/shard_map/all_gather | solution.py:223
  107.0 2.6 copy.155
  110.4 2.3 fusion.28
  120.8 3.0 copy.183
  123.8 2.9 maximum_bitcast_fusion.1.k_ref
  128.3 30.9 %shard_map.195 = (bf16[4,1024,64]{2,1,0:T(8,128)(2,1)}, f32[4,1024,64]{2,1,0:T(8,128)}, f32[4,1024,64]{2,1,0:T(8,128)}, f32[4,1024,64]{2,1,0:T(8,128)}) custom-call(s32[1]{0:T(128)S(6)} %copy.208.span_ref, bf16[4,1024,64]{2,1,0:T(8,128)(2,1)} %fusion.34.q_ref, bf16[4,1024,64]{2,1,0:T(8,128)(2,1)} %maximum_bitcast_fusion.1.k_ref, ...), custom_call_target="tpu_custom_call" | custom-call | flops 3221225472 | bytes 5767168 | tf_op jit(solution)/shard_map/pallas_call | solution.py:158
  160.9 6.3 %multiply_convert_fusion = (bf16[1024,1024]{0,1:T(8,128)(2,1)S(1)}, f32[1024,1024]{0,1:T(8,128)S(1)}) fusion(f32[1024]{0:T(1024)S(1)} %bitcast.249, bf16[1024,1920]{1,0:T(8,128)(2,1)} %bitcast.191, f32[1024]{0:T(1024)S(1)} %get-tuple-element.33, f32[1024]{0:T(1024)S(1)} %get-tuple-element.34, f32[1024]{0:T(1024)S(1)} %add_rsqrt_fusion, ...), kind=kOutput, calls=%fused_computation.16 | convolution fusion | flops 2164260864 | bytes 10506240 | tf_op jit(solution)/shard_map/dot_general | solution.py:275
  167.2 4.0 %convolution_convert_fusion = bf16[1296,1024]{1,0:T(8,128)(2,1)S(1)} fusion(bf16[1024,1024]{0,1:T(8,128)(2,1)S(1)} %get-tuple-element.79, bf16[1024,256]{0,1:T(8,128)(2,1)S(1)} %bitcast.210, bf16[1024,2048]{1,0:T(8,128)(2,1)S(1)} %bitcast.182, bf16[1296]{0:T(1024)(128)(2,1)S(1)} %pad.25.clone), kind=kOutput, calls=%fused_computation.19 | convolution fusion | flops 2727198720 | bytes 7376896 | tf_op jit(solution)/shard_map/dot_general | solution.py:283
  172.8 6.3 %fusion.87 = (bf16[1024]{0:T(1024)(128)(2,1)S(1)}, bf16[1024,1024]{0,1:T(8,128)(2,1)}) fusion(f32[1024,1024]{0,1:T(8,128)S(1)} %get-tuple-element.80, f32[1024]{0:T(1024)S(1)} %bitcast.250, bf16[1024,1024]{1,0:T(8,128)(2,1)S(1)} %bitcast.218, bf16[1024,2048]{1,0:T(8,128)(2,1)S(1)} %bitcast.183), kind=kOutput, calls=%fused_computation.198 | convolution fusion | flops 2170551296 | bytes 10491904 | tf_op jit(solution)/shard_map/dot_general | solution.py:284
  181.8 2.6 fusion.57
  184.5 2.2 copy.167
  186.6 3.8 %multiply_bitcast_fusion = (f32[1024,4,64]{2,0,1:T(8,128)}, bf16[1024,4,64]{2,0,1:T(8,128)(2,1)S(1)}) fusion(f32[4,1024,64]{2,1,0:T(8,128)} %get-tuple-element.27, f32[4,1024,64]{2,1,0:T(8,128)} %get-tuple-element.29), kind=kLoop, calls=%fused_computation.30 | loop fusion | flops 524288 | bytes 3670016 | tf_op jit(solution)/shard_map/mul | solution.py:292
  190.5 2.2 copy.166
  193.8 1.9 fusion.18
  195.8 1.7 subtract_convert_fusion
  198.0 1.9 fusion.26
  201.0 5.5 %multiply_reduce_fusion = (bf16[1024]{0:T(1024)(128)(2,1)S(1)}, bf16[1024]{0:T(1024)(128)(2,1)S(1)}, f32[1024,1024]{1,0:T(8,128)}, f32[1024,1024]{1,0:T(8,128)}) fusion(f32[1024]{0:T(1024)S(1)} %add_rsqrt_fusion, f32[1024]{0:T(1024)S(1)} %broadcast_multiply_fusion, bf16[1024,2048]{1,0:T(8,128)(2,1)S(1)} %bitcast.184, f32[1024,1024]{1,0:T(8,128)S(1)} %fusion.26, ...), kind=kOutput, calls=%fused_computation.15 | convolution fusion | flops 2154821632 | bytes 18886656 | tf_op jit(solution)/shard_map/dot_general | solution.py:300
  206.8 4.1 %convolution_convert_fusion.2 = bf16[1024,768]{1,0:T(8,128)(2,1)S(1)} fusion(bf16[1024,256]{0,1:T(8,128)(2,1)} %bitcast.233, bf16[1024,512]{0,1:T(8,128)(2,1)S(1)} %subtract_convert_fusion, f32[1024]{0:T(1024)S(1)} %get-tuple-element.33, f32[1024]{0:T(1024)S(1)} %get-tuple-element.34, f32[1024]{0:T(1024)S(1)} %add_rsqrt_fusion, ...), kind=kOutput, calls=%fused_computation.37 | convolution fusion | flops 1620836352 | bytes 5259264 | tf_op jit(solution)/shard_map/dot_general | solution.py:298
  210.9 2.7 convolution_convert_fusion.1
  214.0 2.3 copy.179
  216.4 2.7 convert.90
  220.7 1.7 collective-permute-start.13
  222.5 2.4 fusion.88
  228.0 3.2 collective-permute-start.9
  232.9 1.8 collective-permute-start.12
  234.7 2.7 collective-permute-done.7
  239.4 3.9 %collective-permute-start.10 = (bf16[256,1024]{1,0:T(8,128)(2,1)S(1)}, bf16[256,1024]{1,0:T(8,128)(2,1)S(1)}, u32[]{:S(2)}, u32[]{:S(2)}) collective-permute-start(bf16[256,1024]{1,0:T(8,128)(2,1)S(1)} %pad_maximum_fusion.11), channel_id=1, source_target_pairs={{0,24},{8,0},{16,8},{24,16},{1,25},{9,1},{17,9},{25,17},{2,26},{10... | collective-permute-start | bytes 1572872 | tf_op jit(solution)/shard_map/ppermute | solution.py:81
  243.4 5.8 %collective-permute-done.14 = bf16[256,1024]{1,0:T(8,128)(2,1)S(1)} collective-permute-done((bf16[256,1024]{1,0:T(8,128)(2,1)S(1)}, bf16[256,1024]{1,0:T(8,128)(2,1)S(1)}, u32[]{:S(2)}, u32[]{:S(2)}) %collective-permute-start.14) | collective-permute-done | bytes 524320 | tf_op jit(solution)/shard_map/ppermute | solution.py:81
  249.1 1.9 fusion.83
  251.1 7.2 %collective-permute-done.10 = bf16[256,1024]{1,0:T(8,128)(2,1)S(1)} collective-permute-done((bf16[256,1024]{1,0:T(8,128)(2,1)S(1)}, bf16[256,1024]{1,0:T(8,128)(2,1)S(1)}, u32[]{:S(2)}, u32[]{:S(2)}) %collective-permute-start.10) | collective-permute-done | bytes 524320 | tf_op jit(solution)/shard_map/ppermute | solution.py:81
  258.8 2.4 fusion.44
  261.2 16.5 %reduce-scatter.3.cloned.1.call-done = bf16[128,1920]{1,0:T(8,128)(2,1)} async-done(((bf16[1024,1920]{1,0:T(8,128)(2,1)}), bf16[128,1920]{1,0:T(8,128)(2,1)}) %reduce-scatter.3.cloned.1.call-update) | async-done | bytes 491536 | tf_op jit(solution)/shard_map/reduce_scatter | solution.py:321
  277.7 2.4 fusion.43
  281.2 2.9 collective-permute-start.21
  285.0 9.0 %collective-permute-done.21 = bf16[1,176,1024]{2,1,0:T(8,128)(2,1)S(1)} collective-permute-done((bf16[1,176,1024]{2,1,0:T(8,128)(2,1)S(1)}, bf16[1,176,1024]{2,1,0:T(8,128)(2,1)S(1)}, u32[]{:S(2)}, u32[]{:S(2)}) %collective-permute-start.21) | collective-permute-done | bytes 360480 | tf_op jit(solution)/shard_map/ppermute | solution.py:105
  295.7 8.4 %collective-permute-done.16 = bf16[128,1920]{1,0:T(8,128)(2,1)S(1)} collective-permute-done((bf16[128,1920]{1,0:T(8,128)(2,1)S(1)}, bf16[128,1920]{1,0:T(8,128)(2,1)S(1)}, u32[]{:S(2)}, u32[]{:S(2)}) %collective-permute-start.16) | collective-permute-done | bytes 491552 | tf_op jit(solution)/shard_map/ppermute | solution.py:105
  304.2 2.8 collective-permute-start.17
  308.2 2.3 collective-permute-start.18
  310.5 5.3 %collective-permute-done.18 = bf16[32,1920]{1,0:T(8,128)(2,1)S(1)} collective-permute-done((bf16[32,1920]{1,0:T(8,128)(2,1)S(1)}, bf16[32,1920]{1,0:T(8,128)(2,1)S(1)}, u32[]{:S(2)}, u32[]{:S(2)}) %collective-permute-start.18) | collective-permute-done | bytes 122912 | tf_op jit(solution)/shard_map/ppermute | solution.py:90
  (209 shorter events, 63.2 us)
Async XLA Ops:
  7.2 70.8 %all-gather.7.cloned.1.call-start = ((), (), s32[]{:S(2)}) async-start(), calls=%async_computation.5 | async-start | bytes 3244032 | tf_op jit(solution)/shard_map/all_gather | solution.py:233
  9.0 98.0 %all-gather.5.cloned.1.call-start = ((), (), s32[]{:S(2)}) async-start(), calls=%async_computation.4 | async-start | bytes 4423680 | tf_op jit(solution)/shard_map/all_gather | solution.py:223
  13.9 17.3 %copy-start.21 = (bf16[1,256,1024]{2,1,0:T(8,128)(2,1)S(1)}, bf16[1,256,1024]{2,1,0:T(8,128)(2,1)}, u32[]{:S(2)}) copy-start(bf16[1,256,1024]{2,1,0:T(8,128)(2,1)} %param.25) | copy-start | bytes 1572868
  13.9 8.4 %collective-permute-start.4 = (bf16[32,1920]{1,0:T(8,128)(2,1)S(1)}, bf16[32,1920]{1,0:T(8,128)(2,1)S(1)}, u32[]{:S(2)}, u32[]{:S(2)}) collective-permute-start(bf16[32,1920]{1,0:T(8,128)(2,1)S(1)} %bitcast.238), channel_id=1, source_target_pairs={{0,24},{8,0},{16,8},{24,16},{1,25},{9,1},{17,9},{25,17},{2,26},{10... | collective-permute-start | bytes 368648 | tf_op jit(solution)/shard_map/ppermute | solution.py:90
  17.1 7.7 %collective-permute-start.5 = (bf16[32,1920]{1,0:T(8,128)(2,1)S(1)}, bf16[32,1920]{1,0:T(8,128)(2,1)S(1)}, u32[]{:S(2)}, u32[]{:S(2)}) collective-permute-start(bf16[32,1920]{1,0:T(8,128)(2,1)S(1)} %bitcast.240), channel_id=1, source_target_pairs={{0,16},{8,24},{16,0},{24,8},{1,17},{9,25},{17,1},{25,9},{2,18},{10... | collective-permute-start | bytes 368648 | tf_op jit(solution)/shard_map/ppermute | solution.py:90
  17.8 13.5 %copy-start.19 = (bf16[1,256,1024]{2,1,0:T(8,128)(2,1)S(1)}, bf16[1,256,1024]{2,1,0:T(8,128)(2,1)}, u32[]{:S(2)}) copy-start(bf16[1,256,1024]{2,1,0:T(8,128)(2,1)} %param.14) | copy-start | bytes 1572868
  17.9 8.3 %collective-permute-start.6 = (bf16[32,1920]{1,0:T(8,128)(2,1)S(1)}, bf16[32,1920]{1,0:T(8,128)(2,1)S(1)}, u32[]{:S(2)}, u32[]{:S(2)}) collective-permute-start(bf16[32,1920]{1,0:T(8,128)(2,1)S(1)} %bitcast.242), channel_id=1, source_target_pairs={{0,8},{8,16},{16,24},{24,0},{1,9},{9,17},{17,25},{25,1},{2,10},{10... | collective-permute-start | bytes 368648 | tf_op jit(solution)/shard_map/ppermute | solution.py:90
  30.5 230.7 %reduce-scatter.5.cloned.1.call-start = ((), (), s32[]{:S(2)}) async-start(), calls=%async_computation.3 | async-start | bytes 3244032 | tf_op jit(solution)/shard_map/reduce_scatter | solution.py:346
  31.5 24.9 %collective-permute-start = (bf16[256,2048]{1,0:T(8,128)(2,1)S(1)}, bf16[256,2048]{1,0:T(8,128)(2,1)S(1)}, u32[]{:S(2)}, u32[]{:S(2)}) collective-permute-start(bf16[256,2048]{1,0:T(8,128)(2,1)S(1)} %get-tuple-element.58), channel_id=1, source_target_pairs={{0,24},{8,0},{16,8},{24,16},{1,25},{9,1},{17,9},{25,17},{2,26},{10... | collective-permute-start | bytes 3145736 | tf_op jit(solution)/shard_map/ppermute | solution.py:65
  32.1 26.6 %collective-permute-start.1 = (bf16[256,2048]{1,0:T(8,128)(2,1)S(1)}, bf16[256,2048]{1,0:T(8,128)(2,1)S(1)}, u32[]{:S(2)}, u32[]{:S(2)}) collective-permute-start(bf16[256,2048]{1,0:T(8,128)(2,1)S(1)} %get-tuple-element.58), channel_id=1, source_target_pairs={{0,8},{8,16},{16,24},{24,0},{1,9},{9,17},{17,25},{25,1},{2,10},{10... | collective-permute-start | bytes 3145736 | tf_op jit(solution)/shard_map/ppermute | solution.py:64
  57.2 13.1 %collective-permute-start.3 = (bf16[128,2048]{1,0:T(8,128)(2,1)}, bf16[128,2048]{1,0:T(8,128)(2,1)}, u32[]{:S(2)}, u32[]{:S(2)}) collective-permute-start(bf16[128,2048]{1,0:T(8,128)(2,1)} %slice.249), channel_id=1, source_target_pairs={{0,24},{8,0},{16,8},{24,16},{1,25},{9,1},{17,9},{25,17},{2,26},{10... | collective-permute-start | bytes 1572872 | tf_op jit(solution)/shard_map/ppermute | solution.py:67
  59.6 13.6 %collective-permute-start.2 = (bf16[128,2048]{1,0:T(8,128)(2,1)}, bf16[128,2048]{1,0:T(8,128)(2,1)}, u32[]{:S(2)}, u32[]{:S(2)}) collective-permute-start(bf16[128,2048]{1,0:T(8,128)(2,1)} %slice.248), channel_id=1, source_target_pairs={{0,8},{8,16},{16,24},{24,0},{1,9},{9,17},{17,25},{25,1},{2,10},{10... | collective-permute-start | bytes 1572872 | tf_op jit(solution)/shard_map/ppermute | solution.py:66
  60.2 15.1 %copy-start.26 = (s32[1,1,4,256]{3,1,2,0:T(1,128)}, s32[1,1,4,256]{3,1,2,0:T(1,128)S(1)}, u32[]{:S(2)}) copy-start(s32[1,1,4,256]{3,1,2,0:T(1,128)S(1)} %copy.189) | copy-start | bytes 12292
  77.9 156.8 %copy-start.25 = (f32[1024]{0:T(1024)}, f32[1024]{0:T(1024)S(1)}, u32[]{:S(2)}) copy-start(f32[1024]{0:T(1024)S(1)} %add_rsqrt_fusion) | copy-start | bytes 12292
  78.0 4.8 %copy-start.1 = (bf16[4,256,2048]{2,1,0:T(8,128)(2,1)S(1)}, bf16[4,256,2048]{2,1,0:T(8,128)(2,1)}, u32[]{:S(2)}) copy-start(bf16[4,256,2048]{2,1,0:T(8,128)(2,1)} %copy-done) | copy-start | bytes 12582916
  79.2 4.3 %copy-start.15 = (bf16[8,32,1024]{2,1,0:T(8,128)(2,1)}, bf16[8,32,1024]{2,1,0:T(8,128)(2,1)S(1)}, u32[]{:S(2)}) copy-start(bf16[8,32,1024]{2,1,0:T(8,128)(2,1)S(1)} %slice.266) | copy-start | bytes 1572868
  107.0 3.4 %copy-start.2 = (bf16[4,256,2048]{2,1,0:T(8,128)(2,1)S(1)}, bf16[4,256,2048]{2,1,0:T(8,128)(2,1)}, u32[]{:S(2)}) copy-start(bf16[4,256,2048]{2,1,0:T(8,128)(2,1)} %copy-done) | copy-start | bytes 12582916
  109.7 3.0 copy-start.7
  123.8 2.9 copy-start.11
  160.8 6.3 %copy-start.13 = (bf16[1024,4,64]{0,2,1:T(8,128)(2,1)}, bf16[1024,4,64]{0,2,1:T(8,128)(2,1)S(1)}, u32[]{:S(2)}) copy-start(bf16[1024,4,64]{0,2,1:T(8,128)(2,1)S(1)} %copy.165) | copy-start | bytes 1572868
  160.9 6.3 %copy-start.3 = (bf16[4,256,2048]{2,1,0:T(8,128)(2,1)S(1)}, bf16[4,256,2048]{2,1,0:T(8,128)(2,1)}, u32[]{:S(2)}) copy-start(bf16[4,256,2048]{2,1,0:T(8,128)(2,1)} %copy-done) | copy-start | bytes 12582916
  167.2 4.1 %copy-start.27 = (bf16[1024,1024]{0,1:T(8,128)(2,1)}, bf16[1024,1024]{0,1:T(8,128)(2,1)S(1)}, u32[]{:S(2)}) copy-start(bf16[1024,1024]{0,1:T(8,128)(2,1)S(1)} %get-tuple-element.79) | copy-start | bytes 6291460
  181.3 96.4 %reduce-scatter.3.cloned.1.call-start = ((), (), s32[]{:S(2)}) async-start(), calls=%async_computation.2 | async-start | bytes 4423680 | tf_op jit(solution)/shard_map/reduce_scatter | solution.py:321
  198.0 2.9 copy-start.12
  206.8 4.1 %copy-start.5 = (bf16[4,256,2048]{2,1,0:T(8,128)(2,1)S(1)}, bf16[4,256,2048]{2,1,0:T(8,128)(2,1)}, u32[]{:S(2)}) copy-start(bf16[4,256,2048]{2,1,0:T(8,128)(2,1)} %copy-done) | copy-start | bytes 12582916
  216.3 6.1 %copy-start.18 = (bf16[8,128,1024]{2,1,0:T(8,128)(2,1)S(1)}, bf16[8,128,1024]{2,1,0:T(8,128)(2,1)}, u32[]{:S(2)}) copy-start(bf16[8,128,1024]{2,1,0:T(8,128)(2,1)} %slice.269) | copy-start | bytes 6291460
  216.4 6.1 %copy-start.28 = (bf16[1024,1024]{0,1:T(8,128)(2,1)S(1)}, bf16[1024,1024]{0,1:T(8,128)(2,1)}, u32[]{:S(2)}) copy-start(bf16[1024,1024]{0,1:T(8,128)(2,1)} %copy-done.27) | copy-start | bytes 6291460
  219.2 12.0 %collective-permute-start.11 = (bf16[128,1024]{1,0:T(8,128)(2,1)S(1)}, bf16[128,1024]{1,0:T(8,128)(2,1)S(1)}, u32[]{:S(2)}, u32[]{:S(2)}) collective-permute-start(bf16[128,1024]{1,0:T(8,128)(2,1)S(1)} %get-tuple-element.47), channel_id=1, source_target_pairs={{0,8},{8,16},{16,24},{24,0},{1,9},{9,17},{17,25},{25,1},{2,10},{10... | collective-permute-start | bytes 786440 | tf_op jit(solution)/shard_map/ppermute | solution.py:76
  220.7 4.2 %copy-start.14 = (bf16[1024,4,64]{0,2,1:T(8,128)(2,1)S(1)}, bf16[1024,4,64]{0,2,1:T(8,128)(2,1)}, u32[]{:S(2)}) copy-start(bf16[1024,4,64]{0,2,1:T(8,128)(2,1)} %copy-done.13) | copy-start | bytes 1572868
  220.7 4.2 %copy-start.16 = (bf16[8,32,1024]{2,1,0:T(8,128)(2,1)S(1)}, bf16[8,32,1024]{2,1,0:T(8,128)(2,1)}, u32[]{:S(2)}) copy-start(bf16[8,32,1024]{2,1,0:T(8,128)(2,1)} %copy-done.15) | copy-start | bytes 1572868
  220.7 10.4 %collective-permute-start.13 = (bf16[128,1024]{1,0:T(8,128)(2,1)S(1)}, bf16[128,1024]{1,0:T(8,128)(2,1)S(1)}, u32[]{:S(2)}, u32[]{:S(2)}) collective-permute-start(bf16[128,1024]{1,0:T(8,128)(2,1)S(1)} %get-tuple-element.48), channel_id=1, source_target_pairs={{0,24},{8,0},{16,8},{24,16},{1,25},{9,1},{17,9},{25,17},{2,26},{10... | collective-permute-start | bytes 786440 | tf_op jit(solution)/shard_map/ppermute | solution.py:77
  227.7 9.7 %collective-permute-start.7 = (bf16[128,1024]{1,0:T(8,128)(2,1)S(1)}, bf16[128,1024]{1,0:T(8,128)(2,1)S(1)}, u32[]{:S(2)}, u32[]{:S(2)}) collective-permute-start(bf16[128,1024]{1,0:T(8,128)(2,1)S(1)} %get-tuple-element.51), channel_id=1, source_target_pairs={{0,8},{8,16},{16,24},{24,0},{1,9},{9,17},{17,25},{25,1},{2,10},{10... | collective-permute-start | bytes 786440 | tf_op jit(solution)/shard_map/ppermute | solution.py:76
  228.0 9.9 %collective-permute-start.9 = (bf16[128,1024]{1,0:T(8,128)(2,1)S(1)}, bf16[128,1024]{1,0:T(8,128)(2,1)}, u32[]{:S(2)}, u32[]{:S(2)}) collective-permute-start(bf16[128,1024]{1,0:T(8,128)(2,1)S(1)} %get-tuple-element.52), channel_id=1, source_target_pairs={{0,24},{8,0},{16,8},{24,16},{1,25},{9,1},{17,9},{25,17},{2,26},{10... | collective-permute-start | bytes 786440 | tf_op jit(solution)/shard_map/ppermute | solution.py:77
  232.5 16.6 %collective-permute-start.14 = (bf16[256,1024]{1,0:T(8,128)(2,1)S(1)}, bf16[256,1024]{1,0:T(8,128)(2,1)S(1)}, u32[]{:S(2)}, u32[]{:S(2)}) collective-permute-start(bf16[256,1024]{1,0:T(8,128)(2,1)S(1)} %pad_maximum_fusion.13), channel_id=1, source_target_pairs={{0,24},{8,0},{16,8},{24,16},{1,25},{9,1},{17,9},{25,17},{2,26},{10... | collective-permute-start | bytes 1572872 | tf_op jit(solution)/shard_map/ppermute | solution.py:81
  232.9 16.2 %collective-permute-start.12 = (bf16[256,1024]{1,0:T(8,128)(2,1)S(1)}, bf16[256,1024]{1,0:T(8,128)(2,1)S(1)}, u32[]{:S(2)}, u32[]{:S(2)}) collective-permute-start(bf16[256,1024]{1,0:T(8,128)(2,1)S(1)} %pad_maximum_fusion.12), channel_id=1, source_target_pairs={{0,8},{8,16},{16,24},{24,0},{1,9},{9,17},{17,25},{25,1},{2,10},{10... | collective-permute-start | bytes 1572872 | tf_op jit(solution)/shard_map/ppermute | solution.py:80
  234.7 24.1 %copy-start.20 = (bf16[1,256,1024]{2,1,0:T(8,128)(2,1)S(1)}, bf16[1,256,1024]{2,1,0:T(8,128)(2,1)}, u32[]{:S(2)}) copy-start(bf16[1,256,1024]{2,1,0:T(8,128)(2,1)} %param.14) | copy-start | bytes 1572868
  239.4 18.9 %collective-permute-start.10 = (bf16[256,1024]{1,0:T(8,128)(2,1)S(1)}, bf16[256,1024]{1,0:T(8,128)(2,1)S(1)}, u32[]{:S(2)}, u32[]{:S(2)}) collective-permute-start(bf16[256,1024]{1,0:T(8,128)(2,1)S(1)} %pad_maximum_fusion.11), channel_id=1, source_target_pairs={{0,24},{8,0},{16,8},{24,16},{1,25},{9,1},{17,9},{25,17},{2,26},{10... | collective-permute-start | bytes 1572872 | tf_op jit(solution)/shard_map/ppermute | solution.py:81
  243.3 34.4 %copy-start.22 = (bf16[1,256,1024]{2,1,0:T(8,128)(2,1)S(1)}, bf16[1,256,1024]{2,1,0:T(8,128)(2,1)}, u32[]{:S(2)}) copy-start(bf16[1,256,1024]{2,1,0:T(8,128)(2,1)} %param.25) | copy-start | bytes 1572868
  243.3 34.4 %slice-start = ((f32[1024]{0:T(1024)}), f32[256]{0:T(256)S(1)}, s32[]{:S(2)}) async-start(f32[1024]{0:T(1024)} %copy-done.25), calls=%async_computation.6 | async-start | bytes 2048 | tf_op jit(solution)/shard_map/slice | solution.py:306
  243.3 15.5 %collective-permute-start.8 = (bf16[256,1024]{1,0:T(8,128)(2,1)S(1)}, bf16[256,1024]{1,0:T(8,128)(2,1)S(1)}, u32[]{:S(2)}, u32[]{:S(2)}) collective-permute-start(bf16[256,1024]{1,0:T(8,128)(2,1)S(1)} %pad_maximum_fusion.10), channel_id=1, source_target_pairs={{0,8},{8,16},{16,24},{24,0},{1,9},{9,17},{17,25},{25,1},{2,10},{10... | collective-permute-start | bytes 1572872 | tf_op jit(solution)/shard_map/ppermute | solution.py:80
  261.2 18.9 %collective-permute-start.20 = (bf16[1,176,1024]{2,1,0:T(8,128)(2,1)}, bf16[1,176,1024]{2,1,0:T(8,128)(2,1)S(1)}, u32[]{:S(2)}, u32[]{:S(2)}) collective-permute-start(bf16[1,176,1024]{2,1,0:T(8,128)(2,1)} %reduce-scatter.5.cloned.1.call-done), channel_id=1, source_target_pairs={{0,32},{32,0},{64,96},{96,64},{1,33},{33,1},{65,97},{97,65},{2,34}... | collective-permute-start | bytes 1081352 | tf_op jit(solution)/shard_map/ppermute | solution.py:103
  277.7 6.4 %copy-start.24 = (bf16[128,1920]{1,0:T(8,128)(2,1)S(1)}, bf16[128,1920]{1,0:T(8,128)(2,1)}, u32[]{:S(2)}) copy-start(bf16[128,1920]{1,0:T(8,128)(2,1)} %reduce-scatter.3.cloned.1.call-done) | copy-start | bytes 1474564
  277.7 6.4 %collective-permute-start.15 = (bf16[128,1920]{1,0:T(8,128)(2,1)}, bf16[128,1920]{1,0:T(8,128)(2,1)S(1)}, u32[]{:S(2)}, u32[]{:S(2)}) collective-permute-start(bf16[128,1920]{1,0:T(8,128)(2,1)} %reduce-scatter.3.cloned.1.call-done), channel_id=1, source_target_pairs={{0,32},{32,0},{64,96},{96,64},{1,33},{33,1},{65,97},{97,65},{2,34}... | collective-permute-start | bytes 1474568 | tf_op jit(solution)/shard_map/ppermute | solution.py:103
  281.2 12.8 %collective-permute-start.21 = (bf16[1,176,1024]{2,1,0:T(8,128)(2,1)S(1)}, bf16[1,176,1024]{2,1,0:T(8,128)(2,1)S(1)}, u32[]{:S(2)}, u32[]{:S(2)}) collective-permute-start(bf16[1,176,1024]{2,1,0:T(8,128)(2,1)S(1)} %add_convert_fusion.3), channel_id=1, source_target_pairs={{0,64},{32,96},{64,0},{96,32},{1,65},{33,97},{65,1},{97,33},{2,66}... | collective-permute-start | bytes 1081352 | tf_op jit(solution)/shard_map/ppermute | solution.py:105
  284.3 19.8 %collective-permute-start.16 = (bf16[128,1920]{1,0:T(8,128)(2,1)S(1)}, bf16[128,1920]{1,0:T(8,128)(2,1)S(1)}, u32[]{:S(2)}, u32[]{:S(2)}) collective-permute-start(bf16[128,1920]{1,0:T(8,128)(2,1)S(1)} %add_convert_fusion.2), channel_id=1, source_target_pairs={{0,64},{32,96},{64,0},{96,32},{1,65},{33,97},{65,1},{97,33},{2,66}... | collective-permute-start | bytes 1474568 | tf_op jit(solution)/shard_map/ppermute | solution.py:105
  304.2 6.2 %collective-permute-start.17 = (bf16[32,1920]{1,0:T(8,128)(2,1)S(1)}, bf16[32,1920]{1,0:T(8,128)(2,1)S(1)}, u32[]{:S(2)}, u32[]{:S(2)}) collective-permute-start(bf16[32,1920]{1,0:T(8,128)(2,1)S(1)} %get-tuple-element.68), channel_id=1, source_target_pairs={{0,24},{8,0},{16,8},{24,16},{1,25},{9,1},{17,9},{25,17},{2,26},{10... | collective-permute-start | bytes 368648 | tf_op jit(solution)/shard_map/ppermute | solution.py:90
  308.2 8.5 %collective-permute-start.19 = (bf16[32,1920]{1,0:T(8,128)(2,1)S(1)}, bf16[32,1920]{1,0:T(8,128)(2,1)S(1)}, u32[]{:S(2)}, u32[]{:S(2)}) collective-permute-start(bf16[32,1920]{1,0:T(8,128)(2,1)S(1)} %get-tuple-element.65), channel_id=1, source_target_pairs={{0,8},{8,16},{16,24},{24,0},{1,9},{9,17},{17,25},{25,1},{2,10},{10... | collective-permute-start | bytes 368648 | tf_op jit(solution)/shard_map/ppermute | solution.py:90
  308.2 7.6 %collective-permute-start.18 = (bf16[32,1920]{1,0:T(8,128)(2,1)S(1)}, bf16[32,1920]{1,0:T(8,128)(2,1)S(1)}, u32[]{:S(2)}, u32[]{:S(2)}) collective-permute-start(bf16[32,1920]{1,0:T(8,128)(2,1)S(1)} %get-tuple-element.67), channel_id=1, source_target_pairs={{0,16},{8,24},{16,0},{24,8},{1,17},{9,25},{17,1},{25,9},{2,18},{10... | collective-permute-start | bytes 368648 | tf_op jit(solution)/shard_map/ppermute | solution.py:90
  (8 other events, 15.8 us)
Sparse Core Ops, SparseCore 0:
  10.2 45.4 all-gather.6
  57.4 49.5 all-gather.4
  181.4 44.3 reduce-scatter.4
  228.1 49.5 reduce-scatter.2

commit v6 on v5

--- a/solution.py
+++ b/solution.py
@@ -317,11 +317,12 @@
     column_grads = jnp.concatenate(
         [grad_triple_weight, grad_inner_weight, small_grads], -1
     ).astype(bf16)
-    column_grads = column_grads.reshape(nc, nf, shard_rows, -1).swapaxes(0, 1).reshape(width, -1)
+    grad_cols = column_grads.shape[-1]
+    column_grads = ring_all_to_all(column_grads.reshape(nc, nf * shard_rows, grad_cols), "ctx")
+    column_grads = column_grads.swapaxes(0, 1).reshape(nf * shard_rows, nc * grad_cols)
     column_grads = lax.psum_scatter(column_grads, "fsdp", scatter_dimension=0, tiled=True)
-    column_grads = replica_sum(column_grads, "rep").astype(bf16)
-    column_grads = column_grads.reshape(nc, shard_rows, -1)
-    column_grads = ring_all_to_all(column_grads, "ctx").astype(f32)
+    column_grads = replica_sum(column_grads, "rep").astype(bf16).astype(f32)
+    column_grads = column_grads.reshape(shard_rows, nc, grad_cols).swapaxes(0, 1)
     grad_triple_out = (
         column_grads[:, :, : 3 * head_cols]
         .reshape(nc, shard_rows, 3, head_cols)

time: 333 us -> 373 us (1.12)
  the two profiles are of different devices: /device:TPU:0 before, /device:TPU:24 now
where the time goes in v6:
time: 373 us; the launch traced here: 365 us
  waiting for transfers between devices  129 us (35%)
  local copies, waits for them, and re-layouts  62.8 us (17%)
  matrix products  55.2 us (15%)
  other arithmetic  37.4 us (10%)
  starting transfers between devices  33.8 us (9%)
  Pallas kernels  31.1 us (8%)
  between operations  16.6 us (4%)
    ppermute x6, waiting for transfers between devices, ring_all_to_all(): lax.ppermute(pick(me + s), axis, ring_pairs(n, s))  47.4 us
    pallas_call x1, Pallas kernels, fused_attention(): pl.pallas_call(attention_kernel, out_shape=(jax.ShapeDtypeStruct((heads,...  31.1 us
    all_gather x1, waiting for transfers between devices, local(): column_block = lax.all_gather(column_payload, 'fsdp', axis=0, tiled=False)  24.6 us
    ppermute x1, waiting for transfers between devices, ring_gather(): from_right = lax.ppermute(block, axis, ring_pairs(n, -1))  22.4 us
    unnamed x79, local copies, waits for them, and re-layouts  17.9 us
    ppermute x2, waiting for transfers between devices, ring_scatter(): from_right = lax.ppermute(to_left.astype(wire), axis, ring_pairs(n, -1))  12.2 us
    ppermute x2, waiting for transfers between devices, replica_sum(): lax.ppermute(pair, axis, [(i, i ^ 2) for i in range(n)]).astype(f32)  11.8 us
    dot_general x1, matrix products, local(): jnp.dot(grad_before_gelu, inner_here.T, preferred_element_type=f32)  10.6 us
  transfers between devices with their start and end apart: 26, of which 14 were waited for; matrix products, arithmetic and copies ran while one was open for 19% of the time, Pallas kernels for 0%

profile of v6, /device:TPU:24, one launch (start us, length us, event | category | flops | bytes accessed | tf_op | source)
XLA Modules:
  0.0 365.4 jit_solution(5625810225892082772)
XLA Ops:
  15.7 2.3 collective-permute-start.6
  18.1 4.9 %collective-permute-done.4 = bf16[32,1920]{1,0:T(8,128)(2,1)S(1)} collective-permute-done((bf16[32,1920]{1,0:T(8,128)(2,1)S(1)}, bf16[32,1920]{1,0:T(8,128)(2,1)S(1)}, u32[]{:S(2)}, u32[]{:S(2)}) %collective-permute-start.4) | collective-permute-done | bytes 122912 | tf_op jit(solution)/shard_map/ppermute | solution.py:90
  23.8 3.0 concatenate.73
  29.7 2.6 collective-permute-start.1
  32.4 22.4 %collective-permute-done = bf16[256,2048]{1,0:T(8,128)(2,1)S(1)} collective-permute-done((bf16[256,2048]{1,0:T(8,128)(2,1)S(1)}, bf16[256,2048]{1,0:T(8,128)(2,1)S(1)}, u32[]{:S(2)}, u32[]{:S(2)}) %collective-permute-start) | collective-permute-done | bytes 1048608 | tf_op jit(solution)/shard_map/ppermute | solution.py:65
  56.5 3.2 collective-permute-start.2
  61.8 2.6 fusion.61
  64.3 5.2 %collective-permute-done.3 = bf16[128,2048]{1,0:T(8,128)(2,1)} collective-permute-done((bf16[128,2048]{1,0:T(8,128)(2,1)}, bf16[128,2048]{1,0:T(8,128)(2,1)}, u32[]{:S(2)}, u32[]{:S(2)}) %collective-permute-start.3) | collective-permute-done | bytes 524320 | tf_op jit(solution)/shard_map/ppermute | solution.py:67
  75.7 3.5 slice.269
  82.1 24.6 %all-gather.5.cloned.1.call-done = bf16[32,32,1920]{2,1,0:T(8,128)(2,1)} async-done(((bf16[4,32,1920]{2,1,0:T(8,128)(2,1)}), bf16[32,32,1920]{2,1,0:T(8,128)(2,1)}) %all-gather.5.cloned.1.call-update) | async-done | bytes 3932176 | tf_op jit(solution)/shard_map/all_gather | solution.py:223
  106.7 2.6 copy.165
  110.0 2.3 fusion.28
  120.5 3.0 copy.196
  123.5 3.0 maximum_bitcast_fusion.1.k_ref
  128.2 31.1 %shard_map.195 = (bf16[4,1024,64]{2,1,0:T(8,128)(2,1)}, f32[4,1024,64]{2,1,0:T(8,128)}, f32[4,1024,64]{2,1,0:T(8,128)}, f32[4,1024,64]{2,1,0:T(8,128)}) custom-call(s32[1]{0:T(128)S(6)} %copy.226.span_ref, bf16[4,1024,64]{2,1,0:T(8,128)(2,1)} %fusion.34.q_ref, bf16[4,1024,64]{2,1,0:T(8,128)(2,1)} %maximum_bitcast_fusion.1.k_ref, ...), custom_call_target="tpu_custom_call" | custom-call | flops 3221225472 | bytes 5767168 | tf_op jit(solution)/shard_map/pallas_call | solution.py:158
  159.3 2.2 copy.177
  161.5 3.8 %multiply_bitcast_fusion = (f32[1024,4,64]{2,0,1:T(8,128)}, bf16[1024,4,64]{2,0,1:T(8,128)(2,1)S(1)}) fusion(f32[4,1024,64]{2,1,0:T(8,128)} %get-tuple-element.27, f32[4,1024,64]{2,1,0:T(8,128)} %get-tuple-element.29), kind=kLoop, calls=%fused_computation.30 | loop fusion | flops 524288 | bytes 3670016 | tf_op jit(solution)/shard_map/mul | solution.py:292
  165.3 2.2 copy.176
  172.9 3.6 convolution_convert_fusion.2
  176.5 5.4 %fusion.26 = f32[1024,1024]{1,0:T(8,128)} fusion(bf16[1024,1920]{1,0:T(8,128)(2,1)} %bitcast.201, bf16[1024,256]{0,1:T(8,128)(2,1)S(1)} %bitcast.247, bf16[1024,512]{0,1:T(8,128)(2,1)S(1)} %subtract_convert_fusion), kind=kOutput, calls=%fused_computation.44 | convolution fusion | flops 1613758464 | bytes 7340032 | tf_op jit(solution)/shard_map/dot_general | solution.py:299
  182.3 8.3 %multiply_convert_fusion = (bf16[1024,1024]{0,1:T(8,128)(2,1)S(1)}, f32[1024,1024]{0,1:T(8,128)}) fusion(f32[1024]{0:T(1024)S(1)} %bitcast.262, bf16[1024,1920]{1,0:T(8,128)(2,1)} %bitcast.202, f32[1024]{0:T(1024)S(1)} %get-tuple-element.33, f32[1024]{0:T(1024)S(1)} %get-tuple-element.34, f32[1024]{0:T(1024)S(1)} %add_rsqrt_fusion, ...), kind=kOutput, calls=%fused_computation.16 | convolution fusion | flops 2164260864 | bytes 10506240 | tf_op jit(solution)/shard_map/dot_general | solution.py:275
  190.6 4.0 %convolution_convert_fusion = bf16[1296,1024]{1,0:T(8,128)(2,1)S(1)} fusion(bf16[1024,1024]{0,1:T(8,128)(2,1)S(1)} %get-tuple-element.79, bf16[1024,256]{0,1:T(8,128)(2,1)S(1)} %bitcast.223, bf16[1024,2048]{1,0:T(8,128)(2,1)S(1)} %bitcast.194, bf16[1296]{0:T(1024)(128)(2,1)S(1)} %pad.25.clone), kind=kOutput, calls=%fused_computation.19 | convolution fusion | flops 2727198720 | bytes 7376896 | tf_op jit(solution)/shard_map/dot_general | solution.py:283
  196.5 2.6 copy.181
  199.1 8.1 %fusion.91 = (bf16[1024]{0:T(1024)(128)(2,1)S(1)}, bf16[1024,1024]{0,1:T(8,128)(2,1)S(1)}) fusion(f32[1024,1024]{0,1:T(8,128)} %get-tuple-element.80, f32[1024]{0:T(1024)S(1)} %bitcast.263, bf16[1024,1024]{1,0:T(8,128)(2,1)} %bitcast.231, bf16[1024,2048]{1,0:T(8,128)(2,1)} %bitcast.189), kind=kOutput, calls=%fused_computation.204 | convolution fusion | flops 2170551296 | bytes 10491904 | tf_op jit(solution)/shard_map/dot_general | solution.py:284
  207.2 2.7 convolution_convert_fusion.1
  209.9 2.6 copy.182
  212.5 2.0 pad_maximum_fusion.2
  216.7 10.6 %multiply_reduce_fusion = (bf16[1024]{0:T(1024)(128)(2,1)S(1)}, bf16[1024]{0:T(1024)(128)(2,1)S(1)}, f32[1024,1024]{1,0:T(8,128)}, f32[1024,1024]{1,0:T(8,128)}) fusion(f32[1024]{0:T(1024)S(1)} %add_rsqrt_fusion, f32[1024]{0:T(1024)S(1)} %broadcast_multiply_fusion, bf16[1024,2048]{1,0:T(8,128)(2,1)} %bitcast.190, f32[1024,1024]{1,0:T(8,128)} %fusion.26, ...), kind=kOutput, calls=%fused_computation.15 | convolution fusion | flops 2154821632 | bytes 18886656 | tf_op jit(solution)/shard_map/dot_general | solution.py:300
  230.0 2.1 collective-permute-start.17
  232.1 41.8 %collective-permute-done.15 = bf16[256,1920]{0,1:T(8,128)(2,1)S(1)} collective-permute-done((bf16[256,1920]{0,1:T(8,128)(2,1)S(1)}, bf16[256,1920]{0,1:T(8,128)(2,1)S(1)}, u32[]{:S(2)}, u32[]{:S(2)}) %collective-permute-start.15) | collective-permute-done | bytes 983072 | tf_op jit(solution)/shard_map/ppermute | solution.py:90
  274.9 2.1 constant_dynamic-slice_fusion.1
  277.0 6.3 %copy.191 = bf16[256,7680]{1,0:T(8,128)(2,1)} copy(bf16[256,7680]{0,1:T(8,128)(2,1)} %bitcast.198) | data formatting | bytes 7864320
  283.3 2.7 convert.92
  286.1 2.7 collective-permute-start.11
  288.8 2.4 fusion.92
  294.0 3.2 collective-permute-start.7
  300.3 3.5 collective-permute-start.12
  303.7 4.1 %collective-permute-done.9 = bf16[128,1024]{1,0:T(8,128)(2,1)} collective-permute-done((bf16[128,1024]{1,0:T(8,128)(2,1)S(1)}, bf16[128,1024]{1,0:T(8,128)(2,1)}, u32[]{:S(2)}, u32[]{:S(2)}) %collective-permute-start.9) | collective-permute-done | bytes 262176 | tf_op jit(solution)/shard_map/ppermute | solution.py:77
  310.9 3.2 collective-permute-start.8
  314.1 4.8 %collective-permute-done.14 = bf16[256,1024]{1,0:T(8,128)(2,1)S(1)} collective-permute-done((bf16[256,1024]{1,0:T(8,128)(2,1)S(1)}, bf16[256,1024]{1,0:T(8,128)(2,1)S(1)}, u32[]{:S(2)}, u32[]{:S(2)}) %collective-permute-start.14) | collective-permute-done | bytes 524320 | tf_op jit(solution)/shard_map/ppermute | solution.py:81
  318.9 2.0 fusion.87
  321.1 7.3 %collective-permute-done.10 = bf16[256,1024]{1,0:T(8,128)(2,1)} collective-permute-done((bf16[256,1024]{1,0:T(8,128)(2,1)}, bf16[256,1024]{1,0:T(8,128)(2,1)}, u32[]{:S(2)}, u32[]{:S(2)}) %collective-permute-start.10) | collective-permute-done | bytes 524320 | tf_op jit(solution)/shard_map/ppermute | solution.py:81
  328.4 2.7 fusion.44
  332.2 2.9 collective-permute-start.21
  335.2 2.4 fusion.43
  337.6 4.8 %collective-permute-done.21 = bf16[1,176,1024]{2,1,0:T(8,128)(2,1)S(1)} collective-permute-done((bf16[1,176,1024]{2,1,0:T(8,128)(2,1)S(1)}, bf16[1,176,1024]{2,1,0:T(8,128)(2,1)S(1)}, u32[]{:S(2)}, u32[]{:S(2)}) %collective-permute-start.21) | collective-permute-done | bytes 360480 | tf_op jit(solution)/shard_map/ppermute | solution.py:105
  343.2 2.9 collective-permute-start.19
  348.2 7.0 %collective-permute-done.19 = bf16[32,7680]{1,0:T(8,128)(2,1)S(1)} collective-permute-done((bf16[32,7680]{1,0:T(8,128)(2,1)S(1)}, bf16[32,7680]{1,0:T(8,128)(2,1)S(1)}, u32[]{:S(2)}, u32[]{:S(2)}) %collective-permute-start.19) | collective-permute-done | bytes 491552 | tf_op jit(solution)/shard_map/ppermute | solution.py:105
  (217 shorter events, 63.3 us)
Async XLA Ops:
  7.2 67.3 %all-gather.7.cloned.1.call-start = ((), (), s32[]{:S(2)}) async-start(), calls=%async_computation.4 | async-start | bytes 3244032 | tf_op jit(solution)/shard_map/all_gather | solution.py:233
  9.0 97.7 %all-gather.5.cloned.1.call-start = ((), (), s32[]{:S(2)}) async-start(), calls=%async_computation.3 | async-start | bytes 4423680 | tf_op jit(solution)/shard_map/all_gather | solution.py:223
  13.9 14.8 %copy-start.22 = (bf16[1,256,1024]{2,1,0:T(8,128)(2,1)S(1)}, bf16[1,256,1024]{2,1,0:T(8,128)(2,1)}, u32[]{:S(2)}) copy-start(bf16[1,256,1024]{2,1,0:T(8,128)(2,1)} %param.25) | copy-start | bytes 1572868
  13.9 14.9 %copy-start.20 = (bf16[1,256,1024]{2,1,0:T(8,128)(2,1)S(1)}, bf16[1,256,1024]{2,1,0:T(8,128)(2,1)}, u32[]{:S(2)}) copy-start(bf16[1,256,1024]{2,1,0:T(8,128)(2,1)} %param.14) | copy-start | bytes 1572868
  14.0 9.0 %collective-permute-start.4 = (bf16[32,1920]{1,0:T(8,128)(2,1)S(1)}, bf16[32,1920]{1,0:T(8,128)(2,1)S(1)}, u32[]{:S(2)}, u32[]{:S(2)}) collective-permute-start(bf16[32,1920]{1,0:T(8,128)(2,1)S(1)} %bitcast.251), channel_id=1, source_target_pairs={{0,24},{8,0},{16,8},{24,16},{1,25},{9,1},{17,9},{25,17},{2,26},{10... | collective-permute-start | bytes 368648 | tf_op jit(solution)/shard_map/ppermute | solution.py:90
  14.8 8.3 %collective-permute-start.5 = (bf16[32,1920]{1,0:T(8,128)(2,1)S(1)}, bf16[32,1920]{1,0:T(8,128)(2,1)S(1)}, u32[]{:S(2)}, u32[]{:S(2)}) collective-permute-start(bf16[32,1920]{1,0:T(8,128)(2,1)S(1)} %bitcast.253), channel_id=1, source_target_pairs={{0,16},{8,24},{16,0},{24,8},{1,17},{9,25},{17,1},{25,9},{2,18},{10... | collective-permute-start | bytes 368648 | tf_op jit(solution)/shard_map/ppermute | solution.py:90
  15.7 7.9 %collective-permute-start.6 = (bf16[32,1920]{1,0:T(8,128)(2,1)S(1)}, bf16[32,1920]{1,0:T(8,128)(2,1)S(1)}, u32[]{:S(2)}, u32[]{:S(2)}) collective-permute-start(bf16[32,1920]{1,0:T(8,128)(2,1)S(1)} %bitcast.255), channel_id=1, source_target_pairs={{0,8},{8,16},{16,24},{24,0},{1,9},{9,17},{17,25},{25,1},{2,10},{10... | collective-permute-start | bytes 368648 | tf_op jit(solution)/shard_map/ppermute | solution.py:90
  28.0 292.9 %reduce-scatter.5.cloned.1.call-start = ((), (), s32[]{:S(2)}) async-start(), calls=%async_computation.2 | async-start | bytes 3244032 | tf_op jit(solution)/shard_map/reduce_scatter | solution.py:347
  29.0 25.8 %collective-permute-start = (bf16[256,2048]{1,0:T(8,128)(2,1)S(1)}, bf16[256,2048]{1,0:T(8,128)(2,1)S(1)}, u32[]{:S(2)}, u32[]{:S(2)}) collective-permute-start(bf16[256,2048]{1,0:T(8,128)(2,1)S(1)} %get-tuple-element.62), channel_id=1, source_target_pairs={{0,24},{8,0},{16,8},{24,16},{1,25},{9,1},{17,9},{25,17},{2,26},{10... | collective-permute-start | bytes 3145736 | tf_op jit(solution)/shard_map/ppermute | solution.py:65
  29.7 26.0 %collective-permute-start.1 = (bf16[256,2048]{1,0:T(8,128)(2,1)S(1)}, bf16[256,2048]{1,0:T(8,128)(2,1)S(1)}, u32[]{:S(2)}, u32[]{:S(2)}) collective-permute-start(bf16[256,2048]{1,0:T(8,128)(2,1)S(1)} %get-tuple-element.62), channel_id=1, source_target_pairs={{0,8},{8,16},{16,24},{24,0},{1,9},{9,17},{17,25},{25,1},{2,10},{10... | collective-permute-start | bytes 3145736 | tf_op jit(solution)/shard_map/ppermute | solution.py:64
  55.6 13.9 %collective-permute-start.3 = (bf16[128,2048]{1,0:T(8,128)(2,1)}, bf16[128,2048]{1,0:T(8,128)(2,1)}, u32[]{:S(2)}, u32[]{:S(2)}) collective-permute-start(bf16[128,2048]{1,0:T(8,128)(2,1)} %slice.249), channel_id=1, source_target_pairs={{0,24},{8,0},{16,8},{24,16},{1,25},{9,1},{17,9},{25,17},{2,26},{10... | collective-permute-start | bytes 1572872 | tf_op jit(solution)/shard_map/ppermute | solution.py:67
  56.5 13.2 %collective-permute-start.2 = (bf16[128,2048]{1,0:T(8,128)(2,1)}, bf16[128,2048]{1,0:T(8,128)(2,1)}, u32[]{:S(2)}, u32[]{:S(2)}) collective-permute-start(bf16[128,2048]{1,0:T(8,128)(2,1)} %slice.248), channel_id=1, source_target_pairs={{0,8},{8,16},{16,24},{24,0},{1,9},{9,17},{17,25},{25,1},{2,10},{10... | collective-permute-start | bytes 1572872 | tf_op jit(solution)/shard_map/ppermute | solution.py:66
  60.4 11.3 %copy-start.28 = (s32[1,1,4,256]{3,1,2,0:T(1,128)}, s32[1,1,4,256]{3,1,2,0:T(1,128)S(1)}, u32[]{:S(2)}) copy-start(s32[1,1,4,256]{3,1,2,0:T(1,128)S(1)} %copy.203) | copy-start | bytes 12292
  74.4 229.3 %copy-start.27 = (f32[1024]{0:T(1024)}, f32[1024]{0:T(1024)S(1)}, u32[]{:S(2)}) copy-start(f32[1024]{0:T(1024)S(1)} %add_rsqrt_fusion) | copy-start | bytes 12292
  74.5 4.8 %copy-start.1 = (bf16[4,256,2048]{2,1,0:T(8,128)(2,1)S(1)}, bf16[4,256,2048]{2,1,0:T(8,128)(2,1)}, u32[]{:S(2)}) copy-start(bf16[4,256,2048]{2,1,0:T(8,128)(2,1)} %copy-done) | copy-start | bytes 12582916
  75.7 4.3 %copy-start.17 = (bf16[8,32,1024]{2,1,0:T(8,128)(2,1)}, bf16[8,32,1024]{2,1,0:T(8,128)(2,1)S(1)}, u32[]{:S(2)}) copy-start(bf16[8,32,1024]{2,1,0:T(8,128)(2,1)S(1)} %slice.266) | copy-start | bytes 1572868
  106.7 3.4 copy-start.2
  123.5 3.0 copy-start.10
  176.5 5.4 %copy-start.24 = (bf16[4,1024,64]{2,1,0:T(8,128)(2,1)S(1)}, bf16[4,1024,64]{2,1,0:T(8,128)(2,1)}, u32[]{:S(2)}) copy-start(bf16[4,1024,64]{2,1,0:T(8,128)(2,1)} %get-tuple-element.26) | copy-start | bytes 1572868
  182.3 8.4 %copy-start.15 = (bf16[1024,4,64]{0,2,1:T(8,128)(2,1)}, bf16[1024,4,64]{0,2,1:T(8,128)(2,1)S(1)}, u32[]{:S(2)}) copy-start(bf16[1024,4,64]{0,2,1:T(8,128)(2,1)S(1)} %copy.175) | copy-start | bytes 1572868
  182.3 8.4 %copy-start.4 = (bf16[4,256,2048]{2,1,0:T(8,128)(2,1)S(1)}, bf16[4,256,2048]{2,1,0:T(8,128)(2,1)}, u32[]{:S(2)}) copy-start(bf16[4,256,2048]{2,1,0:T(8,128)(2,1)} %copy-done) | copy-start | bytes 12582916
  190.6 4.1 %copy-start.29 = (bf16[1024,1024]{0,1:T(8,128)(2,1)}, bf16[1024,1024]{0,1:T(8,128)(2,1)S(1)}, u32[]{:S(2)}) copy-start(bf16[1024,1024]{0,1:T(8,128)(2,1)S(1)} %get-tuple-element.79) | copy-start | bytes 6291460
  194.7 4.4 %copy-start.13 = (bf16[1296,1024]{1,0:T(8,128)(2,1)}, bf16[1296,1024]{1,0:T(8,128)(2,1)S(1)}, u32[]{:S(2)}) copy-start(bf16[1296,1024]{1,0:T(8,128)(2,1)S(1)} %convolution_convert_fusion) | copy-start | bytes 7962628
  199.1 8.1 %copy-start.5 = (bf16[4,256,2048]{2,1,0:T(8,128)(2,1)S(1)}, bf16[4,256,2048]{2,1,0:T(8,128)(2,1)}, u32[]{:S(2)}) copy-start(bf16[4,256,2048]{2,1,0:T(8,128)(2,1)} %copy-done) | copy-start | bytes 12582916
  216.4 10.9 %copy-start.11 = (bf16[4,256,1024]{1,2,0:T(8,128)(2,1)S(1)}, bf16[4,256,1024]{1,2,0:T(8,128)(2,1)}, u32[]{:S(2)}) copy-start(bf16[4,256,1024]{1,2,0:T(8,128)(2,1)} %copy.182) | copy-start | bytes 6291460
  216.4 118.7 %reduce-scatter.7.cloned.1.call-start = ((), (), s32[]{:S(2)}) async-start(), calls=%async_computation.5 | async-start | bytes 4423680 | tf_op jit(solution)/shard_map/reduce_scatter | solution.py:323
  216.7 10.7 %copy-start.12 = (bf16[4,256,768]{1,2,0:T(8,128)(2,1)S(1)}, bf16[4,256,768]{1,2,0:T(8,128)(2,1)}, u32[]{:S(2)}) copy-start(bf16[4,256,768]{1,2,0:T(8,128)(2,1)} %copy.181) | copy-start | bytes 4718596
  228.0 45.9 %collective-permute-start.15 = (bf16[256,1920]{0,1:T(8,128)(2,1)S(1)}, bf16[256,1920]{0,1:T(8,128)(2,1)S(1)}, u32[]{:S(2)}, u32[]{:S(2)}) collective-permute-start(bf16[256,1920]{0,1:T(8,128)(2,1)S(1)} %get-tuple-element.48), channel_id=1, source_target_pairs={{0,24},{8,0},{16,8},{24,16},{1,25},{9,1},{17,9},{25,17},{2,26},{10... | collective-permute-start | bytes 2949128 | tf_op jit(solution)/shard_map/ppermute | solution.py:90
  228.9 45.1 %collective-permute-start.16 = (bf16[256,1920]{0,1:T(8,128)(2,1)S(1)}, bf16[256,1920]{0,1:T(8,128)(2,1)S(1)}, u32[]{:S(2)}, u32[]{:S(2)}) collective-permute-start(bf16[256,1920]{0,1:T(8,128)(2,1)S(1)} %get-tuple-element.47), channel_id=1, source_target_pairs={{0,16},{8,24},{16,0},{24,8},{1,17},{9,25},{17,1},{25,9},{2,18},{10... | collective-permute-start | bytes 2949128 | tf_op jit(solution)/shard_map/ppermute | solution.py:90
  230.0 44.5 %collective-permute-start.17 = (bf16[256,1920]{0,1:T(8,128)(2,1)S(1)}, bf16[256,1920]{0,1:T(8,128)(2,1)S(1)}, u32[]{:S(2)}, u32[]{:S(2)}) collective-permute-start(bf16[256,1920]{0,1:T(8,128)(2,1)S(1)} %get-tuple-element.45), channel_id=1, source_target_pairs={{0,8},{8,16},{16,24},{24,0},{1,9},{9,17},{17,25},{25,1},{2,10},{10... | collective-permute-start | bytes 2949128 | tf_op jit(solution)/shard_map/ppermute | solution.py:90
  283.3 5.5 %copy-start.19 = (bf16[8,128,1024]{2,1,0:T(8,128)(2,1)S(1)}, bf16[8,128,1024]{2,1,0:T(8,128)(2,1)}, u32[]{:S(2)}) copy-start(bf16[8,128,1024]{2,1,0:T(8,128)(2,1)} %slice.269) | copy-start | bytes 6291460
  283.3 5.5 %copy-start.30 = (bf16[1024,1024]{0,1:T(8,128)(2,1)S(1)}, bf16[1024,1024]{0,1:T(8,128)(2,1)}, u32[]{:S(2)}) copy-start(bf16[1024,1024]{0,1:T(8,128)(2,1)} %copy-done.29) | copy-start | bytes 6291460
  286.1 11.1 %collective-permute-start.11 = (bf16[128,1024]{1,0:T(8,128)(2,1)S(1)}, bf16[128,1024]{1,0:T(8,128)(2,1)S(1)}, u32[]{:S(2)}, u32[]{:S(2)}) collective-permute-start(bf16[128,1024]{1,0:T(8,128)(2,1)S(1)} %get-tuple-element.51), channel_id=1, source_target_pairs={{0,8},{8,16},{16,24},{24,0},{1,9},{9,17},{17,25},{25,1},{2,10},{10... | collective-permute-start | bytes 786440 | tf_op jit(solution)/shard_map/ppermute | solution.py:76
  288.8 9.2 %collective-permute-start.13 = (bf16[128,1024]{1,0:T(8,128)(2,1)S(1)}, bf16[128,1024]{1,0:T(8,128)(2,1)S(1)}, u32[]{:S(2)}, u32[]{:S(2)}) collective-permute-start(bf16[128,1024]{1,0:T(8,128)(2,1)S(1)} %get-tuple-element.52), channel_id=1, source_target_pairs={{0,24},{8,0},{16,8},{24,16},{1,25},{9,1},{17,9},{25,17},{2,26},{10... | collective-permute-start | bytes 786440 | tf_op jit(solution)/shard_map/ppermute | solution.py:77
  294.0 9.7 %collective-permute-start.7 = (bf16[128,1024]{1,0:T(8,128)(2,1)S(1)}, bf16[128,1024]{1,0:T(8,128)(2,1)S(1)}, u32[]{:S(2)}, u32[]{:S(2)}) collective-permute-start(bf16[128,1024]{1,0:T(8,128)(2,1)S(1)} %get-tuple-element.55), channel_id=1, source_target_pairs={{0,8},{8,16},{16,24},{24,0},{1,9},{9,17},{17,25},{25,1},{2,10},{10... | collective-permute-start | bytes 786440 | tf_op jit(solution)/shard_map/ppermute | solution.py:76
  297.2 10.6 %collective-permute-start.9 = (bf16[128,1024]{1,0:T(8,128)(2,1)S(1)}, bf16[128,1024]{1,0:T(8,128)(2,1)}, u32[]{:S(2)}, u32[]{:S(2)}) collective-permute-start(bf16[128,1024]{1,0:T(8,128)(2,1)S(1)} %get-tuple-element.56), channel_id=1, source_target_pairs={{0,24},{8,0},{16,8},{24,16},{1,25},{9,1},{17,9},{25,17},{2,26},{10... | collective-permute-start | bytes 786440 | tf_op jit(solution)/shard_map/ppermute | solution.py:77
  299.4 19.6 %collective-permute-start.14 = (bf16[256,1024]{1,0:T(8,128)(2,1)S(1)}, bf16[256,1024]{1,0:T(8,128)(2,1)S(1)}, u32[]{:S(2)}, u32[]{:S(2)}) collective-permute-start(bf16[256,1024]{1,0:T(8,128)(2,1)S(1)} %pad_maximum_fusion.13), channel_id=1, source_target_pairs={{0,24},{8,0},{16,8},{24,16},{1,25},{9,1},{17,9},{25,17},{2,26},{10... | collective-permute-start | bytes 1572872 | tf_op jit(solution)/shard_map/ppermute | solution.py:81
  300.3 18.6 %collective-permute-start.12 = (bf16[256,1024]{1,0:T(8,128)(2,1)}, bf16[256,1024]{1,0:T(8,128)(2,1)S(1)}, u32[]{:S(2)}, u32[]{:S(2)}) collective-permute-start(bf16[256,1024]{1,0:T(8,128)(2,1)} %pad_maximum_fusion.12), channel_id=1, source_target_pairs={{0,8},{8,16},{16,24},{24,0},{1,9},{9,17},{17,25},{25,1},{2,10},{10... | collective-permute-start | bytes 1572872 | tf_op jit(solution)/shard_map/ppermute | solution.py:80
  303.7 24.7 %copy-start.21 = (bf16[1,256,1024]{2,1,0:T(8,128)(2,1)S(1)}, bf16[1,256,1024]{2,1,0:T(8,128)(2,1)}, u32[]{:S(2)}) copy-start(bf16[1,256,1024]{2,1,0:T(8,128)(2,1)} %param.14) | copy-start | bytes 1572868
  310.0 18.4 %collective-permute-start.10 = (bf16[256,1024]{1,0:T(8,128)(2,1)}, bf16[256,1024]{1,0:T(8,128)(2,1)}, u32[]{:S(2)}, u32[]{:S(2)}) collective-permute-start(bf16[256,1024]{1,0:T(8,128)(2,1)} %pad_maximum_fusion.11), channel_id=1, source_target_pairs={{0,24},{8,0},{16,8},{24,16},{1,25},{9,1},{17,9},{25,17},{2,26},{10... | collective-permute-start | bytes 1572872 | tf_op jit(solution)/shard_map/ppermute | solution.py:81
  310.9 17.5 %collective-permute-start.8 = (bf16[256,1024]{1,0:T(8,128)(2,1)}, bf16[256,1024]{1,0:T(8,128)(2,1)}, u32[]{:S(2)}, u32[]{:S(2)}) collective-permute-start(bf16[256,1024]{1,0:T(8,128)(2,1)} %pad_maximum_fusion.10), channel_id=1, source_target_pairs={{0,8},{8,16},{16,24},{24,0},{1,9},{9,17},{17,25},{25,1},{2,10},{10... | collective-permute-start | bytes 1572872 | tf_op jit(solution)/shard_map/ppermute | solution.py:80
  318.9 16.2 %copy-start.23 = (bf16[1,256,1024]{2,1,0:T(8,128)(2,1)S(1)}, bf16[1,256,1024]{2,1,0:T(8,128)(2,1)}, u32[]{:S(2)}) copy-start(bf16[1,256,1024]{2,1,0:T(8,128)(2,1)} %param.25) | copy-start | bytes 1572868
  318.9 16.3 %slice-start.2 = ((f32[1024]{0:T(1024)}), f32[256]{0:T(256)S(1)}, s32[]{:S(2)}) async-start(f32[1024]{0:T(1024)} %copy-done.27), calls=%async_computation.8 | async-start | bytes 2048 | tf_op jit(solution)/shard_map/slice | solution.py:306
  321.0 10.2 %collective-permute-start.20 = (bf16[1,176,1024]{2,1,0:T(8,128)(2,1)}, bf16[1,176,1024]{2,1,0:T(8,128)(2,1)S(1)}, u32[]{:S(2)}, u32[]{:S(2)}) collective-permute-start(bf16[1,176,1024]{2,1,0:T(8,128)(2,1)} %reduce-scatter.5.cloned.1.call-done), channel_id=1, source_target_pairs={{0,32},{32,0},{64,96},{96,64},{1,33},{33,1},{65,97},{97,65},{2,34}... | collective-permute-start | bytes 1081352 | tf_op jit(solution)/shard_map/ppermute | solution.py:103
  332.2 10.1 %collective-permute-start.21 = (bf16[1,176,1024]{2,1,0:T(8,128)(2,1)S(1)}, bf16[1,176,1024]{2,1,0:T(8,128)(2,1)S(1)}, u32[]{:S(2)}, u32[]{:S(2)}) collective-permute-start(bf16[1,176,1024]{2,1,0:T(8,128)(2,1)S(1)} %add_convert_fusion.3), channel_id=1, source_target_pairs={{0,64},{32,96},{64,0},{96,32},{1,65},{33,97},{65,1},{97,33},{2,66}... | collective-permute-start | bytes 1081352 | tf_op jit(solution)/shard_map/ppermute | solution.py:105
  335.2 7.9 %copy-start.26 = (bf16[32,7680]{1,0:T(8,128)(2,1)S(1)}, bf16[32,7680]{1,0:T(8,128)(2,1)}, u32[]{:S(2)}) copy-start(bf16[32,7680]{1,0:T(8,128)(2,1)} %reduce-scatter.7.cloned.1.call-done) | copy-start | bytes 1474564
  335.2 7.9 %collective-permute-start.18 = (bf16[32,7680]{1,0:T(8,128)(2,1)}, bf16[32,7680]{1,0:T(8,128)(2,1)S(1)}, u32[]{:S(2)}, u32[]{:S(2)}) collective-permute-start(bf16[32,7680]{1,0:T(8,128)(2,1)} %reduce-scatter.7.cloned.1.call-done), channel_id=1, source_target_pairs={{0,32},{32,0},{64,96},{96,64},{1,33},{33,1},{65,97},{97,65},{2,34}... | collective-permute-start | bytes 1474568 | tf_op jit(solution)/shard_map/ppermute | solution.py:103
  343.2 12.0 %collective-permute-start.19 = (bf16[32,7680]{1,0:T(8,128)(2,1)S(1)}, bf16[32,7680]{1,0:T(8,128)(2,1)S(1)}, u32[]{:S(2)}, u32[]{:S(2)}) collective-permute-start(bf16[32,7680]{1,0:T(8,128)(2,1)S(1)} %add_convert_fusion.2), channel_id=1, source_target_pairs={{0,64},{32,96},{64,0},{96,32},{1,65},{33,97},{65,1},{97,33},{2,66}... | collective-permute-start | bytes 1474568 | tf_op jit(solution)/shard_map/ppermute | solution.py:105
  (12 other events, 27.9 us)
Sparse Core Ops, SparseCore 0:
  10.2 45.1 all-gather.6
  57.0 49.5 all-gather.4
  216.6 44.1 reduce-scatter.4
  283.4 49.2 reduce-scatter.6

commit v7 on v5

--- a/solution.py
+++ b/solution.py
@@ -220,20 +220,38 @@
     small = jnp.broadcast_to(small[None], (nc,) + small.shape)
     column_payload = jnp.concatenate([triple_cols, inner_cols, small], -1)
     column_payload = ring_all_to_all(column_payload, "ctx")
-    column_block = lax.all_gather(column_payload, "fsdp", axis=0, tiled=False)
-    column_block = column_block.swapaxes(0, 1).reshape(nc * nf * shard_rows, -1)
-    triple_here = column_block[:, : 3 * head_cols]
-    inner_here = column_block[:, 3 * head_cols : 3 * head_cols + ff_here]
-    gain = column_block[:, 3 * head_cols + ff_here].astype(f32)
-    shift = column_block[:, 3 * head_cols + ff_here + 1].astype(f32)
-    obias = column_block[:, 3 * head_cols + ff_here + 2].astype(f32)
+    split = 3 * head_cols
 
     bias_rows = jnp.pad(inner_bias[None], ((0, 15), (0, width - inner_bias.shape[0])))
-    row_payload = jnp.concatenate([mixer_weight, outer_weight, bias_rows], 0)
-    row_block = lax.all_gather(row_payload, "fsdp", axis=0, tiled=False)
-    mixer_here = row_block[:, :shard_rows].reshape(nf * shard_rows, width)
-    outer_here = row_block[:, shard_rows : shard_rows + ff_rows].reshape(nf * ff_rows, width)
-    ibias_here = row_block[:, shard_rows + ff_rows, : inner_bias.shape[0]].reshape(-1).astype(f32)
+    triple_payload = jnp.concatenate([column_payload[..., :split], column_payload[..., split + ff_here :]], -1)
+    pieces = (triple_payload, mixer_weight, bias_rows)
+    first_payload = jnp.concatenate([piece.reshape(-1) for piece in pieces]).reshape(-1, width)
+    first_block = lax.all_gather(first_payload, "fsdp", axis=0, tiled=False).reshape(nf, -1)
+    sizes = [piece.size for piece in pieces]
+    triple_block = first_block[:, : sizes[0]].reshape((nf,) + triple_payload.shape)
+    triple_block = triple_block.swapaxes(0, 1).reshape(nc * nf * shard_rows, -1)
+    mixer_here = first_block[:, sizes[0] : sizes[0] + sizes[1]].reshape(nf * shard_rows, width)
+    ibias_here = (
+        first_block[:, sizes[0] + sizes[1] : sizes[0] + sizes[1] + inner_bias.shape[0]].reshape(-1).astype(f32)
+    )
+
+    ff_payload = jnp.concatenate(
+        [column_payload[..., split : split + ff_here].reshape(nc * shard_rows, ff_here), outer_weight], 0
+    )
+    ff_payload, triple_block = lax.optimization_barrier((ff_payload, triple_block))
+    ff_block = lax.all_gather(ff_payload, "fsdp", axis=0, tiled=False)
+    inner_here = (
+        ff_block[:, : nc * shard_rows]
+        .reshape(nf, nc, shard_rows, ff_here)
+        .swapaxes(0, 1)
+        .reshape(nc * nf * shard_rows, ff_here)
+    )
+    outer_here = ff_block[:, nc * shard_rows :].reshape(nf * ff_rows, width)
+
+    triple_here = triple_block[:, :split]
+    gain = triple_block[:, split].astype(f32)
+    shift = triple_block[:, split + 1].astype(f32)
+    obias = triple_block[:, split + 2].astype(f32)
 
     visible = (pad_mask[0] != 0).astype(f32)
     own_upstream = cotangent[0].astype(f32) * visible

time: 333 us -> 364 us (1.093)
  waiting for transfers between devices: 119 us -> 131 us
  local copies, waits for them, and re-layouts: 53.1 us -> 61.6 us
  other arithmetic: 32.9 us -> 39 us
    all_gather x2, waiting for transfers between devices: 21.4 us -> 41.5 us  [the longest x1 41.5 us: local(): lax.all_gather(first_payload, 'fsdp', axis=0, tiled=False).reshape(nf, -1)]
    ppermute x1, waiting for transfers between devices: 8.82 us -> 3.56 us  [ring_gather(): far_second = lax.ppermute(from_right[half:], axis, ring_pairs(n, -1))]
    unnamed x75 -> x104, local copies, waits for them, and re-layouts: 13.9 us -> 19 us
    ppermute x2, waiting for transfers between devices: 13 us -> 8.58 us  [ring_scatter(): from_right = lax.ppermute(to_left.astype(wire), axis, ring_pairs(n, -1))]
    slice x4, local copies, waits for them, and re-layouts: 1.58 us -> 5.45 us  [rotate(): paired = field[..., :ROT].reshape(leading + (ROT // 2, 2))]
  transfers between devices with their start and end apart: 26 -> 26, of which waited for: 17 -> 17; matrix products, arithmetic and copies ran while one was open for 23% -> 29% of each run, Pallas kernels for 0% -> 9%
where the time goes in v7:
time: 364 us; the launch traced here: 358 us
  waiting for transfers between devices  131 us (36%)
  local copies, waits for them, and re-layouts  61.6 us (17%)
  matrix products  44.9 us (12%)
  other arithmetic  39 us (11%)
  starting transfers between devices  33.6 us (9%)
  Pallas kernels  31 us (9%)
  between operations  16.4 us (5%)
    all_gather x1, waiting for transfers between devices, local(): lax.all_gather(first_payload, 'fsdp', axis=0, tiled=False).reshape(nf, -1)  41.5 us
    pallas_call x1, Pallas kernels, fused_attention(): pl.pallas_call(attention_kernel, out_shape=(jax.ShapeDtypeStruct((heads,...  31 us
    unnamed x104, local copies, waits for them, and re-layouts  19 us
    ppermute x1, waiting for transfers between devices, ring_gather(): from_right = lax.ppermute(block, axis, ring_pairs(n, -1))  18.8 us
    reduce_scatter x1, waiting for transfers between devices, local(): lax.psum_scatter(column_grads, 'fsdp', scatter_dimension=0, tiled=True)  18.3 us
    ppermute x2, waiting for transfers between devices, replica_sum(): lax.ppermute(pair, axis, [(i, i ^ 2) for i in range(n)]).astype(f32)  17.4 us
    ppermute x6, waiting for transfers between devices, ring_all_to_all(): lax.ppermute(pick(me + s), axis, ring_pairs(n, s))  12.5 us
    ppermute x6, starting transfers between devices, ring_all_to_all(): lax.ppermute(pick(me + s), axis, ring_pairs(n, s))  10.5 us
  transfers between devices with their start and end apart: 26, of which 17 were waited for; matrix products, arithmetic and copies ran while one was open for 29% of the time, Pallas kernels for 9%

profile of v7, /device:TPU:0, one launch (start us, length us, event | category | flops | bytes accessed | tf_op | source)
XLA Modules:
  0.0 357.5 jit_solution(12449889190332190239)
XLA Ops:
  10.7 3.2 collective-permute-start.4
  13.9 2.2 collective-permute-start.5
  16.4 5.1 %collective-permute-done.5 = bf16[32,1920]{1,0:T(8,128)(2,1)S(1)} collective-permute-done((bf16[32,1920]{1,0:T(8,128)(2,1)S(1)}, bf16[32,1920]{1,0:T(8,128)(2,1)S(1)}, u32[]{:S(2)}, u32[]{:S(2)}) %collective-permute-start.5) | collective-permute-done | bytes 122912 | tf_op jit(solution)/shard_map/ppermute | solution.py:90
  24.8 41.5 %all-gather.4.cloned.1.call-done = bf16[8,160,1024]{2,1,0:T(8,128)(2,1)} async-done(((bf16[1,160,1024]{2,1,0:T(8,128)(2,1)}), bf16[8,160,1024]{2,1,0:T(8,128)(2,1)}) %all-gather.4.cloned.1.call-update) | async-done | bytes 2621456 | tf_op jit(solution)/shard_map/all_gather | solution.py:229
  66.2 3.2 copy.168
  74.1 2.7 collective-permute-start
  77.5 18.8 %collective-permute-done = bf16[256,2048]{1,0:T(8,128)(2,1)S(1)} collective-permute-done((bf16[256,2048]{1,0:T(8,128)(2,1)S(1)}, bf16[256,2048]{1,0:T(8,128)(2,1)S(1)}, u32[]{:S(2)}, u32[]{:S(2)}) %collective-permute-start) | collective-permute-done | bytes 1048608 | tf_op jit(solution)/shard_map/ppermute | solution.py:65
  97.3 3.8 %collective-permute-start.3 = (bf16[128,2048]{1,0:T(8,128)(2,1)S(1)}, bf16[128,2048]{1,0:T(8,128)(2,1)}, u32[]{:S(2)}, u32[]{:S(2)}) collective-permute-start(bf16[128,2048]{1,0:T(8,128)(2,1)S(1)} %slice.265), channel_id=1, source_target_pairs={{0,24},{8,0},{16,8},{24,16},{1,25},{9,1},{17,9},{25,17},{2,26},{10... | collective-permute-start | bytes 1572872 | tf_op jit(solution)/shard_map/ppermute | solution.py:67
  104.9 3.6 collective-permute-done.3
  108.5 5.5 %collective-permute-done.2 = bf16[128,2048]{1,0:T(8,128)(2,1)} collective-permute-done((bf16[128,2048]{1,0:T(8,128)(2,1)}, bf16[128,2048]{1,0:T(8,128)(2,1)}, u32[]{:S(2)}, u32[]{:S(2)}) %collective-permute-start.2) | collective-permute-done | bytes 524320 | tf_op jit(solution)/shard_map/ppermute | solution.py:66
  115.3 2.3 pad_maximum_fusion
  121.0 2.2 fusion.25
  127.5 3.3 fusion.28
  130.8 2.4 copy.142
  135.6 2.2 copy.138
  137.8 2.4 copy.141
  148.4 3.0 copy.160
  151.4 3.3 maximum_bitcast_fusion.1.k_ref
  154.6 3.2 fusion.31.q_ref
  157.8 31.0 %shard_map.195 = (bf16[4,1024,64]{2,1,0:T(8,128)(2,1)}, f32[4,1024,64]{2,1,0:T(8,128)}, f32[4,1024,64]{2,1,0:T(8,128)}, f32[4,1024,64]{2,1,0:T(8,128)}) custom-call(s32[1]{0:T(128)S(6)} %copy.194.span_ref, bf16[4,1024,64]{2,1,0:T(8,128)(2,1)} %fusion.31.q_ref, bf16[4,1024,64]{2,1,0:T(8,128)(2,1)} %maximum_bitcast_fusion.1.k_ref, ...), custom_call_target="tpu_custom_call" | custom-call | flops 3221225472 | bytes 5767168 | tf_op jit(solution)/shard_map/pallas_call | solution.py:158
  190.4 2.9 fusion.82
  193.6 3.4 copy-done.1
  197.0 3.9 %multiply_convert_fusion = (bf16[1024,1024]{0,1:T(8,128)(2,1)S(1)}, f32[1024,1024]{0,1:T(8,128)S(1)}) fusion(f32[1024]{0:T(1024)S(1)} %fusion.60, bf16[1024,1024]{1,0:T(8,128)(2,1)S(1)} %bitcast.226, f32[1024]{0:T(1024)S(1)} %copy-done.35, f32[1024]{0:T(1024)S(1)} %copy-done.30, f32[1024]{0:T(1024)S(1)} %add_rsqrt_fusion, ...), kind=kOutput, calls=%fused_computation.16 | convolution fusion | flops 2164260864 | bytes 10506240 | tf_op jit(solution)/shard_map/dot_general | solution.py:293
  201.0 4.0 %convolution_convert_fusion = bf16[1296,1024]{1,0:T(8,128)(2,1)S(1)} fusion(bf16[1024,1024]{0,1:T(8,128)(2,1)S(1)} %get-tuple-element.85, bf16[1024,256]{0,1:T(8,128)(2,1)S(1)} %bitcast.243, bf16[1024,2048]{1,0:T(8,128)(2,1)S(1)} %bitcast.212, bf16[1296]{0:T(1024)(128)(2,1)S(1)} %copy-done.36), kind=kOutput, calls=%fused_computation.19 | convolution fusion | flops 2727198720 | bytes 7376896 | tf_op jit(solution)/shard_map/dot_general | solution.py:301
  205.3 6.4 %fusion.85 = (bf16[1024]{0:T(1024)(128)(2,1)S(1)}, bf16[1024,1024]{0,1:T(8,128)(2,1)}) fusion(f32[1024,1024]{0,1:T(8,128)S(1)} %get-tuple-element.86, f32[1024]{0:T(1024)S(1)} %fusion.60, bf16[1024,1024]{1,0:T(8,128)(2,1)S(1)} %bitcast.251, bf16[1024,2048]{1,0:T(8,128)(2,1)S(1)} %bitcast.213), kind=kOutput, calls=%fused_computation.206 | convolution fusion | flops 2170551296 | bytes 10491904 | tf_op jit(solution)/shard_map/dot_general | solution.py:302
  214.4 2.7 fusion.52
  219.2 4.0 %multiply_bitcast_fusion = (f32[1024,4,64]{2,0,1:T(8,128)}, bf16[1024,4,64]{2,0,1:T(8,128)(2,1)S(1)}) fusion(f32[4,1024,64]{2,1,0:T(8,128)} %get-tuple-element.31, f32[4,1024,64]{2,1,0:T(8,128)} %get-tuple-element.33), kind=kLoop, calls=%fused_computation.30 | loop fusion | flops 524288 | bytes 3670016 | tf_op jit(solution)/shard_map/mul | solution.py:310
  232.5 3.6 %convolution_convert_fusion.2 = bf16[1024,768]{1,0:T(8,128)(2,1)} fusion(bf16[1024,256]{0,1:T(8,128)(2,1)S(1)} %bitcast.266, bf16[1024,512]{0,1:T(8,128)(2,1)S(1)} %subtract_convert_fusion, f32[1024]{0:T(1024)S(1)} %copy-done.35, f32[1024]{0:T(1024)S(1)} %copy-done.30, f32[1024]{0:T(1024)S(1)} %add_rsqrt_fusion, f32[1024]{0:T(1024)S(1)} %broadcast_multiply_fusion, ...), kind=kOutput, calls=%fused_computation.34 | convolution fusion | flops 1620836352 | bytes 5259264 | tf_op jit(solution)/shard_map/dot_general | solution.py:316
  236.1 5.6 %multiply_reduce_fusion = (bf16[1024]{0:T(1024)(128)(2,1)S(1)}, bf16[1024]{0:T(1024)(128)(2,1)S(1)}, f32[1024,1024]{1,0:T(8,128)}, f32[1024,1024]{1,0:T(8,128)}) fusion(f32[1024]{0:T(1024)S(1)} %add_rsqrt_fusion, f32[1024]{0:T(1024)S(1)} %broadcast_multiply_fusion, bf16[1024,2048]{1,0:T(8,128)(2,1)S(1)} %bitcast.215, f32[1024,1024]{1,0:T(8,128)S(1)} %fusion.23, ...), kind=kOutput, calls=%fused_computation.15 | convolution fusion | flops 2154821632 | bytes 18886656 | tf_op jit(solution)/shard_map/dot_general | solution.py:318
  242.0 4.4 %convolution_convert_fusion.1 = bf16[1024,1024]{1,0:T(8,128)(2,1)S(1)} fusion(bf16[1024,1024]{0,1:T(8,128)(2,1)S(1)} %copy-done.13, f32[1024]{0:T(1024)S(1)} %copy-done.35, f32[1024]{0:T(1024)S(1)} %copy-done.30, f32[1024]{0:T(1024)S(1)} %add_rsqrt_fusion, f32[1024]{0:T(1024)S(1)} %broadcast_multiply_fusion, bf16[1024,2048]{1,0:T(8,128)(2,1)} %bitcast.210), kind=kOutput, calls=%fused_computation.32 | convolution fusion | flops 2154823680 | bytes 6307840 | tf_op jit(solution)/shard_map/dot_general | solution.py:305
  246.8 2.3 copy.159
  249.2 2.7 convert.90
  252.1 3.2 collective-permute-start.13
  255.3 2.4 fusion.86
  260.5 3.2 collective-permute-start.9
  267.3 3.6 %collective-permute-done.7 = bf16[128,1024]{1,0:T(8,128)(2,1)S(1)} collective-permute-done((bf16[128,1024]{1,0:T(8,128)(2,1)S(1)}, bf16[128,1024]{1,0:T(8,128)(2,1)S(1)}, u32[]{:S(2)}, u32[]{:S(2)}) %collective-permute-start.7) | collective-permute-done | bytes 262176 | tf_op jit(solution)/shard_map/ppermute | solution.py:76
  272.4 3.4 collective-permute-start.10
  276.2 5.5 %collective-permute-done.14 = bf16[256,1024]{1,0:T(8,128)(2,1)S(1)} collective-permute-done((bf16[256,1024]{1,0:T(8,128)(2,1)S(1)}, bf16[256,1024]{1,0:T(8,128)(2,1)S(1)}, u32[]{:S(2)}, u32[]{:S(2)}) %collective-permute-start.14) | collective-permute-done | bytes 524320 | tf_op jit(solution)/shard_map/ppermute | solution.py:81
  284.1 3.1 collective-permute-done.10
  288.0 2.4 fusion.40
  290.4 18.3 %reduce-scatter.3.cloned.1.call-done = bf16[128,1920]{1,0:T(8,128)(2,1)} async-done(((bf16[1024,1920]{1,0:T(8,128)(2,1)}), bf16[128,1920]{1,0:T(8,128)(2,1)}) %reduce-scatter.3.cloned.1.call-update) | async-done | bytes 491536 | tf_op jit(solution)/shard_map/reduce_scatter | solution.py:339
  308.6 2.4 fusion.39
  312.1 2.9 collective-permute-start.21
  315.9 9.0 %collective-permute-done.21 = bf16[1,176,1024]{2,1,0:T(8,128)(2,1)S(1)} collective-permute-done((bf16[1,176,1024]{2,1,0:T(8,128)(2,1)S(1)}, bf16[1,176,1024]{2,1,0:T(8,128)(2,1)S(1)}, u32[]{:S(2)}, u32[]{:S(2)}) %collective-permute-start.21) | collective-permute-done | bytes 360480 | tf_op jit(solution)/shard_map/ppermute | solution.py:105
  326.6 8.4 %collective-permute-done.16 = bf16[128,1920]{1,0:T(8,128)(2,1)S(1)} collective-permute-done((bf16[128,1920]{1,0:T(8,128)(2,1)S(1)}, bf16[128,1920]{1,0:T(8,128)(2,1)S(1)}, u32[]{:S(2)}, u32[]{:S(2)}) %collective-permute-start.16) | collective-permute-done | bytes 491552 | tf_op jit(solution)/shard_map/ppermute | solution.py:105
  335.2 2.8 collective-permute-start.17
  339.1 2.3 collective-permute-start.18
  341.4 5.3 %collective-permute-done.18 = bf16[32,1920]{1,0:T(8,128)(2,1)S(1)} collective-permute-done((bf16[32,1920]{1,0:T(8,128)(2,1)S(1)}, bf16[32,1920]{1,0:T(8,128)(2,1)S(1)}, u32[]{:S(2)}, u32[]{:S(2)}) %collective-permute-start.18) | collective-permute-done | bytes 122912 | tf_op jit(solution)/shard_map/ppermute | solution.py:90
  (242 shorter events, 72.3 us)
Async XLA Ops:
  7.2 8.9 %copy-start.37 = (bf16[128]{0:T(256)(128)(2,1)S(1)}, bf16[128]{0:T(256)(128)(2,1)}, u32[]{:S(2)}) copy-start(bf16[128]{0:T(256)(128)(2,1)} %param.20) | copy-start | bytes 772
  7.2 8.9 %copy-start.27 = (bf16[32,1024]{1,0:T(8,128)(2,1)S(1)}, bf16[32,1024]{1,0:T(8,128)(2,1)}, u32[]{:S(2)}) copy-start(bf16[32,1024]{1,0:T(8,128)(2,1)} %param.18) | copy-start | bytes 196612
  7.2 59.1 %all-gather.4.cloned.1.call-start = ((), (), s32[]{:S(2)}) async-start(), calls=%async_computation.2 | async-start | bytes 2949120 | tf_op jit(solution)/shard_map/all_gather | solution.py:229
  9.5 14.4 %copy-start.26 = (bf16[128,1024]{1,0:T(8,128)(2,1)S(1)}, bf16[128,1024]{1,0:T(8,128)(2,1)}, u32[]{:S(2)}) copy-start(bf16[128,1024]{1,0:T(8,128)(2,1)} %param.21) | copy-start | bytes 786436
  10.7 5.7 %collective-permute-start.4 = (bf16[32,1920]{1,0:T(8,128)(2,1)S(1)}, bf16[32,1920]{1,0:T(8,128)(2,1)S(1)}, u32[]{:S(2)}, u32[]{:S(2)}) collective-permute-start(bf16[32,1920]{1,0:T(8,128)(2,1)S(1)} %get-tuple-element.78), channel_id=1, source_target_pairs={{0,24},{8,0},{16,8},{24,16},{1,25},{9,1},{17,9},{25,17},{2,26},{10... | collective-permute-start | bytes 368648 | tf_op jit(solution)/shard_map/ppermute | solution.py:90
  13.8 8.6 %collective-permute-start.6 = (bf16[32,1920]{1,0:T(8,128)(2,1)S(1)}, bf16[32,1920]{1,0:T(8,128)(2,1)S(1)}, u32[]{:S(2)}, u32[]{:S(2)}) collective-permute-start(bf16[32,1920]{1,0:T(8,128)(2,1)S(1)} %get-tuple-element.75), channel_id=1, source_target_pairs={{0,8},{8,16},{16,24},{24,0},{1,9},{9,17},{17,25},{25,1},{2,10},{10... | collective-permute-start | bytes 368648 | tf_op jit(solution)/shard_map/ppermute | solution.py:90
  13.9 7.7 %collective-permute-start.5 = (bf16[32,1920]{1,0:T(8,128)(2,1)S(1)}, bf16[32,1920]{1,0:T(8,128)(2,1)S(1)}, u32[]{:S(2)}, u32[]{:S(2)}) collective-permute-start(bf16[32,1920]{1,0:T(8,128)(2,1)S(1)} %get-tuple-element.77), channel_id=1, source_target_pairs={{0,16},{8,24},{16,0},{24,8},{1,17},{9,25},{17,1},{25,9},{2,18},{10... | collective-permute-start | bytes 368648 | tf_op jit(solution)/shard_map/ppermute | solution.py:90
  23.8 166.6 %all-gather.6.cloned.1.call-start = ((), (), s32[]{:S(2)}) async-start(), calls=%async_computation.5 | async-start | bytes 4718592 | tf_op jit(solution)/shard_map/all_gather | solution.py:242
  71.1 219.3 %reduce-scatter.5.cloned.1.call-start = ((), (), s32[]{:S(2)}) async-start(), calls=%async_computation.4 | async-start | bytes 3244032 | tf_op jit(solution)/shard_map/reduce_scatter | solution.py:364
  74.1 22.2 %collective-permute-start = (bf16[256,2048]{1,0:T(8,128)(2,1)S(1)}, bf16[256,2048]{1,0:T(8,128)(2,1)S(1)}, u32[]{:S(2)}, u32[]{:S(2)}) collective-permute-start(bf16[256,2048]{1,0:T(8,128)(2,1)S(1)} %get-tuple-element.64), channel_id=1, source_target_pairs={{0,24},{8,0},{16,8},{24,16},{1,25},{9,1},{17,9},{25,17},{2,26},{10... | collective-permute-start | bytes 3145736 | tf_op jit(solution)/shard_map/ppermute | solution.py:65
  76.8 24.3 %collective-permute-start.1 = (bf16[256,2048]{1,0:T(8,128)(2,1)S(1)}, bf16[256,2048]{1,0:T(8,128)(2,1)S(1)}, u32[]{:S(2)}, u32[]{:S(2)}) collective-permute-start(bf16[256,2048]{1,0:T(8,128)(2,1)S(1)} %get-tuple-element.64), channel_id=1, source_target_pairs={{0,8},{8,16},{16,24},{24,0},{1,9},{9,17},{17,25},{25,1},{2,10},{10... | collective-permute-start | bytes 3145736 | tf_op jit(solution)/shard_map/ppermute | solution.py:64
  97.3 11.2 %collective-permute-start.3 = (bf16[128,2048]{1,0:T(8,128)(2,1)S(1)}, bf16[128,2048]{1,0:T(8,128)(2,1)}, u32[]{:S(2)}, u32[]{:S(2)}) collective-permute-start(bf16[128,2048]{1,0:T(8,128)(2,1)S(1)} %slice.265), channel_id=1, source_target_pairs={{0,24},{8,0},{16,8},{24,16},{1,25},{9,1},{17,9},{25,17},{2,26},{10... | collective-permute-start | bytes 1572872 | tf_op jit(solution)/shard_map/ppermute | solution.py:67
  102.9 11.2 %collective-permute-start.2 = (bf16[128,2048]{1,0:T(8,128)(2,1)}, bf16[128,2048]{1,0:T(8,128)(2,1)}, u32[]{:S(2)}, u32[]{:S(2)}) collective-permute-start(bf16[128,2048]{1,0:T(8,128)(2,1)} %slice.264), channel_id=1, source_target_pairs={{0,8},{8,16},{16,24},{24,0},{1,9},{9,17},{17,25},{25,1},{2,10},{10... | collective-permute-start | bytes 1572872 | tf_op jit(solution)/shard_map/ppermute | solution.py:66
  103.0 14.7 %copy-start.31 = (s32[1,1,4,256]{3,1,2,0:T(1,128)}, s32[1,1,4,256]{3,1,2,0:T(1,128)S(1)}, u32[]{:S(2)}) copy-start(s32[1,1,4,256]{3,1,2,0:T(1,128)S(1)} %copy.171) | copy-start | bytes 12292
  104.6 13.1 %copy-start.32 = (f32[16]{0:T(128)}, f32[16]{0:T(128)S(1)}, u32[]{:S(2)}) copy-start(f32[16]{0:T(128)S(1)} %multiply_power_fusion) | copy-start | bytes 196
  117.7 5.6 %copy-start = (bf16[4,256,2048]{2,1,0:T(8,128)(2,1)}, bf16[4,256,2048]{2,1,0:T(8,128)(2,1)S(1)}, u32[]{:S(2)}) copy-start(bf16[4,256,2048]{2,1,0:T(8,128)(2,1)S(1)} %pad_maximum_fusion) | copy-start | bytes 12582916
  118.8 148.6 %copy-start.28 = (f32[1024]{0:T(1024)}, f32[1024]{0:T(1024)S(1)}, u32[]{:S(2)}) copy-start(f32[1024]{0:T(1024)S(1)} %add_rsqrt_fusion) | copy-start | bytes 12292
  127.5 7.8 %copy-start.16 = (bf16[256,1024]{1,0:T(8,128)(2,1)}, bf16[256,1024]{1,0:T(8,128)(2,1)S(1)}, u32[]{:S(2)}) copy-start(bf16[256,1024]{1,0:T(8,128)(2,1)S(1)} %reshape.482) | copy-start | bytes 1572868
  190.3 10.6 %copy-start.14 = (bf16[1024,4,64]{0,2,1:T(8,128)(2,1)}, bf16[1024,4,64]{0,2,1:T(8,128)(2,1)S(1)}, u32[]{:S(2)}) copy-start(bf16[1024,4,64]{0,2,1:T(8,128)(2,1)S(1)} %copy.144) | copy-start | bytes 1572868
  193.3 12.0 %copy-start.18 = (bf16[8,128,1024]{2,1,0:T(8,128)(2,1)}, bf16[8,128,1024]{2,1,0:T(8,128)(2,1)S(1)}, u32[]{:S(2)}) copy-start(bf16[8,128,1024]{2,1,0:T(8,128)(2,1)S(1)} %get-tuple-element.49) | copy-start | bytes 6291460
  193.6 7.3 %copy-start.5 = (bf16[4,8,32,1024]{3,2,1,0:T(8,128)(2,1)}, bf16[4,8,32,1024]{3,2,1,0:T(8,128)(2,1)S(1)}, u32[]{:S(2)}) copy-start(bf16[4,8,32,1024]{3,2,1,0:T(8,128)(2,1)S(1)} %copy.145) | copy-start | bytes 6291460
  197.0 3.9 %copy-start.36 = (bf16[1296]{0:T(1024)(128)(2,1)S(1)}, bf16[1296]{0:T(1024)(128)(2,1)}, u32[]{:S(2)}) copy-start(bf16[1296]{0:T(1024)(128)(2,1)} %pad.25.clone) | copy-start | bytes 7780
  200.9 4.1 %copy-start.38 = (bf16[1024,1024]{0,1:T(8,128)(2,1)}, bf16[1024,1024]{0,1:T(8,128)(2,1)S(1)}, u32[]{:S(2)}) copy-start(bf16[1024,1024]{0,1:T(8,128)(2,1)S(1)} %get-tuple-element.85) | copy-start | bytes 6291460
  213.8 94.8 %reduce-scatter.3.cloned.1.call-start = ((), (), s32[]{:S(2)}) async-start(), calls=%async_computation.3 | async-start | bytes 4423680 | tf_op jit(solution)/shard_map/reduce_scatter | solution.py:339
  242.0 4.5 %copy-start.23 = (bf16[1024,768]{1,0:T(8,128)(2,1)S(1)}, bf16[1024,768]{1,0:T(8,128)(2,1)}, u32[]{:S(2)}) copy-start(bf16[1024,768]{1,0:T(8,128)(2,1)} %convolution_convert_fusion.2) | copy-start | bytes 4718596
  249.1 6.1 %copy-start.19 = (bf16[8,128,1024]{2,1,0:T(8,128)(2,1)S(1)}, bf16[8,128,1024]{2,1,0:T(8,128)(2,1)}, u32[]{:S(2)}) copy-start(bf16[8,128,1024]{2,1,0:T(8,128)(2,1)} %copy-done.18) | copy-start | bytes 6291460
  249.2 6.1 %copy-start.39 = (bf16[1024,1024]{0,1:T(8,128)(2,1)S(1)}, bf16[1024,1024]{0,1:T(8,128)(2,1)}, u32[]{:S(2)}) copy-start(bf16[1024,1024]{0,1:T(8,128)(2,1)} %copy-done.38) | copy-start | bytes 6291460
  252.0 11.8 %collective-permute-start.11 = (bf16[128,1024]{1,0:T(8,128)(2,1)S(1)}, bf16[128,1024]{1,0:T(8,128)(2,1)S(1)}, u32[]{:S(2)}, u32[]{:S(2)}) collective-permute-start(bf16[128,1024]{1,0:T(8,128)(2,1)S(1)} %get-tuple-element.53), channel_id=1, source_target_pairs={{0,8},{8,16},{16,24},{24,0},{1,9},{9,17},{17,25},{25,1},{2,10},{10... | collective-permute-start | bytes 786440 | tf_op jit(solution)/shard_map/ppermute | solution.py:76
  252.0 5.7 %copy-start.15 = (bf16[1024,4,64]{0,2,1:T(8,128)(2,1)S(1)}, bf16[1024,4,64]{0,2,1:T(8,128)(2,1)}, u32[]{:S(2)}) copy-start(bf16[1024,4,64]{0,2,1:T(8,128)(2,1)} %copy-done.14) | copy-start | bytes 1572868
  252.0 5.7 %copy-start.17 = (bf16[256,1024]{1,0:T(8,128)(2,1)S(1)}, bf16[256,1024]{1,0:T(8,128)(2,1)}, u32[]{:S(2)}) copy-start(bf16[256,1024]{1,0:T(8,128)(2,1)} %copy-done.16) | copy-start | bytes 1572868
  252.1 11.7 %collective-permute-start.13 = (bf16[128,1024]{1,0:T(8,128)(2,1)S(1)}, bf16[128,1024]{1,0:T(8,128)(2,1)S(1)}, u32[]{:S(2)}, u32[]{:S(2)}) collective-permute-start(bf16[128,1024]{1,0:T(8,128)(2,1)S(1)} %get-tuple-element.54), channel_id=1, source_target_pairs={{0,24},{8,0},{16,8},{24,16},{1,25},{9,1},{17,9},{25,17},{2,26},{10... | collective-permute-start | bytes 786440 | tf_op jit(solution)/shard_map/ppermute | solution.py:77
  260.5 10.5 %collective-permute-start.7 = (bf16[128,1024]{1,0:T(8,128)(2,1)S(1)}, bf16[128,1024]{1,0:T(8,128)(2,1)S(1)}, u32[]{:S(2)}, u32[]{:S(2)}) collective-permute-start(bf16[128,1024]{1,0:T(8,128)(2,1)S(1)} %get-tuple-element.57), channel_id=1, source_target_pairs={{0,8},{8,16},{16,24},{24,0},{1,9},{9,17},{17,25},{25,1},{2,10},{10... | collective-permute-start | bytes 786440 | tf_op jit(solution)/shard_map/ppermute | solution.py:76
  260.5 10.5 %collective-permute-start.9 = (bf16[128,1024]{1,0:T(8,128)(2,1)S(1)}, bf16[128,1024]{1,0:T(8,128)(2,1)}, u32[]{:S(2)}, u32[]{:S(2)}) collective-permute-start(bf16[128,1024]{1,0:T(8,128)(2,1)S(1)} %get-tuple-element.58), channel_id=1, source_target_pairs={{0,24},{8,0},{16,8},{24,16},{1,25},{9,1},{17,9},{25,17},{2,26},{10... | collective-permute-start | bytes 786440 | tf_op jit(solution)/shard_map/ppermute | solution.py:77
  265.1 16.5 %collective-permute-start.14 = (bf16[256,1024]{1,0:T(8,128)(2,1)S(1)}, bf16[256,1024]{1,0:T(8,128)(2,1)S(1)}, u32[]{:S(2)}, u32[]{:S(2)}) collective-permute-start(bf16[256,1024]{1,0:T(8,128)(2,1)S(1)} %pad_maximum_fusion.14), channel_id=1, source_target_pairs={{0,24},{8,0},{16,8},{24,16},{1,25},{9,1},{17,9},{25,17},{2,26},{10... | collective-permute-start | bytes 1572872 | tf_op jit(solution)/shard_map/ppermute | solution.py:81
  265.8 16.4 %collective-permute-start.12 = (bf16[256,1024]{1,0:T(8,128)(2,1)S(1)}, bf16[256,1024]{1,0:T(8,128)(2,1)S(1)}, u32[]{:S(2)}, u32[]{:S(2)}) collective-permute-start(bf16[256,1024]{1,0:T(8,128)(2,1)S(1)} %pad_maximum_fusion.13), channel_id=1, source_target_pairs={{0,8},{8,16},{16,24},{24,0},{1,9},{9,17},{17,25},{25,1},{2,10},{10... | collective-permute-start | bytes 1572872 | tf_op jit(solution)/shard_map/ppermute | solution.py:80
  267.3 20.6 %copy-start.21 = (bf16[1,256,1024]{2,1,0:T(8,128)(2,1)S(1)}, bf16[1,256,1024]{2,1,0:T(8,128)(2,1)}, u32[]{:S(2)}) copy-start(bf16[1,256,1024]{2,1,0:T(8,128)(2,1)} %param.14) | copy-start | bytes 1572868
  272.4 14.8 %collective-permute-start.10 = (bf16[256,1024]{1,0:T(8,128)(2,1)S(1)}, bf16[256,1024]{1,0:T(8,128)(2,1)S(1)}, u32[]{:S(2)}, u32[]{:S(2)}) collective-permute-start(bf16[256,1024]{1,0:T(8,128)(2,1)S(1)} %pad_maximum_fusion.12), channel_id=1, source_target_pairs={{0,24},{8,0},{16,8},{24,16},{1,25},{9,1},{17,9},{25,17},{2,26},{10... | collective-permute-start | bytes 1572872 | tf_op jit(solution)/shard_map/ppermute | solution.py:81
  275.9 32.8 %copy-start.22 = (bf16[1,256,1024]{2,1,0:T(8,128)(2,1)S(1)}, bf16[1,256,1024]{2,1,0:T(8,128)(2,1)}, u32[]{:S(2)}) copy-start(bf16[1,256,1024]{2,1,0:T(8,128)(2,1)} %param.25) | copy-start | bytes 1572868
  275.9 32.8 %slice-start = ((f32[1024]{0:T(1024)}), f32[256]{0:T(256)S(1)}, s32[]{:S(2)}) async-start(f32[1024]{0:T(1024)} %copy-done.28), calls=%async_computation.6 | async-start | bytes 2048 | tf_op jit(solution)/shard_map/slice | solution.py:324
  275.9 12.1 %collective-permute-start.8 = (bf16[256,1024]{1,0:T(8,128)(2,1)S(1)}, bf16[256,1024]{1,0:T(8,128)(2,1)S(1)}, u32[]{:S(2)}, u32[]{:S(2)}) collective-permute-start(bf16[256,1024]{1,0:T(8,128)(2,1)S(1)} %pad_maximum_fusion.11), channel_id=1, source_target_pairs={{0,8},{8,16},{16,24},{24,0},{1,9},{9,17},{17,25},{25,1},{2,10},{10... | collective-permute-start | bytes 1572872 | tf_op jit(solution)/shard_map/ppermute | solution.py:80
  290.3 20.7 %collective-permute-start.20 = (bf16[1,176,1024]{2,1,0:T(8,128)(2,1)}, bf16[1,176,1024]{2,1,0:T(8,128)(2,1)S(1)}, u32[]{:S(2)}, u32[]{:S(2)}) collective-permute-start(bf16[1,176,1024]{2,1,0:T(8,128)(2,1)} %reduce-scatter.5.cloned.1.call-done), channel_id=1, source_target_pairs={{0,32},{32,0},{64,96},{96,64},{1,33},{33,1},{65,97},{97,65},{2,34}... | collective-permute-start | bytes 1081352 | tf_op jit(solution)/shard_map/ppermute | solution.py:103
  308.6 6.4 %copy-start.25 = (bf16[128,1920]{1,0:T(8,128)(2,1)S(1)}, bf16[128,1920]{1,0:T(8,128)(2,1)}, u32[]{:S(2)}) copy-start(bf16[128,1920]{1,0:T(8,128)(2,1)} %reduce-scatter.3.cloned.1.call-done) | copy-start | bytes 1474564
  308.6 6.4 %collective-permute-start.15 = (bf16[128,1920]{1,0:T(8,128)(2,1)}, bf16[128,1920]{1,0:T(8,128)(2,1)S(1)}, u32[]{:S(2)}, u32[]{:S(2)}) collective-permute-start(bf16[128,1920]{1,0:T(8,128)(2,1)} %reduce-scatter.3.cloned.1.call-done), channel_id=1, source_target_pairs={{0,32},{32,0},{64,96},{96,64},{1,33},{33,1},{65,97},{97,65},{2,34}... | collective-permute-start | bytes 1474568 | tf_op jit(solution)/shard_map/ppermute | solution.py:103
  312.1 12.8 %collective-permute-start.21 = (bf16[1,176,1024]{2,1,0:T(8,128)(2,1)S(1)}, bf16[1,176,1024]{2,1,0:T(8,128)(2,1)S(1)}, u32[]{:S(2)}, u32[]{:S(2)}) collective-permute-start(bf16[1,176,1024]{2,1,0:T(8,128)(2,1)S(1)} %add_convert_fusion.3), channel_id=1, source_target_pairs={{0,64},{32,96},{64,0},{96,32},{1,65},{33,97},{65,1},{97,33},{2,66}... | collective-permute-start | bytes 1081352 | tf_op jit(solution)/shard_map/ppermute | solution.py:105
  315.2 19.8 %collective-permute-start.16 = (bf16[128,1920]{1,0:T(8,128)(2,1)S(1)}, bf16[128,1920]{1,0:T(8,128)(2,1)S(1)}, u32[]{:S(2)}, u32[]{:S(2)}) collective-permute-start(bf16[128,1920]{1,0:T(8,128)(2,1)S(1)} %add_convert_fusion.2), channel_id=1, source_target_pairs={{0,64},{32,96},{64,0},{96,32},{1,65},{33,97},{65,1},{97,33},{2,66}... | collective-permute-start | bytes 1474568 | tf_op jit(solution)/shard_map/ppermute | solution.py:105
  335.2 6.2 %collective-permute-start.17 = (bf16[32,1920]{1,0:T(8,128)(2,1)S(1)}, bf16[32,1920]{1,0:T(8,128)(2,1)S(1)}, u32[]{:S(2)}, u32[]{:S(2)}) collective-permute-start(bf16[32,1920]{1,0:T(8,128)(2,1)S(1)} %get-tuple-element.74), channel_id=1, source_target_pairs={{0,24},{8,0},{16,8},{24,16},{1,25},{9,1},{17,9},{25,17},{2,26},{10... | collective-permute-start | bytes 368648 | tf_op jit(solution)/shard_map/ppermute | solution.py:90
  339.1 8.5 %collective-permute-start.19 = (bf16[32,1920]{1,0:T(8,128)(2,1)S(1)}, bf16[32,1920]{1,0:T(8,128)(2,1)S(1)}, u32[]{:S(2)}, u32[]{:S(2)}) collective-permute-start(bf16[32,1920]{1,0:T(8,128)(2,1)S(1)} %get-tuple-element.71), channel_id=1, source_target_pairs={{0,8},{8,16},{16,24},{24,0},{1,9},{9,17},{17,25},{25,1},{2,10},{10... | collective-permute-start | bytes 368648 | tf_op jit(solution)/shard_map/ppermute | solution.py:90
  339.1 7.6 %collective-permute-start.18 = (bf16[32,1920]{1,0:T(8,128)(2,1)S(1)}, bf16[32,1920]{1,0:T(8,128)(2,1)S(1)}, u32[]{:S(2)}, u32[]{:S(2)}) collective-permute-start(bf16[32,1920]{1,0:T(8,128)(2,1)S(1)} %get-tuple-element.73), channel_id=1, source_target_pairs={{0,16},{8,24},{16,0},{24,8},{1,17},{9,25},{17,1},{25,9},{2,18},{10... | collective-permute-start | bytes 368648 | tf_op jit(solution)/shard_map/ppermute | solution.py:90
  (19 other events, 47.8 us)
Sparse Core Ops, SparseCore 0:
  24.0 42.2 all-gather.3
  71.2 52.4 all-gather.5
  214.0 42.3 reduce-scatter.4
  258.6 49.9 reduce-scatter.2

commit v8 on v7

--- a/solution.py
+++ b/solution.py
@@ -238,25 +238,17 @@
     ff_payload = jnp.concatenate(
         [column_payload[..., split : split + ff_here].reshape(nc * shard_rows, ff_here), outer_weight], 0
     )
-    ff_payload, triple_block = lax.optimization_barrier((ff_payload, triple_block))
+    visible = (pad_mask[0] != 0).astype(f32)
+    own_upstream = cotangent[0].astype(f32) * visible
+    both = jnp.concatenate([tokens[0], own_upstream.astype(bf16)], -1)
+    both = ring_gather(both, "ctx").reshape(length, 2 * width)
+    ff_payload, triple_block, both = lax.optimization_barrier((ff_payload, triple_block, both))
     ff_block = lax.all_gather(ff_payload, "fsdp", axis=0, tiled=False)
-    inner_here = (
-        ff_block[:, : nc * shard_rows]
-        .reshape(nf, nc, shard_rows, ff_here)
-        .swapaxes(0, 1)
-        .reshape(nc * nf * shard_rows, ff_here)
-    )
-    outer_here = ff_block[:, nc * shard_rows :].reshape(nf * ff_rows, width)
-
     triple_here = triple_block[:, :split]
     gain = triple_block[:, split].astype(f32)
     shift = triple_block[:, split + 1].astype(f32)
     obias = triple_block[:, split + 2].astype(f32)
 
-    visible = (pad_mask[0] != 0).astype(f32)
-    own_upstream = cotangent[0].astype(f32) * visible
-    both = jnp.concatenate([tokens[0], own_upstream.astype(bf16)], -1)
-    both = ring_gather(both, "ctx").reshape(length, 2 * width)
     all_tokens = both[:, :width]
     all_upstream = both[:, width:]
 
@@ -289,6 +281,15 @@
         values.swapaxes(0, 1) for values in (grad_queries, grad_keys, grad_values)
     )
     mixture = mixture.swapaxes(0, 1).reshape(length, head_cols)
+    ff_block, mixture = lax.optimization_barrier((ff_block, mixture))
+    inner_here = (
+        ff_block[:, : nc * shard_rows]
+        .reshape(nf, nc, shard_rows, ff_here)
+        .swapaxes(0, 1)
+        .reshape(nc * nf * shard_rows, ff_here)
+    )
+    outer_here = ff_block[:, nc * shard_rows :].reshape(nf * ff_rows, width)
+
     attention = jnp.dot(mixture, mixer_here, preferred_element_type=f32)
     preact = jnp.dot(normed, inner_here, preferred_element_type=f32) + ibias_here
     gelu_result = jax.nn.gelu(preact, approximate=True).astype(bf16)

time: 364 us -> 329 us (0.904)
  waiting for transfers between devices: 131 us -> 96.7 us
    all_gather x1, waiting for transfers between devices: 41.5 us -> 0.01 us  [local(): lax.all_gather(first_payload, 'fsdp', axis=0, tiled=False).reshape(nf, -1)]
    ppermute x1, waiting for transfers between devices: 3.56 us -> 7.91 us  [ring_gather(): far_second = lax.ppermute(from_right[half:], axis, ring_pairs(n, -1))]
  transfers between devices with their start and end apart: 26 -> 26, of which waited for: 17 -> 16; matrix products, arithmetic and copies ran while one was open for 29% -> 34% of each run, Pallas kernels for 9% -> 10%
where the time goes in v8:
time: 329 us; the launch traced here: 323 us
  waiting for transfers between devices  96.7 us (29%)
  local copies, waits for them, and re-layouts  60.4 us (18%)
  matrix products  45.1 us (14%)
  other arithmetic  41.4 us (13%)
  starting transfers between devices  31.6 us (10%)
  Pallas kernels  30.9 us (9%)
  between operations  16.4 us (5%)
    pallas_call x1, Pallas kernels, fused_attention(): pl.pallas_call(attention_kernel, out_shape=(jax.ShapeDtypeStruct((heads,...  30.9 us
    ppermute x1, waiting for transfers between devices, ring_gather(): from_right = lax.ppermute(block, axis, ring_pairs(n, -1))  22.3 us
    reduce_scatter x1, waiting for transfers between devices, local(): lax.psum_scatter(column_grads, 'fsdp', scatter_dimension=0, tiled=True)  19.3 us
    ppermute x2, waiting for transfers between devices, replica_sum(): lax.ppermute(pair, axis, [(i, i ^ 2) for i in range(n)]).astype(f32)  17.4 us
    unnamed x104, local copies, waits for them, and re-layouts  16.1 us
    ppermute x6, waiting for transfers between devices, ring_all_to_all(): lax.ppermute(pick(me + s), axis, ring_pairs(n, s))  12.5 us
    ppermute x6, starting transfers between devices, ring_all_to_all(): lax.ppermute(pick(me + s), axis, ring_pairs(n, s))  10.5 us
    ppermute x2, waiting for transfers between devices, ring_scatter(): from_right = lax.ppermute(to_left.astype(wire), axis, ring_pairs(n, -1))  9.54 us
  transfers between devices with their start and end apart: 26, of which 16 were waited for; matrix products, arithmetic and copies ran while one was open for 34% of the time, Pallas kernels for 10%

profile of v8, /device:TPU:0, one launch (start us, length us, event | category | flops | bytes accessed | tf_op | source)
XLA Modules:
  0.0 322.6 jit_solution(16122682336223020953)
XLA Ops:
  10.7 3.2 collective-permute-start
  13.8 2.2 collective-permute-start.1
  16.4 5.1 %collective-permute-done.1 = bf16[32,1920]{1,0:T(8,128)(2,1)S(1)} collective-permute-done((bf16[32,1920]{1,0:T(8,128)(2,1)S(1)}, bf16[32,1920]{1,0:T(8,128)(2,1)S(1)}, u32[]{:S(2)}, u32[]{:S(2)}) %collective-permute-start.1) | collective-permute-done | bytes 122912 | tf_op jit(solution)/shard_map/ppermute | solution.py:90
  26.9 22.3 %collective-permute-done.3 = bf16[256,2048]{1,0:T(8,128)(2,1)S(1)} collective-permute-done((bf16[256,2048]{1,0:T(8,128)(2,1)S(1)}, bf16[256,2048]{1,0:T(8,128)(2,1)S(1)}, u32[]{:S(2)}, u32[]{:S(2)}) %collective-permute-start.3) | collective-permute-done | bytes 1048608 | tf_op jit(solution)/shard_map/ppermute | solution.py:65
  54.7 7.9 %collective-permute-done.6 = bf16[128,2048]{1,0:T(8,128)(2,1)} collective-permute-done((bf16[128,2048]{1,0:T(8,128)(2,1)}, bf16[128,2048]{1,0:T(8,128)(2,1)}, u32[]{:S(2)}, u32[]{:S(2)}) %collective-permute-start.6) | collective-permute-done | bytes 524320 | tf_op jit(solution)/shard_map/ppermute | solution.py:67
  62.6 2.4 collective-permute-done.5
  66.3 2.3 pad_maximum_fusion
  68.6 3.2 copy.168
  81.3 2.4 fusion.2
  83.8 2.2 fusion.25
  90.2 3.3 %fusion.28 = bf16[1024,256]{0,1:T(8,128)(2,1)} fusion(bf16[256,1024]{1,0:T(8,128)(2,1)S(1)} %reshape.482, bf16[1024,2048]{1,0:T(8,128)(2,1)} %bitcast.208), kind=kOutput, calls=%fused_computation.46 | convolution fusion | flops 537133056 | bytes 3145728 | tf_op jit(solution)/shard_map/dot_general | solution.py:275
  93.5 2.4 copy.142
  98.4 2.2 copy.138
  100.5 2.4 copy.141
  111.1 3.0 copy.160
  114.1 3.3 %maximum_bitcast_fusion.1.k_ref = bf16[4,1024,64]{2,1,0:T(8,128)(2,1)} fusion(bf16[1024,4,32]{2,0,1:T(8,128)(2,1)} %copy.161, bf16[1024,4,32]{2,0,1:T(8,128)(2,1)} %copy.140), kind=kLoop, calls=%fused_computation.59 | loop fusion | flops 1048576 | bytes 1048576 | tf_op jit(solution)/shard_map/transpose | solution.py:276
  117.4 3.2 %fusion.31.q_ref = bf16[4,1024,64]{2,1,0:T(8,128)(2,1)} fusion(f32[1024,4,32]{2,0,1:T(8,128)} %copy.160, f32[1024,4,32]{2,0,1:T(8,128)S(1)} %copy-done.8), kind=kLoop, calls=%fused_computation.47 | loop fusion | flops 786432 | bytes 1572864 | tf_op jit(solution)/shard_map/transpose | solution.py:276
  120.6 30.9 %shard_map.195 = (bf16[4,1024,64]{2,1,0:T(8,128)(2,1)}, f32[4,1024,64]{2,1,0:T(8,128)}, f32[4,1024,64]{2,1,0:T(8,128)}, f32[4,1024,64]{2,1,0:T(8,128)}) custom-call(s32[1]{0:T(128)S(6)} %copy.194.span_ref, bf16[4,1024,64]{2,1,0:T(8,128)(2,1)} %fusion.31.q_ref, bf16[4,1024,64]{2,1,0:T(8,128)(2,1)} %maximum_bitcast_fusion.1.k_ref, ...), custom_call_target="tpu_custom_call" | custom-call | flops 3221225472 | bytes 5767168 | tf_op jit(solution)/shard_map/pallas_call | solution.py:158
  153.2 2.9 fusion.82
  156.4 3.4 %copy-done.1 = bf16[4,256,2048]{2,1,0:T(8,128)(2,1)S(1)} copy-done((bf16[4,256,2048]{2,1,0:T(8,128)(2,1)S(1)}, bf16[4,256,2048]{2,1,0:T(8,128)(2,1)}, u32[]{:S(2)}) %copy-start.1) | copy-done | bytes 4194328
  159.8 3.9 %multiply_convert_fusion = (bf16[1024,1024]{0,1:T(8,128)(2,1)S(1)}, f32[1024,1024]{0,1:T(8,128)S(1)}) fusion(f32[1024]{0:T(1024)S(1)} %fusion.60, bf16[1024,1024]{1,0:T(8,128)(2,1)S(1)} %bitcast.226, f32[1024]{0:T(1024)S(1)} %copy-done.35, f32[1024]{0:T(1024)S(1)} %copy-done.30, f32[1024]{0:T(1024)S(1)} %add_rsqrt_fusion, ...), kind=kOutput, calls=%fused_computation.16 | convolution fusion | flops 2164260864 | bytes 10506240 | tf_op jit(solution)/shard_map/dot_general | solution.py:294
  163.7 4.0 %convolution_convert_fusion = bf16[1296,1024]{1,0:T(8,128)(2,1)S(1)} fusion(bf16[1024,1024]{0,1:T(8,128)(2,1)S(1)} %get-tuple-element.91, bf16[1024,256]{0,1:T(8,128)(2,1)S(1)} %bitcast.243, bf16[1024,2048]{1,0:T(8,128)(2,1)S(1)} %bitcast.212, bf16[1296]{0:T(1024)(128)(2,1)S(1)} %copy-done.36), kind=kOutput, calls=%fused_computation.19 | convolution fusion | flops 2727198720 | bytes 7376896 | tf_op jit(solution)/shard_map/dot_general | solution.py:302
  168.0 6.4 %fusion.85 = (bf16[1024]{0:T(1024)(128)(2,1)S(1)}, bf16[1024,1024]{0,1:T(8,128)(2,1)}) fusion(f32[1024,1024]{0,1:T(8,128)S(1)} %get-tuple-element.92, f32[1024]{0:T(1024)S(1)} %fusion.60, bf16[1024,1024]{1,0:T(8,128)(2,1)S(1)} %bitcast.251, bf16[1024,2048]{1,0:T(8,128)(2,1)S(1)} %bitcast.213), kind=kOutput, calls=%fused_computation.206 | convolution fusion | flops 2170551296 | bytes 10491904 | tf_op jit(solution)/shard_map/dot_general | solution.py:303
  176.9 2.7 fusion.52
  179.6 2.2 copy.147
  181.8 3.8 %multiply_bitcast_fusion = (f32[1024,4,64]{2,0,1:T(8,128)}, bf16[1024,4,64]{2,0,1:T(8,128)(2,1)S(1)}) fusion(f32[4,1024,64]{2,1,0:T(8,128)} %get-tuple-element.37, f32[4,1024,64]{2,1,0:T(8,128)} %get-tuple-element.39), kind=kLoop, calls=%fused_computation.30 | loop fusion | flops 524288 | bytes 3670016 | tf_op jit(solution)/shard_map/mul | solution.py:311
  185.6 2.2 copy.146
  194.9 3.6 %convolution_convert_fusion.2 = bf16[1024,768]{1,0:T(8,128)(2,1)} fusion(bf16[1024,256]{0,1:T(8,128)(2,1)S(1)} %bitcast.266, bf16[1024,512]{0,1:T(8,128)(2,1)S(1)} %subtract_convert_fusion, f32[1024]{0:T(1024)S(1)} %copy-done.35, f32[1024]{0:T(1024)S(1)} %copy-done.30, f32[1024]{0:T(1024)S(1)} %add_rsqrt_fusion, f32[1024]{0:T(1024)S(1)} %broadcast_multiply_fusion, ...), kind=kOutput, calls=%fused_computation.34 | convolution fusion | flops 1620836352 | bytes 5259264 | tf_op jit(solution)/shard_map/dot_general | solution.py:317
  198.4 5.8 %multiply_reduce_fusion = (bf16[1024]{0:T(1024)(128)(2,1)S(1)}, bf16[1024]{0:T(1024)(128)(2,1)S(1)}, f32[1024,1024]{1,0:T(8,128)}, f32[1024,1024]{1,0:T(8,128)}) fusion(f32[1024]{0:T(1024)S(1)} %add_rsqrt_fusion, f32[1024]{0:T(1024)S(1)} %broadcast_multiply_fusion, bf16[1024,2048]{1,0:T(8,128)(2,1)S(1)} %bitcast.215, f32[1024,1024]{1,0:T(8,128)S(1)} %fusion.23, ...), kind=kOutput, calls=%fused_computation.15 | convolution fusion | flops 2154821632 | bytes 18886656 | tf_op jit(solution)/shard_map/dot_general | solution.py:319
  204.6 4.4 %convolution_convert_fusion.1 = bf16[1024,1024]{1,0:T(8,128)(2,1)S(1)} fusion(bf16[1024,1024]{0,1:T(8,128)(2,1)S(1)} %copy-done.11, f32[1024]{0:T(1024)S(1)} %copy-done.35, f32[1024]{0:T(1024)S(1)} %copy-done.30, f32[1024]{0:T(1024)S(1)} %add_rsqrt_fusion, f32[1024]{0:T(1024)S(1)} %broadcast_multiply_fusion, bf16[1024,2048]{1,0:T(8,128)(2,1)} %bitcast.209), kind=kOutput, calls=%fused_computation.32 | convolution fusion | flops 2154823680 | bytes 6307840 | tf_op jit(solution)/shard_map/dot_general | solution.py:306
  209.4 2.3 copy.159
  211.7 2.7 convert.90
  214.8 3.0 collective-permute-start.13
  217.9 2.4 fusion.86
  223.1 3.2 %collective-permute-start.9 = (bf16[128,1024]{1,0:T(8,128)(2,1)S(1)}, bf16[128,1024]{1,0:T(8,128)(2,1)}, u32[]{:S(2)}, u32[]{:S(2)}) collective-permute-start(bf16[128,1024]{1,0:T(8,128)(2,1)S(1)} %get-tuple-element.64), channel_id=1, source_target_pairs={{0,24},{8,0},{16,8},{24,16},{1,25},{9,1},{17,9},{25,17},{2,26},{10... | collective-permute-start | bytes 786440 | tf_op jit(solution)/shard_map/ppermute | solution.py:77
  229.9 3.6 %collective-permute-done.7 = bf16[128,1024]{1,0:T(8,128)(2,1)S(1)} collective-permute-done((bf16[128,1024]{1,0:T(8,128)(2,1)S(1)}, bf16[128,1024]{1,0:T(8,128)(2,1)S(1)}, u32[]{:S(2)}, u32[]{:S(2)}) %collective-permute-start.7) | collective-permute-done | bytes 262176 | tf_op jit(solution)/shard_map/ppermute | solution.py:76
  234.9 3.5 %collective-permute-start.10 = (bf16[256,1024]{1,0:T(8,128)(2,1)S(1)}, bf16[256,1024]{1,0:T(8,128)(2,1)S(1)}, u32[]{:S(2)}, u32[]{:S(2)}) collective-permute-start(bf16[256,1024]{1,0:T(8,128)(2,1)S(1)} %pad_maximum_fusion.12), channel_id=1, source_target_pairs={{0,24},{8,0},{16,8},{24,16},{1,25},{9,1},{17,9},{25,17},{2,26},{10... | collective-permute-start | bytes 1572872 | tf_op jit(solution)/shard_map/ppermute | solution.py:81
  238.7 5.5 %collective-permute-done.14 = bf16[256,1024]{1,0:T(8,128)(2,1)S(1)} collective-permute-done((bf16[256,1024]{1,0:T(8,128)(2,1)S(1)}, bf16[256,1024]{1,0:T(8,128)(2,1)S(1)}, u32[]{:S(2)}, u32[]{:S(2)}) %collective-permute-start.14) | collective-permute-done | bytes 524320 | tf_op jit(solution)/shard_map/ppermute | solution.py:81
  246.6 4.0 %collective-permute-done.10 = bf16[256,1024]{1,0:T(8,128)(2,1)S(1)} collective-permute-done((bf16[256,1024]{1,0:T(8,128)(2,1)S(1)}, bf16[256,1024]{1,0:T(8,128)(2,1)S(1)}, u32[]{:S(2)}, u32[]{:S(2)}) %collective-permute-start.10) | collective-permute-done | bytes 524320 | tf_op jit(solution)/shard_map/ppermute | solution.py:81
  252.0 2.4 fusion.40
  254.4 19.3 %reduce-scatter.3.cloned.1.call-done = bf16[128,1920]{1,0:T(8,128)(2,1)} async-done(((bf16[1024,1920]{1,0:T(8,128)(2,1)}), bf16[128,1920]{1,0:T(8,128)(2,1)}) %reduce-scatter.3.cloned.1.call-update) | async-done | bytes 491536 | tf_op jit(solution)/shard_map/reduce_scatter | solution.py:340
  273.7 2.4 fusion.39
  277.2 2.9 collective-permute-start.21
  281.0 9.0 %collective-permute-done.21 = bf16[1,176,1024]{2,1,0:T(8,128)(2,1)S(1)} collective-permute-done((bf16[1,176,1024]{2,1,0:T(8,128)(2,1)S(1)}, bf16[1,176,1024]{2,1,0:T(8,128)(2,1)S(1)}, u32[]{:S(2)}, u32[]{:S(2)}) %collective-permute-start.21) | collective-permute-done | bytes 360480 | tf_op jit(solution)/shard_map/ppermute | solution.py:105
  291.7 8.4 %collective-permute-done.16 = bf16[128,1920]{1,0:T(8,128)(2,1)S(1)} collective-permute-done((bf16[128,1920]{1,0:T(8,128)(2,1)S(1)}, bf16[128,1920]{1,0:T(8,128)(2,1)S(1)}, u32[]{:S(2)}, u32[]{:S(2)}) %collective-permute-start.16) | collective-permute-done | bytes 491552 | tf_op jit(solution)/shard_map/ppermute | solution.py:105
  300.2 2.8 collective-permute-start.17
  304.2 2.3 collective-permute-start.18
  306.5 5.3 %collective-permute-done.18 = bf16[32,1920]{1,0:T(8,128)(2,1)S(1)} collective-permute-done((bf16[32,1920]{1,0:T(8,128)(2,1)S(1)}, bf16[32,1920]{1,0:T(8,128)(2,1)S(1)}, u32[]{:S(2)}, u32[]{:S(2)}) %collective-permute-start.18) | collective-permute-done | bytes 122912 | tf_op jit(solution)/shard_map/ppermute | solution.py:90
  (242 shorter events, 72.1 us)
Async XLA Ops:
  7.2 8.8 %copy-start.37 = (bf16[128]{0:T(256)(128)(2,1)S(1)}, bf16[128]{0:T(256)(128)(2,1)}, u32[]{:S(2)}) copy-start(bf16[128]{0:T(256)(128)(2,1)} %param.20) | copy-start | bytes 772
  7.2 8.9 %copy-start.27 = (bf16[32,1024]{1,0:T(8,128)(2,1)S(1)}, bf16[32,1024]{1,0:T(8,128)(2,1)}, u32[]{:S(2)}) copy-start(bf16[32,1024]{1,0:T(8,128)(2,1)} %param.18) | copy-start | bytes 196612
  7.2 61.4 %all-gather.4.cloned.1.call-start = ((), (), s32[]{:S(2)}) async-start(), calls=%async_computation.2 | async-start | bytes 2949120 | tf_op jit(solution)/shard_map/all_gather | solution.py:229
  9.3 15.3 %copy-start.20 = (bf16[1,256,1024]{2,1,0:T(8,128)(2,1)S(1)}, bf16[1,256,1024]{2,1,0:T(8,128)(2,1)}, u32[]{:S(2)}) copy-start(bf16[1,256,1024]{2,1,0:T(8,128)(2,1)} %param.25) | copy-start | bytes 1572868
  10.5 14.1 %copy-start.18 = (bf16[1,256,1024]{2,1,0:T(8,128)(2,1)S(1)}, bf16[1,256,1024]{2,1,0:T(8,128)(2,1)}, u32[]{:S(2)}) copy-start(bf16[1,256,1024]{2,1,0:T(8,128)(2,1)} %param.14) | copy-start | bytes 1572868
  10.7 5.7 %collective-permute-start = (bf16[32,1920]{1,0:T(8,128)(2,1)S(1)}, bf16[32,1920]{1,0:T(8,128)(2,1)S(1)}, u32[]{:S(2)}, u32[]{:S(2)}) collective-permute-start(bf16[32,1920]{1,0:T(8,128)(2,1)S(1)} %get-tuple-element.84), channel_id=1, source_target_pairs={{0,24},{8,0},{16,8},{24,16},{1,25},{9,1},{17,9},{25,17},{2,26},{10... | collective-permute-start | bytes 368648 | tf_op jit(solution)/shard_map/ppermute | solution.py:90
  13.8 8.6 %collective-permute-start.2 = (bf16[32,1920]{1,0:T(8,128)(2,1)S(1)}, bf16[32,1920]{1,0:T(8,128)(2,1)S(1)}, u32[]{:S(2)}, u32[]{:S(2)}) collective-permute-start(bf16[32,1920]{1,0:T(8,128)(2,1)S(1)} %get-tuple-element.81), channel_id=1, source_target_pairs={{0,8},{8,16},{16,24},{24,0},{1,9},{9,17},{17,25},{25,1},{2,10},{10... | collective-permute-start | bytes 368648 | tf_op jit(solution)/shard_map/ppermute | solution.py:90
  13.8 7.7 %collective-permute-start.1 = (bf16[32,1920]{1,0:T(8,128)(2,1)S(1)}, bf16[32,1920]{1,0:T(8,128)(2,1)S(1)}, u32[]{:S(2)}, u32[]{:S(2)}) collective-permute-start(bf16[32,1920]{1,0:T(8,128)(2,1)S(1)} %get-tuple-element.83), channel_id=1, source_target_pairs={{0,16},{8,24},{16,0},{24,8},{1,17},{9,25},{17,1},{25,9},{2,18},{10... | collective-permute-start | bytes 368648 | tf_op jit(solution)/shard_map/ppermute | solution.py:90
  22.9 30.9 %copy-start.26 = (bf16[128,1024]{1,0:T(8,128)(2,1)S(1)}, bf16[128,1024]{1,0:T(8,128)(2,1)}, u32[]{:S(2)}) copy-start(bf16[128,1024]{1,0:T(8,128)(2,1)} %param.21) | copy-start | bytes 786436
  23.8 129.3 %all-gather.6.cloned.1.call-start = ((), (), s32[]{:S(2)}) async-start(), calls=%async_computation.5 | async-start | bytes 4718592 | tf_op jit(solution)/shard_map/all_gather | solution.py:246
  24.8 24.4 %collective-permute-start.3 = (bf16[256,2048]{1,0:T(8,128)(2,1)S(1)}, bf16[256,2048]{1,0:T(8,128)(2,1)S(1)}, u32[]{:S(2)}, u32[]{:S(2)}) collective-permute-start(bf16[256,2048]{1,0:T(8,128)(2,1)S(1)} %get-tuple-element.70), channel_id=1, source_target_pairs={{0,24},{8,0},{16,8},{24,16},{1,25},{9,1},{17,9},{25,17},{2,26},{10... | collective-permute-start | bytes 3145736 | tf_op jit(solution)/shard_map/ppermute | solution.py:65
  25.9 25.6 %collective-permute-start.4 = (bf16[256,2048]{1,0:T(8,128)(2,1)S(1)}, bf16[256,2048]{1,0:T(8,128)(2,1)S(1)}, u32[]{:S(2)}, u32[]{:S(2)}) collective-permute-start(bf16[256,2048]{1,0:T(8,128)(2,1)S(1)} %get-tuple-element.70), channel_id=1, source_target_pairs={{0,8},{8,16},{16,24},{24,0},{1,9},{9,17},{17,25},{25,1},{2,10},{10... | collective-permute-start | bytes 3145736 | tf_op jit(solution)/shard_map/ppermute | solution.py:64
  50.0 12.6 %collective-permute-start.6 = (bf16[128,2048]{1,0:T(8,128)(2,1)}, bf16[128,2048]{1,0:T(8,128)(2,1)}, u32[]{:S(2)}, u32[]{:S(2)}) collective-permute-start(bf16[128,2048]{1,0:T(8,128)(2,1)} %slice.266), channel_id=1, source_target_pairs={{0,24},{8,0},{16,8},{24,16},{1,25},{9,1},{17,9},{25,17},{2,26},{10... | collective-permute-start | bytes 1572872 | tf_op jit(solution)/shard_map/ppermute | solution.py:67
  52.3 12.7 %collective-permute-start.5 = (bf16[128,2048]{1,0:T(8,128)(2,1)}, bf16[128,2048]{1,0:T(8,128)(2,1)}, u32[]{:S(2)}, u32[]{:S(2)}) collective-permute-start(bf16[128,2048]{1,0:T(8,128)(2,1)} %slice.265), channel_id=1, source_target_pairs={{0,8},{8,16},{16,24},{24,0},{1,9},{9,17},{17,25},{25,1},{2,10},{10... | collective-permute-start | bytes 1572872 | tf_op jit(solution)/shard_map/ppermute | solution.py:66
  73.4 181.0 %reduce-scatter.5.cloned.1.call-start = ((), (), s32[]{:S(2)}) async-start(), calls=%async_computation.4 | async-start | bytes 3244032 | tf_op jit(solution)/shard_map/reduce_scatter | solution.py:365
  75.7 8.0 %copy-start = (bf16[4,256,2048]{2,1,0:T(8,128)(2,1)S(1)}, bf16[4,256,2048]{2,1,0:T(8,128)(2,1)}, u32[]{:S(2)}) copy-start(bf16[4,256,2048]{2,1,0:T(8,128)(2,1)} %pad_maximum_fusion) | copy-start | bytes 12582916
  75.7 8.0 %copy-start.9 = (bf16[4,8,32,896]{3,2,1,0:T(8,128)(2,1)S(1)}, bf16[4,8,32,896]{3,2,1,0:T(8,128)(2,1)}, u32[]{:S(2)}) copy-start(bf16[4,8,32,896]{3,2,1,0:T(8,128)(2,1)} %copy.134) | copy-start | bytes 5505028
  79.3 6.7 %copy-start.29 = (f32[1024]{0:T(1024)}, f32[1024]{0:T(1024)S(1)}, u32[]{:S(2)}) copy-start(f32[1024]{0:T(1024)S(1)} %get-tuple-element.44) | copy-start | bytes 12292
  79.3 6.7 %copy-start.34 = (f32[1024]{0:T(1024)}, f32[1024]{0:T(1024)S(1)}, u32[]{:S(2)}) copy-start(f32[1024]{0:T(1024)S(1)} %get-tuple-element.43) | copy-start | bytes 12292
  83.7 146.2 %copy-start.28 = (f32[1024]{0:T(1024)}, f32[1024]{0:T(1024)S(1)}, u32[]{:S(2)}) copy-start(f32[1024]{0:T(1024)S(1)} %add_rsqrt_fusion) | copy-start | bytes 12292
  90.2 7.8 %copy-start.14 = (bf16[256,1024]{1,0:T(8,128)(2,1)}, bf16[256,1024]{1,0:T(8,128)(2,1)S(1)}, u32[]{:S(2)}) copy-start(bf16[256,1024]{1,0:T(8,128)(2,1)S(1)} %reshape.482) | copy-start | bytes 1572868
  153.1 10.6 %copy-start.12 = (bf16[1024,4,64]{0,2,1:T(8,128)(2,1)}, bf16[1024,4,64]{0,2,1:T(8,128)(2,1)S(1)}, u32[]{:S(2)}) copy-start(bf16[1024,4,64]{0,2,1:T(8,128)(2,1)S(1)} %copy.144) | copy-start | bytes 1572868
  156.0 12.0 %copy-start.16 = (bf16[8,128,1024]{2,1,0:T(8,128)(2,1)}, bf16[8,128,1024]{2,1,0:T(8,128)(2,1)S(1)}, u32[]{:S(2)}) copy-start(bf16[8,128,1024]{2,1,0:T(8,128)(2,1)S(1)} %get-tuple-element.55) | copy-start | bytes 6291460
  156.4 7.3 %copy-start.5 = (bf16[4,8,32,1024]{3,2,1,0:T(8,128)(2,1)}, bf16[4,8,32,1024]{3,2,1,0:T(8,128)(2,1)S(1)}, u32[]{:S(2)}) copy-start(bf16[4,8,32,1024]{3,2,1,0:T(8,128)(2,1)S(1)} %copy.145) | copy-start | bytes 6291460
  176.6 97.1 %reduce-scatter.3.cloned.1.call-start = ((), (), s32[]{:S(2)}) async-start(), calls=%async_computation.3 | async-start | bytes 4423680 | tf_op jit(solution)/shard_map/reduce_scatter | solution.py:340
  211.7 6.1 %copy-start.17 = (bf16[8,128,1024]{2,1,0:T(8,128)(2,1)S(1)}, bf16[8,128,1024]{2,1,0:T(8,128)(2,1)}, u32[]{:S(2)}) copy-start(bf16[8,128,1024]{2,1,0:T(8,128)(2,1)} %copy-done.16) | copy-start | bytes 6291460
  211.7 6.1 %copy-start.39 = (bf16[1024,1024]{0,1:T(8,128)(2,1)S(1)}, bf16[1024,1024]{0,1:T(8,128)(2,1)}, u32[]{:S(2)}) copy-start(bf16[1024,1024]{0,1:T(8,128)(2,1)} %copy-done.38) | copy-start | bytes 6291460
  214.5 11.8 %collective-permute-start.11 = (bf16[128,1024]{1,0:T(8,128)(2,1)S(1)}, bf16[128,1024]{1,0:T(8,128)(2,1)S(1)}, u32[]{:S(2)}, u32[]{:S(2)}) collective-permute-start(bf16[128,1024]{1,0:T(8,128)(2,1)S(1)} %get-tuple-element.59), channel_id=1, source_target_pairs={{0,8},{8,16},{16,24},{24,0},{1,9},{9,17},{17,25},{25,1},{2,10},{10... | collective-permute-start | bytes 786440 | tf_op jit(solution)/shard_map/ppermute | solution.py:76
  214.8 5.5 %copy-start.13 = (bf16[1024,4,64]{0,2,1:T(8,128)(2,1)S(1)}, bf16[1024,4,64]{0,2,1:T(8,128)(2,1)}, u32[]{:S(2)}) copy-start(bf16[1024,4,64]{0,2,1:T(8,128)(2,1)} %copy-done.12) | copy-start | bytes 1572868
  214.8 5.5 %copy-start.15 = (bf16[256,1024]{1,0:T(8,128)(2,1)S(1)}, bf16[256,1024]{1,0:T(8,128)(2,1)}, u32[]{:S(2)}) copy-start(bf16[256,1024]{1,0:T(8,128)(2,1)} %copy-done.14) | copy-start | bytes 1572868
  214.8 11.5 %collective-permute-start.13 = (bf16[128,1024]{1,0:T(8,128)(2,1)S(1)}, bf16[128,1024]{1,0:T(8,128)(2,1)S(1)}, u32[]{:S(2)}, u32[]{:S(2)}) collective-permute-start(bf16[128,1024]{1,0:T(8,128)(2,1)S(1)} %get-tuple-element.60), channel_id=1, source_target_pairs={{0,24},{8,0},{16,8},{24,16},{1,25},{9,1},{17,9},{25,17},{2,26},{10... | collective-permute-start | bytes 786440 | tf_op jit(solution)/shard_map/ppermute | solution.py:77
  223.1 10.4 %collective-permute-start.7 = (bf16[128,1024]{1,0:T(8,128)(2,1)S(1)}, bf16[128,1024]{1,0:T(8,128)(2,1)S(1)}, u32[]{:S(2)}, u32[]{:S(2)}) collective-permute-start(bf16[128,1024]{1,0:T(8,128)(2,1)S(1)} %get-tuple-element.63), channel_id=1, source_target_pairs={{0,8},{8,16},{16,24},{24,0},{1,9},{9,17},{17,25},{25,1},{2,10},{10... | collective-permute-start | bytes 786440 | tf_op jit(solution)/shard_map/ppermute | solution.py:76
  223.1 10.4 %collective-permute-start.9 = (bf16[128,1024]{1,0:T(8,128)(2,1)S(1)}, bf16[128,1024]{1,0:T(8,128)(2,1)}, u32[]{:S(2)}, u32[]{:S(2)}) collective-permute-start(bf16[128,1024]{1,0:T(8,128)(2,1)S(1)} %get-tuple-element.64), channel_id=1, source_target_pairs={{0,24},{8,0},{16,8},{24,16},{1,25},{9,1},{17,9},{25,17},{2,26},{10... | collective-permute-start | bytes 786440 | tf_op jit(solution)/shard_map/ppermute | solution.py:77
  227.7 16.5 %collective-permute-start.14 = (bf16[256,1024]{1,0:T(8,128)(2,1)S(1)}, bf16[256,1024]{1,0:T(8,128)(2,1)S(1)}, u32[]{:S(2)}, u32[]{:S(2)}) collective-permute-start(bf16[256,1024]{1,0:T(8,128)(2,1)S(1)} %pad_maximum_fusion.14), channel_id=1, source_target_pairs={{0,24},{8,0},{16,8},{24,16},{1,25},{9,1},{17,9},{25,17},{2,26},{10... | collective-permute-start | bytes 1572872 | tf_op jit(solution)/shard_map/ppermute | solution.py:81
  227.8 16.9 %collective-permute-start.12 = (bf16[256,1024]{1,0:T(8,128)(2,1)S(1)}, bf16[256,1024]{1,0:T(8,128)(2,1)S(1)}, u32[]{:S(2)}, u32[]{:S(2)}) collective-permute-start(bf16[256,1024]{1,0:T(8,128)(2,1)S(1)} %pad_maximum_fusion.13), channel_id=1, source_target_pairs={{0,8},{8,16},{16,24},{24,0},{1,9},{9,17},{17,25},{25,1},{2,10},{10... | collective-permute-start | bytes 1572872 | tf_op jit(solution)/shard_map/ppermute | solution.py:80
  229.9 22.1 %copy-start.19 = (bf16[1,256,1024]{2,1,0:T(8,128)(2,1)S(1)}, bf16[1,256,1024]{2,1,0:T(8,128)(2,1)}, u32[]{:S(2)}) copy-start(bf16[1,256,1024]{2,1,0:T(8,128)(2,1)} %param.14) | copy-start | bytes 1572868
  234.9 15.8 %collective-permute-start.10 = (bf16[256,1024]{1,0:T(8,128)(2,1)S(1)}, bf16[256,1024]{1,0:T(8,128)(2,1)S(1)}, u32[]{:S(2)}, u32[]{:S(2)}) collective-permute-start(bf16[256,1024]{1,0:T(8,128)(2,1)S(1)} %pad_maximum_fusion.12), channel_id=1, source_target_pairs={{0,24},{8,0},{16,8},{24,16},{1,25},{9,1},{17,9},{25,17},{2,26},{10... | collective-permute-start | bytes 1572872 | tf_op jit(solution)/shard_map/ppermute | solution.py:81
  238.4 35.2 %copy-start.21 = (bf16[1,256,1024]{2,1,0:T(8,128)(2,1)S(1)}, bf16[1,256,1024]{2,1,0:T(8,128)(2,1)}, u32[]{:S(2)}) copy-start(bf16[1,256,1024]{2,1,0:T(8,128)(2,1)} %param.25) | copy-start | bytes 1572868
  238.5 35.2 %slice-start = ((f32[1024]{0:T(1024)}), f32[256]{0:T(256)S(1)}, s32[]{:S(2)}) async-start(f32[1024]{0:T(1024)} %copy-done.28), calls=%async_computation.6 | async-start | bytes 2048 | tf_op jit(solution)/shard_map/slice | solution.py:325
  238.5 13.6 %collective-permute-start.8 = (bf16[256,1024]{1,0:T(8,128)(2,1)S(1)}, bf16[256,1024]{1,0:T(8,128)(2,1)S(1)}, u32[]{:S(2)}, u32[]{:S(2)}) collective-permute-start(bf16[256,1024]{1,0:T(8,128)(2,1)S(1)} %pad_maximum_fusion.11), channel_id=1, source_target_pairs={{0,8},{8,16},{16,24},{24,0},{1,9},{9,17},{17,25},{25,1},{2,10},{10... | collective-permute-start | bytes 1572872 | tf_op jit(solution)/shard_map/ppermute | solution.py:80
  254.4 21.7 %collective-permute-start.20 = (bf16[1,176,1024]{2,1,0:T(8,128)(2,1)}, bf16[1,176,1024]{2,1,0:T(8,128)(2,1)S(1)}, u32[]{:S(2)}, u32[]{:S(2)}) collective-permute-start(bf16[1,176,1024]{2,1,0:T(8,128)(2,1)} %reduce-scatter.5.cloned.1.call-done), channel_id=1, source_target_pairs={{0,32},{32,0},{64,96},{96,64},{1,33},{33,1},{65,97},{97,65},{2,34}... | collective-permute-start | bytes 1081352 | tf_op jit(solution)/shard_map/ppermute | solution.py:103
  273.7 6.4 %copy-start.24 = (bf16[128,1920]{1,0:T(8,128)(2,1)S(1)}, bf16[128,1920]{1,0:T(8,128)(2,1)}, u32[]{:S(2)}) copy-start(bf16[128,1920]{1,0:T(8,128)(2,1)} %reduce-scatter.3.cloned.1.call-done) | copy-start | bytes 1474564
  273.7 6.4 %collective-permute-start.15 = (bf16[128,1920]{1,0:T(8,128)(2,1)}, bf16[128,1920]{1,0:T(8,128)(2,1)S(1)}, u32[]{:S(2)}, u32[]{:S(2)}) collective-permute-start(bf16[128,1920]{1,0:T(8,128)(2,1)} %reduce-scatter.3.cloned.1.call-done), channel_id=1, source_target_pairs={{0,32},{32,0},{64,96},{96,64},{1,33},{33,1},{65,97},{97,65},{2,34}... | collective-permute-start | bytes 1474568 | tf_op jit(solution)/shard_map/ppermute | solution.py:103
  277.2 12.8 %collective-permute-start.21 = (bf16[1,176,1024]{2,1,0:T(8,128)(2,1)S(1)}, bf16[1,176,1024]{2,1,0:T(8,128)(2,1)S(1)}, u32[]{:S(2)}, u32[]{:S(2)}) collective-permute-start(bf16[1,176,1024]{2,1,0:T(8,128)(2,1)S(1)} %add_convert_fusion.3), channel_id=1, source_target_pairs={{0,64},{32,96},{64,0},{96,32},{1,65},{33,97},{65,1},{97,33},{2,66}... | collective-permute-start | bytes 1081352 | tf_op jit(solution)/shard_map/ppermute | solution.py:105
  280.2 19.8 %collective-permute-start.16 = (bf16[128,1920]{1,0:T(8,128)(2,1)S(1)}, bf16[128,1920]{1,0:T(8,128)(2,1)S(1)}, u32[]{:S(2)}, u32[]{:S(2)}) collective-permute-start(bf16[128,1920]{1,0:T(8,128)(2,1)S(1)} %add_convert_fusion.2), channel_id=1, source_target_pairs={{0,64},{32,96},{64,0},{96,32},{1,65},{33,97},{65,1},{97,33},{2,66}... | collective-permute-start | bytes 1474568 | tf_op jit(solution)/shard_map/ppermute | solution.py:105
  300.2 6.2 %collective-permute-start.17 = (bf16[32,1920]{1,0:T(8,128)(2,1)S(1)}, bf16[32,1920]{1,0:T(8,128)(2,1)S(1)}, u32[]{:S(2)}, u32[]{:S(2)}) collective-permute-start(bf16[32,1920]{1,0:T(8,128)(2,1)S(1)} %get-tuple-element.80), channel_id=1, source_target_pairs={{0,24},{8,0},{16,8},{24,16},{1,25},{9,1},{17,9},{25,17},{2,26},{10... | collective-permute-start | bytes 368648 | tf_op jit(solution)/shard_map/ppermute | solution.py:90
  304.2 8.5 %collective-permute-start.19 = (bf16[32,1920]{1,0:T(8,128)(2,1)S(1)}, bf16[32,1920]{1,0:T(8,128)(2,1)S(1)}, u32[]{:S(2)}, u32[]{:S(2)}) collective-permute-start(bf16[32,1920]{1,0:T(8,128)(2,1)S(1)} %get-tuple-element.77), channel_id=1, source_target_pairs={{0,8},{8,16},{16,24},{24,0},{1,9},{9,17},{17,25},{25,1},{2,10},{10... | collective-permute-start | bytes 368648 | tf_op jit(solution)/shard_map/ppermute | solution.py:90
  304.2 7.6 %collective-permute-start.18 = (bf16[32,1920]{1,0:T(8,128)(2,1)S(1)}, bf16[32,1920]{1,0:T(8,128)(2,1)S(1)}, u32[]{:S(2)}, u32[]{:S(2)}) collective-permute-start(bf16[32,1920]{1,0:T(8,128)(2,1)S(1)} %get-tuple-element.79), channel_id=1, source_target_pairs={{0,16},{8,24},{16,0},{24,8},{1,17},{9,25},{17,1},{25,9},{2,18},{10... | collective-permute-start | bytes 368648 | tf_op jit(solution)/shard_map/ppermute | solution.py:90
  (19 other events, 56.4 us)
Sparse Core Ops, SparseCore 0:
  23.9 42.2 all-gather.3
  73.5 52.4 all-gather.5
  176.7 44.7 reduce-scatter.4
  223.9 49.7 reduce-scatter.2
